TPU v7x, 32 devices: a whole 2x2x4 slice. The times are simulated.
32 devices in a mesh: dp: 16 (over z, y, x), section: 2 (over core).
Axes of the slice: x: 2, y: 2, z: 4, core: 2. Of those that a mesh axis runs over, the one named last changes fastest.
Arguments:
- tokens: bfloat16 [32, 384, 768], P('dp'), may hold values from -6 to 6
- cotangent: float32 [32, 384, 768], P('dp'), may hold values from -6 to 6
- bucket: int32 [32], P('dp'), may hold values from 0 to 2, as said below
- batch_size: int32 [32], P('dp'), may hold values from 1 to 6, as said below
- lengths: int32 [32, 6], P('dp'), may hold values from 0 to 192, as said below
- query_weight: bfloat16 [2, 768, 768], P('section'), may hold values from -0.21875 to 0.21875
- query_offset: float32 [2, 768], P('section'), may hold values from -3 to 3
- keys_weight: bfloat16 [2, 768, 768], P('section'), may hold values from -0.21875 to 0.21875
- value_weight: bfloat16 [2, 768, 768], P('section'), may hold values from -0.21875 to 0.21875
- value_offset: float32 [2, 768], P('section'), may hold values from -3 to 3
- mixer_weight: bfloat16 [2, 768, 768], P('section'), may hold values from -1.75 to 1.75
- mixer_offset: float32 [2, 768], P('section'), may hold values from -3 to 3
- first_gain: float32 [2, 768], P('section'), may hold values from 0.25 to 1.75
- first_shift: float32 [2, 768], P('section'), may hold values from -3 to 3
- inner_weight: bfloat16 [2, 768, 3072], P('section'), may hold values from -0.21875 to 0.21875
- inner_offset: float32 [2, 3072], P('section'), may hold values from -3 to 3
- outer_weight: bfloat16 [2, 3072, 768], P('section'), may hold values from -0.15625 to 0.15625
- outer_offset: float32 [2, 768], P('section'), may hold values from -3 to 3
- second_gain: float32 [2, 768], P('section'), may hold values from 0.25 to 1.75
- second_shift: float32 [2, 768], P('section'), may hold values from -3 to 3
Outputs:
- layer_out: bfloat16 [2, 32, 384, 768], P('section', 'dp')
- input_grad: float32 [2, 32, 384, 768], P('section', 'dp')
- query_weight_gradient: float32 [2, 768, 768], P('section', 'dp')
- query_offset_gradient: float32 [2, 768], P('section', 'dp')
- keys_weight_gradient: float32 [2, 768, 768], P('section', 'dp')
- value_weight_gradient: float32 [2, 768, 768], P('section', 'dp')
- value_offset_gradient: float32 [2, 768], P('section', 'dp')
- mixer_weight_gradient: float32 [2, 768, 768], P('section', 'dp')
- mixer_offset_gradient: float32 [2, 768], P('section', 'dp')
- first_gain_gradient: float32 [2, 768], P('section', 'dp')
- first_shift_gradient: float32 [2, 768], P('section', 'dp')
- inner_weight_gradient: float32 [2, 768, 3072], P('section', 'dp')
- inner_offset_gradient: float32 [2, 3072], P('section', 'dp')
- outer_weight_gradient: float32 [2, 3072, 768], P('section', 'dp')
- outer_offset_gradient: float32 [2, 768], P('section', 'dp')
- second_gain_gradient: float32 [2, 768], P('section', 'dp')
- second_shift_gradient: float32 [2, 768], P('section', 'dp')
Inputs may be any that keep to these rules, and one draw needn't show every extreme that they name: Bucket b holds sequences of more than b * 64 and at most (b + 1) * 64 tokens in 6 // (b + 1) slots of (b + 1) * 64 rows; every bucket occurs. `batch_size`: at most the bucket's slots; the first slots are the used ones; each bucket is full in some micro-batch. `lengths`: 0 for unused slots; a used slot's length lies in its bucket's range, and slot 0 holds exactly (b + 1) * 64 tokens.
All inputs are finite; a program needn't handle non-finite values.
Results may differ from a plain program's by a relative error of at most 0.03.
Values may be sent and summed in bfloat16 or wider, within the bound.
No kernel may reach another device: no remote copies, remote signals or barrier semaphores. Data moves between devices by JAX's collectives and lax.ppermute only.
A program may use at most 256 MiB of HBM per device.

v0:
```python
import jax
import jax.numpy as jnp
from jax import lax
from jax.sharding import PartitionSpec as P

HEADS = 12
HEAD_DIM = 64
BUCKET = 64


masked_score = -1000000000.0
norm_epsilon = 1e-06


def from_behind(value, axis, steps):
    count = lax.axis_size(axis)
    initial, last = (max(0, -steps), min(count, count - steps))
    return lax.ppermute(value, axis, [(source, source + steps) for source in range(initial, last)])


def normalize(values, gain, shift):
    center = jnp.mean(values, axis=-1, keepdims=True)
    centred = values - center
    spread = jnp.mean(centred * centred, axis=-1, keepdims=True)
    return centred * lax.rsqrt(spread + norm_epsilon) * gain + shift


def gelu_exact(values):
    return jax.nn.gelu(values, approximate=False)


def build_masks(bucket_id, seq_count, seq_lengths, row_count):
    seq_span = BUCKET * (bucket_id + 1)
    position = jnp.arange(row_count, dtype=jnp.int32)
    slot_of = position // seq_span
    inner_place = position - slot_of * seq_span
    slot_ids = jnp.arange(seq_lengths.shape[0], dtype=jnp.int32)
    zero_int = jnp.zeros((), jnp.int32)
    seq_len = jnp.sum(
        jnp.where(slot_of[:, None] == slot_ids[None, :], seq_lengths[None, :], zero_int), axis=1
    )
    row_valid = (slot_of < seq_count) & (inner_place < seq_len)
    allowed = (slot_of[:, None] == slot_of[None, :]) & row_valid[None, :] | (
        position[:, None] == position[None, :]
    )
    return (allowed, row_valid.astype(jnp.float32))


def product(left, right):
    return jnp.dot(left, right, preferred_element_type=jnp.float32)


def contract(pattern, left, right):
    return jnp.einsum(pattern, left, right, preferred_element_type=jnp.float32)


def split_heads(values):
    return values.reshape(values.shape[0], HEADS, HEAD_DIM)


def column_sum(values):
    return jnp.sum(values, axis=0, dtype=jnp.float32)


def forward_pieces(hidden, params, allowed, row_valid):
    (
        w_query,
        b_query,
        w_keys,
        w_value,
        b_value,
        w_mixer,
        b_mixer,
        gain_one,
        shift_one,
        w_inner,
        b_inner,
        w_outer,
        b_outer,
        gain_two,
        shift_two,
    ) = params
    score_scale = HEAD_DIM ** (-0.5)
    row_count = hidden.shape[0]
    query_low = (product(hidden, w_query) + b_query).astype(jnp.bfloat16)
    keys_low = product(hidden, w_keys).astype(jnp.bfloat16)
    value_low = (product(hidden, w_value) + b_value).astype(jnp.bfloat16)
    scores = contract("qhe,khe->hqk", split_heads(query_low), split_heads(keys_low)) * score_scale
    scores = jnp.where(allowed[None], scores, masked_score)
    attention = jax.nn.softmax(scores, axis=-1)
    attention_low = attention.astype(jnp.bfloat16)
    context_low = (
        contract("hqk,khe->qhe", attention_low, split_heads(value_low))
        .reshape(row_count, HEADS * HEAD_DIM)
        .astype(jnp.bfloat16)
    )
    first_sum = hidden.astype(jnp.float32) + (product(context_low, w_mixer) + b_mixer)
    middle = normalize(first_sum, gain_one, shift_one)
    middle_low = middle.astype(jnp.bfloat16)
    inner = product(middle_low, w_inner) + b_inner
    active_low = gelu_exact(inner).astype(jnp.bfloat16)
    second_sum = middle + (product(active_low, w_outer) + b_outer)
    result = normalize(second_sum, gain_two, shift_two) * row_valid[:, None]
    kept = (
        query_low,
        keys_low,
        value_low,
        attention,
        attention_low,
        context_low,
        first_sum,
        middle_low,
        inner,
        active_low,
        second_sum,
    )
    return (result, kept)


def backward_feed(grad_out, params, kept, row_valid):
    (
        w_query,
        b_query,
        w_keys,
        w_value,
        b_value,
        w_mixer,
        b_mixer,
        gain_one,
        shift_one,
        w_inner,
        b_inner,
        w_outer,
        b_outer,
        gain_two,
        shift_two,
    ) = params
    (
        query_low,
        keys_low,
        value_low,
        attention,
        attention_low,
        context_low,
        first_sum,
        middle_low,
        inner,
        active_low,
        second_sum,
    ) = kept
    grad_out = grad_out * row_valid[:, None]
    _, norm_back = jax.vjp(normalize, second_sum, gain_two, shift_two)
    grad_second, grad_gain_two, grad_shift_two = norm_back(grad_out)
    grad_outer_low = grad_second.astype(jnp.bfloat16)
    grad_b_outer = column_sum(grad_outer_low)
    grad_w_outer = contract("rf,rd->fd", active_low, grad_outer_low)
    grad_active = contract("rd,fd->rf", grad_outer_low, w_outer)
    _, gelu_back = jax.vjp(gelu_exact, inner)
    grad_inner_low = gelu_back(grad_active)[0].astype(jnp.bfloat16)
    grad_b_inner = column_sum(grad_inner_low)
    grad_w_inner = contract("rd,rf->df", middle_low, grad_inner_low)
    grad_middle = grad_second + contract("rf,df->rd", grad_inner_low, w_inner)
    feed_grads = (
        grad_w_inner,
        grad_b_inner,
        grad_w_outer,
        grad_b_outer,
        grad_gain_two,
        grad_shift_two,
    )
    return (grad_middle, feed_grads)


def backward_mixer(grad_middle, params, kept):
    (
        w_query,
        b_query,
        w_keys,
        w_value,
        b_value,
        w_mixer,
        b_mixer,
        gain_one,
        shift_one,
        w_inner,
        b_inner,
        w_outer,
        b_outer,
        gain_two,
        shift_two,
    ) = params
    (
        query_low,
        keys_low,
        value_low,
        attention,
        attention_low,
        context_low,
        first_sum,
        middle_low,
        inner,
        active_low,
        second_sum,
    ) = kept
    _, norm_first = jax.vjp(normalize, first_sum, gain_one, shift_one)
    grad_first, grad_gain_one, grad_shift_one = norm_first(grad_middle)
    grad_branch_low = grad_first.astype(jnp.bfloat16)
    grad_b_mixer = column_sum(grad_branch_low)
    grad_w_mixer = contract("re,rd->ed", context_low, grad_branch_low)
    grad_context_low = split_heads(
        contract("rd,ed->re", grad_branch_low, w_mixer).astype(jnp.bfloat16)
    )
    mixer_grads = (grad_w_mixer, grad_b_mixer, grad_gain_one, grad_shift_one)
    return (grad_first, grad_context_low, mixer_grads)


def backward_attend(grad_first, grad_context_low, hidden, params, kept):
    (
        w_query,
        b_query,
        w_keys,
        w_value,
        b_value,
        w_mixer,
        b_mixer,
        gain_one,
        shift_one,
        w_inner,
        b_inner,
        w_outer,
        b_outer,
        gain_two,
        shift_two,
    ) = params
    (
        query_low,
        keys_low,
        value_low,
        attention,
        attention_low,
        context_low,
        first_sum,
        middle_low,
        inner,
        active_low,
        second_sum,
    ) = kept
    score_scale = HEAD_DIM ** (-0.5)
    row_count = hidden.shape[0]
    grad_attention = contract("qhe,khe->hqk", grad_context_low, split_heads(value_low))
    grad_value_low = (
        contract("hqk,qhe->khe", attention_low, grad_context_low)
        .reshape(row_count, -1)
        .astype(jnp.bfloat16)
    )
    grad_scores = attention * (
        grad_attention - jnp.sum(grad_attention * attention, axis=-1, keepdims=True)
    )
    grad_scores_low = grad_scores.astype(jnp.bfloat16)
    grad_query_low = (
        (contract("hqk,khe->qhe", grad_scores_low, split_heads(keys_low)) * score_scale)
        .reshape(row_count, -1)
        .astype(jnp.bfloat16)
    )
    grad_keys_low = (
        (contract("hqk,qhe->khe", grad_scores_low, split_heads(query_low)) * score_scale)
        .reshape(row_count, -1)
        .astype(jnp.bfloat16)
    )
    grad_b_query = column_sum(grad_query_low)
    grad_b_value = column_sum(grad_value_low)
    grad_w_query = contract("rd,re->de", hidden, grad_query_low)
    grad_w_keys = contract("rd,re->de", hidden, grad_keys_low)
    grad_w_value = contract("rd,re->de", hidden, grad_value_low)
    grad_hidden = grad_first + contract("re,de->rd", grad_query_low, w_query)
    grad_hidden = grad_hidden + contract("re,de->rd", grad_keys_low, w_keys)
    grad_hidden = grad_hidden + contract("re,de->rd", grad_value_low, w_value)
    attend_grads = (grad_w_query, grad_b_query, grad_w_keys, grad_w_value, grad_b_value)
    return (grad_hidden, attend_grads)


def backward_pieces(grad_out, hidden, params, kept, row_valid):
    grad_middle, feed_grads = backward_feed(grad_out, params, kept, row_valid)
    grad_first, grad_context_low, mixer_grads = backward_mixer(grad_middle, params, kept)
    grad_hidden, attend_grads = backward_attend(grad_first, grad_context_low, hidden, params, kept)
    return (grad_hidden, attend_grads + mixer_grads + feed_grads)


def per_device(
    tokens,
    cotangent,
    bucket,
    batch_size,
    lengths,
    query_weight,
    query_offset,
    keys_weight,
    value_weight,
    value_offset,
    mixer_weight,
    mixer_offset,
    first_gain,
    first_shift,
    inner_weight,
    inner_offset,
    outer_weight,
    outer_offset,
    second_gain,
    second_shift,
):
    stacked = (
        query_weight,
        query_offset,
        keys_weight,
        value_weight,
        value_offset,
        mixer_weight,
        mixer_offset,
        first_gain,
        first_shift,
        inner_weight,
        inner_offset,
        outer_weight,
        outer_offset,
        second_gain,
        second_shift,
    )
    params = tuple((piece[0] for piece in stacked))
    section_index = lax.axis_index("section")
    micro_count = tokens.shape[0]
    row_count = tokens.shape[1]
    width = tokens.shape[2]

    def masks_of(slot_index):
        return build_masks(
            bucket[slot_index], batch_size[slot_index], lengths[slot_index], row_count
        )

    def forward_tick(received, tick_index):
        micro_index = tick_index - section_index
        is_live = (micro_index >= 0) & (micro_index < micro_count)
        slot_index = jnp.clip(micro_index, 0, micro_count - 1)
        incoming = jnp.where(section_index == 0, tokens[slot_index], received)
        allowed, row_valid = masks_of(slot_index)

        def forward_compute(entry_rows):
            return forward_pieces(entry_rows, params, allowed, row_valid)[0].astype(jnp.bfloat16)

        def forward_skipped(entry_rows):
            return jnp.zeros_like(entry_rows)

        result = lax.cond(is_live, forward_compute, forward_skipped, incoming)
        passed = from_behind(result, "section", 1)
        return (passed, (incoming, result))

    start_rows = jnp.zeros((row_count, width), jnp.bfloat16)
    _, (inputs_all, results_all) = lax.scan(forward_tick, start_rows, jnp.arange(micro_count + 1))
    inputs_kept = lax.dynamic_slice_in_dim(inputs_all, section_index, micro_count, 0)
    layer_out = lax.dynamic_slice_in_dim(results_all, section_index, micro_count, 0)
    start_totals = tuple((jnp.zeros(piece.shape, jnp.float32) for piece in params))

    def backward_tick(state_pair, tick_index):
        received, totals = state_pair
        micro_index = tick_index - (1 - section_index)
        is_live = (micro_index >= 0) & (micro_index < micro_count)
        slot_index = jnp.clip(micro_index, 0, micro_count - 1)
        incoming = jnp.where(
            section_index == 1, cotangent[slot_index], received.astype(jnp.float32)
        )
        allowed, row_valid = masks_of(slot_index)

        def backward_compute(inputs_pair):
            entry_rows, grad_rows = inputs_pair
            _, kept = forward_pieces(entry_rows, params, allowed, row_valid)
            return backward_pieces(grad_rows, entry_rows, params, kept, row_valid)

        def backward_skipped(inputs_pair):
            return (
                jnp.zeros((row_count, width), jnp.float32),
                tuple((jnp.zeros(piece.shape, jnp.float32) for piece in params)),
            )

        grad_hidden, grads = lax.cond(
            is_live, backward_compute, backward_skipped, (inputs_kept[slot_index], incoming)
        )
        returned = from_behind(grad_hidden.astype(jnp.bfloat16), "section", -1)
        totals = tuple((total + piece for total, piece in zip(totals, grads)))
        return ((returned, totals), grad_hidden)

    start_back = jnp.zeros((row_count, width), jnp.bfloat16)
    (_, totals), grads_all = lax.scan(
        backward_tick, (start_back, start_totals), jnp.arange(micro_count + 1)
    )
    summed = lax.psum_scatter(totals, "dp", scatter_dimension=0, tiled=True)
    input_grad = lax.dynamic_slice_in_dim(grads_all, 1 - section_index, micro_count, 0)
    outputs = (layer_out[None], input_grad[None]) + tuple((piece[None] for piece in summed))
    return outputs


def solution(mesh):
    in_specs = (
        P("dp", None, None),
        P("dp", None, None),
        P("dp"),
        P("dp"),
        P("dp", None),
        P("section", None, None),
        P("section", None),
        P("section", None, None),
        P("section", None, None),
        P("section", None),
        P("section", None, None),
        P("section", None),
        P("section", None),
        P("section", None),
        P("section", None, None),
        P("section", None),
        P("section", None, None),
        P("section", None),
        P("section", None),
        P("section", None),
    )
    out_specs = (
        P("section", "dp", None, None),
        P("section", "dp", None, None),
        P("section", "dp", None),
        P("section", "dp"),
        P("section", "dp", None),
        P("section", "dp", None),
        P("section", "dp"),
        P("section", "dp", None),
        P("section", "dp"),
        P("section", "dp"),
        P("section", "dp"),
        P("section", "dp", None),
        P("section", "dp"),
        P("section", "dp", None),
        P("section", "dp"),
        P("section", "dp"),
        P("section", "dp"),
    )
    return jax.shard_map(
        per_device, mesh=mesh, in_specs=in_specs, out_specs=out_specs, check_vma=False
    )
```

profile of v0, /device:TPU:0, one launch (start us, length us, event | category | flops | bytes accessed | tf_op | source)
XLA Modules:
  0.0 1514.5 jit_solution(8180200490425901456)
XLA Ops:
  8.0 163.1 %while.61 = (s32[]{:T(128)}, bf16[384,768]{1,0:T(8,128)(2,1)S(1)}, bf16[3,384,768]{2,1,0:T(8,128)(2,1)}, bf16[3,384,768]{2,1,0:T(8,128)(2,1)}, s32[3]{0:T(128)},...) while((s32[]{:T(128)}, bf16[384,768]{1,0:T(8,128)(2,1)S(1)}, ...), condition=%wide.region_10.11_spmd, body=%wide.region_0.10_spmd.sunk | while | flops 5989978624 | bytes 76105104 | solution.py:357
  17.1 40.6 %conditional.5 = (bf16[384,768]{1,0:T(8,128)(2,1)S(1)}, bf16[1,384,768]{2,1,0:T(8,128)(2,1)S(1)}) conditional(s32[]{:T(128)} %convert_element_type.334, () %tuple.132, (bf16[384,768]{1,0:T(8,128)(2,1)}, bf16[768,768]{1,0:T(8,128)(2,1)}, f32[1,768]{1,0:T(1,128)}, s32[384]{0:T(512)S(1)}, s32[1,384]{1,0:T(1,128)S(1)}, /*index=5*/s32[]{:T(128)}, ...), branch_computations={%region_2.2_spmd, %region_3.9_spmd} | conditional | flops 5989668864 | bytes 61938776 | solution.py:352
  39.9 16.8 %fusion.140 = (f32[384]{0:T(512)S(1)}, f32[384,768]{1,0:T(8,128)S(1)}) fusion(f32[768]{0:T(1024)S(1)} %copy-done.69, bf16[3072,768]{1,0:T(8,128)(2,1)} %get-tuple-element.1206, bf16[768,3072]{1,0:T(8,128)(2,1)} %get-tuple-element.1204, f32[3072]{0:T(1024)S(1)} %bitcast.217, f32[384,768]{1,0:T(8,128)S(1)} %get-tuple-element.1688, f32[768]{0:T(1024)S(1)} %reduce.14, ...), kind=kOutput, calls=%fused_computation.253 | convolution fusion | flops 3705273856 | bytes 11822592 | tf_op jit(solution)/shard_map/while/body/eval_jaxpr/cond/branch_1_fun/dot_general | solution.py:50
  70.8 40.6 %conditional.5 = (bf16[384,768]{1,0:T(8,128)(2,1)S(1)}, bf16[1,384,768]{2,1,0:T(8,128)(2,1)S(1)}) conditional(s32[]{:T(128)} %convert_element_type.334, () %tuple.132, (bf16[384,768]{1,0:T(8,128)(2,1)}, bf16[768,768]{1,0:T(8,128)(2,1)}, f32[1,768]{1,0:T(1,128)}, s32[384]{0:T(512)S(1)}, s32[1,384]{1,0:T(1,128)S(1)}, /*index=5*/s32[]{:T(128)}, ...), branch_computations={%region_2.2_spmd, %region_3.9_spmd} | conditional | flops 5989668864 | bytes 61938776 | solution.py:352
  93.6 16.8 %fusion.140 = (f32[384]{0:T(512)S(1)}, f32[384,768]{1,0:T(8,128)S(1)}) fusion(f32[768]{0:T(1024)S(1)} %copy-done.69, bf16[3072,768]{1,0:T(8,128)(2,1)} %get-tuple-element.1206, bf16[768,3072]{1,0:T(8,128)(2,1)} %get-tuple-element.1204, f32[3072]{0:T(1024)S(1)} %bitcast.217, f32[384,768]{1,0:T(8,128)S(1)} %get-tuple-element.1688, f32[768]{0:T(1024)S(1)} %reduce.14, ...), kind=kOutput, calls=%fused_computation.253 | convolution fusion | flops 3705273856 | bytes 11822592 | tf_op jit(solution)/shard_map/while/body/eval_jaxpr/cond/branch_1_fun/dot_general | solution.py:50
  126.4 42.8 %collective-permute-start = (bf16[384,768]{1,0:T(8,128)(2,1)}, bf16[384,768]{1,0:T(8,128)(2,1)S(1)}, u32[]{:S(2)}, u32[]{:S(2)}) collective-permute-start(bf16[384,768]{1,0:T(8,128)(2,1)} %copy-done.28), channel_id=1, source_target_pairs={{0,1},{2,3},{4,5},{6,7},{8,9},{10,11},{12,13},{14,15},{16,17},{18,... | collective-permute-start | bytes 1769480 | tf_op jit(solution)/shard_map/while/body/eval_jaxpr/ppermute | solution.py:18
  173.8 450.8 %while.62 = (s32[]{:T(128)}, bf16[384,768]{1,0:T(8,128)(2,1)}, f32[768,768]{1,0:T(8,128)}, f32[768]{0:T(1024)}, f32[768,768]{1,0:T(8,128)}, /*index=5*/f32[768,7...) while((s32[]{:T(128)}, bf16[384,768]{1,0:T(8,128)(2,1)}, ...), condition=%wide.region_35.36_spmd.clone, body=%wide.region_11.35_spmd.clone.sunk | while | flops 17832177664 | bytes 492144448 | solution.py:391
  181.5 25.3 %conditional.6 = (f32[384,768]{1,0:T(8,128)S(1)}, f32[768,768]{1,0:T(8,128)}, f32[768]{0:T(1024)S(1)}, f32[768,768]{1,0:T(8,128)}, f32[768,768]{1,0:T(8,128)}, /...) conditional(s32[]{:T(128)} %convert_element_type.336, ...), branch_computations={%region_13.13_spmd, %region_14.34_spmd} | conditional | flops 17817694208 | bytes 370776768 | solution.py:383
  210.1 10.4 select_add_fusion.29
  221.2 8.7 select_add_fusion.31
  244.2 52.2 %collective-permute-done.1 = bf16[384,768]{1,0:T(8,128)(2,1)} collective-permute-done((bf16[384,768]{1,0:T(8,128)(2,1)}, bf16[384,768]{1,0:T(8,128)(2,1)}, u32[]{:S(2)}, u32[]{:S(2)}) %collective-permute-start.1) | collective-permute-done | bytes 589856 | tf_op jit(solution)/shard_map/while/body/eval_jaxpr/ppermute | solution.py:18
  303.9 110.5 %conditional.6 = (f32[384,768]{1,0:T(8,128)S(1)}, f32[768,768]{1,0:T(8,128)}, f32[768]{0:T(1024)S(1)}, f32[768,768]{1,0:T(8,128)}, f32[768,768]{1,0:T(8,128)}, /...) conditional(s32[]{:T(128)} %convert_element_type.336, ...), branch_computations={%region_13.13_spmd, %region_14.34_spmd} | conditional | flops 17817694208 | bytes 370776768 | solution.py:383
  324.0 15.5 %multiply_convert_fusion.2 = (bf16[384,3072]{1,0:T(8,128)(2,1)}, f32[384,3072]{1,0:T(8,128)}, f32[384,3072]{1,0:T(8,128)}) fusion(f32[3072]{0:T(1024)S(1)} %bitcast.218, bf16[768,3072]{1,0:T(8,128)(2,1)} %get-tuple-element.1267, f32[384,768]{1,0:T(8,128)S(1)} %get-tuple-element.1694, f32[768]{0:T(1024)S(1)} %reduce.25, f32[768]{0:T(1024)S(1)} %reduce.24, ...), kind=kOutput, calls=%fused_computation.112 | convolution fusion | flops 1891270656 | bytes 17716224 | tf_op jit(solution)/shard_map/while/body/eval_jaxpr/cond/branch_1_fun/dot_general | solution.py:50
  350.4 8.1 convert_reduce_fusion
  366.9 7.4 multiply_reduce_fusion.2
  417.7 13.2 select_add_fusion.29
  431.6 11.4 select_add_fusion.31
  452.8 6.6 select_add_fusion.26
  467.1 110.3 %conditional.6 = (f32[384,768]{1,0:T(8,128)S(1)}, f32[768,768]{1,0:T(8,128)}, f32[768]{0:T(1024)S(1)}, f32[768,768]{1,0:T(8,128)}, f32[768,768]{1,0:T(8,128)}, /...) conditional(s32[]{:T(128)} %convert_element_type.336, ...), branch_computations={%region_13.13_spmd, %region_14.34_spmd} | conditional | flops 17817694208 | bytes 370776768 | solution.py:383
  487.2 15.5 %multiply_convert_fusion.2 = (bf16[384,3072]{1,0:T(8,128)(2,1)}, f32[384,3072]{1,0:T(8,128)}, f32[384,3072]{1,0:T(8,128)}) fusion(f32[3072]{0:T(1024)S(1)} %bitcast.218, bf16[768,3072]{1,0:T(8,128)(2,1)} %get-tuple-element.1267, f32[384,768]{1,0:T(8,128)S(1)} %get-tuple-element.1694, f32[768]{0:T(1024)S(1)} %reduce.25, f32[768]{0:T(1024)S(1)} %reduce.24, ...), kind=kOutput, calls=%fused_computation.112 | convolution fusion | flops 1891270656 | bytes 17716224 | tf_op jit(solution)/shard_map/while/body/eval_jaxpr/cond/branch_1_fun/dot_general | solution.py:50
  513.6 7.8 convert_reduce_fusion
  529.8 7.4 multiply_reduce_fusion.2
  580.7 13.2 select_add_fusion.29
  594.7 11.4 select_add_fusion.31
  615.9 6.6 select_add_fusion.26
  630.6 80.3 %all-reduce.9 = (f32[768]{0:T(1024)}, f32[768]{0:T(1024)}, f32[768]{0:T(1024)}, f32[768]{0:T(1024)}, f32[768]{0:T(1024)}, /*index=5*/f32[3072]{0:T(1024)}, f32[768]{0:T(1024)}, f32[768]{0:T(1024)}, f32[768]{0:T(1024)}) all-reduce(f32[768]{0:T(1024)S(1)} %copy-done.54, ...), channel_id=3, replica_groups=mesh['dp'=16,'section'=2] {'dp'}, use_global_device_ids=true, to_apply=%region_37.38.clone | all-reduce | flops 9216 | bytes 73728
  721.3 35.5 %reduce-scatter.7.cloned.1.call-done = f32[48,768]{1,0:T(8,128)} async-done(((f32[768,768]{1,0:T(8,128)}), f32[48,768]{1,0:T(8,128)}) %reduce-scatter.7.cloned.1.call-update) | async-done | bytes 147472 | tf_op jit(solution)/shard_map/reduce_scatter | solution.py:394
  756.8 133.0 %reduce-scatter.9.cloned.1.call-done = f32[48,768]{1,0:T(8,128)} async-done(((f32[768,768]{1,0:T(8,128)}), f32[48,768]{1,0:T(8,128)}) %reduce-scatter.9.cloned.1.call-update) | async-done | bytes 147472 | tf_op jit(solution)/shard_map/reduce_scatter | solution.py:394
  889.8 132.1 %reduce-scatter.11.cloned.1.call-done = f32[48,768]{1,0:T(8,128)} async-done(((f32[768,768]{1,0:T(8,128)}), f32[48,768]{1,0:T(8,128)}) %reduce-scatter.11.cloned.1.call-update) | async-done | bytes 147472 | tf_op jit(solution)/shard_map/reduce_scatter | solution.py:394
  1021.9 132.5 %reduce-scatter.13.cloned.1.call-done = f32[48,768]{1,0:T(8,128)} async-done(((f32[768,768]{1,0:T(8,128)}), f32[48,768]{1,0:T(8,128)}) %reduce-scatter.13.cloned.1.call-update) | async-done | bytes 147472 | tf_op jit(solution)/shard_map/reduce_scatter | solution.py:394
  1154.4 175.6 %reduce-scatter.15.cloned.1.call-done = f32[48,3072]{1,0:T(8,128)} async-done(((f32[768,3072]{1,0:T(8,128)}), f32[48,3072]{1,0:T(8,128)}) %reduce-scatter.15.cloned.1.call-update) | async-done | bytes 589840 | tf_op jit(solution)/shard_map/reduce_scatter | solution.py:394
  1330.0 177.1 %reduce-scatter.17.cloned.1.call-done = f32[192,768]{1,0:T(8,128)} async-done(((f32[3072,768]{1,0:T(8,128)}), f32[192,768]{1,0:T(8,128)}) %reduce-scatter.17.cloned.1.call-update) | async-done | bytes 589840 | tf_op jit(solution)/shard_map/reduce_scatter | solution.py:394
  (703 shorter events, 341.9 us)
Async XLA Ops:
  7.2 749.6 %reduce-scatter.7.cloned.1.call-start = ((), (), s32[]{:S(2)}) async-start(), calls=%async_computation.6 | async-start | bytes 2506752 | tf_op jit(solution)/shard_map/reduce_scatter | solution.py:394
  39.9 16.9 %copy-start.71 = (f32[1,768]{1,0:T(1,128)S(1)}, f32[1,768]{1,0:T(1,128)}, u32[]{:S(2)}) copy-start(f32[1,768]{1,0:T(1,128)} %get-tuple-element.1209) | copy-start | bytes 9220 | tf_op jit(solution)/shard_map/while/body/eval_jaxpr/cond
  39.9 16.9 %copy-start.50 = (f32[1,768]{1,0:T(1,128)S(1)}, f32[1,768]{1,0:T(1,128)}, u32[]{:S(2)}) copy-start(f32[1,768]{1,0:T(1,128)} %get-tuple-element.1208) | copy-start | bytes 9220 | tf_op jit(solution)/shard_map/while/body/eval_jaxpr/cond
  58.6 3.1 collective-permute-start
  93.6 16.9 %copy-start.71 = (f32[1,768]{1,0:T(1,128)S(1)}, f32[1,768]{1,0:T(1,128)}, u32[]{:S(2)}) copy-start(f32[1,768]{1,0:T(1,128)} %get-tuple-element.1209) | copy-start | bytes 9220 | tf_op jit(solution)/shard_map/while/body/eval_jaxpr/cond
  93.6 16.9 %copy-start.50 = (f32[1,768]{1,0:T(1,128)S(1)}, f32[1,768]{1,0:T(1,128)}, u32[]{:S(2)}) copy-start(f32[1,768]{1,0:T(1,128)} %get-tuple-element.1208) | copy-start | bytes 9220 | tf_op jit(solution)/shard_map/while/body/eval_jaxpr/cond
  112.3 4.1 collective-permute-start
  126.4 44.6 %collective-permute-start = (bf16[384,768]{1,0:T(8,128)(2,1)}, bf16[384,768]{1,0:T(8,128)(2,1)S(1)}, u32[]{:S(2)}, u32[]{:S(2)}) collective-permute-start(bf16[384,768]{1,0:T(8,128)(2,1)} %copy-done.28), channel_id=1, source_target_pairs={{0,1},{2,3},{4,5},{6,7},{8,9},{10,11},{12,13},{14,15},{16,17},{18,... | collective-permute-start | bytes 1769480 | tf_op jit(solution)/shard_map/while/body/eval_jaxpr/ppermute | solution.py:18
  206.8 13.7 copy-start.40
  207.7 88.7 %collective-permute-start.1 = (bf16[384,768]{1,0:T(8,128)(2,1)}, bf16[384,768]{1,0:T(8,128)(2,1)}, u32[]{:S(2)}, u32[]{:S(2)}) collective-permute-start(bf16[384,768]{1,0:T(8,128)(2,1)} %convert_element_type.337), channel_id=1, source_target_pairs={{1,0},{3,2},{5,4},{7,6},{9,8},{11,10},{13,12},{15,14},{17,16},{19,... | collective-permute-start | bytes 1769480 | tf_op jit(solution)/shard_map/while/body/eval_jaxpr/ppermute | solution.py:18
  239.0 57.4 %copy-start.1 = (bf16[2,384,768]{2,1,0:T(8,128)(2,1)S(1)}, bf16[2,384,768]{2,1,0:T(8,128)(2,1)}, u32[]{:S(2)}) copy-start(bf16[2,384,768]{2,1,0:T(8,128)(2,1)} %copy-done) | copy-start | bytes 3538948 | tf_op jit(solution)/shard_map/while
  239.0 57.4 %copy-start.43 = (f32[1,768]{1,0:T(1,128)S(1)}, f32[1,768]{1,0:T(1,128)}, u32[]{:S(2)}) copy-start(f32[1,768]{1,0:T(1,128)} %get-tuple-element.2520) | copy-start | bytes 9220 | tf_op jit(solution)/shard_map/while
  304.0 18.9 %copy-start.2 = (bf16[2,384,768]{2,1,0:T(8,128)(2,1)}, bf16[2,384,768]{2,1,0:T(8,128)(2,1)S(1)}, u32[]{:S(2)}) copy-start(bf16[2,384,768]{2,1,0:T(8,128)(2,1)S(1)} %get-tuple-element.1246) | copy-start | bytes 3538948 | tf_op jit(solution)/shard_map/while/body/eval_jaxpr/cond
  324.0 15.5 %copy-start.49 = (f32[1,768]{1,0:T(1,128)S(1)}, f32[1,768]{1,0:T(1,128)}, u32[]{:S(2)}) copy-start(f32[1,768]{1,0:T(1,128)} %get-tuple-element.1270) | copy-start | bytes 9220 | tf_op jit(solution)/shard_map/while/body/eval_jaxpr/cond
  414.4 16.5 %copy-start.40 = (f32[768]{0:T(1024)}, f32[768]{0:T(1024)S(1)}, u32[]{:S(2)}) copy-start(f32[768]{0:T(1024)S(1)} %get-tuple-element.2164) | copy-start | bytes 9220 | tf_op jit(solution)/shard_map/while
  415.3 44.1 %collective-permute-start.1 = (bf16[384,768]{1,0:T(8,128)(2,1)}, bf16[384,768]{1,0:T(8,128)(2,1)}, u32[]{:S(2)}, u32[]{:S(2)}) collective-permute-start(bf16[384,768]{1,0:T(8,128)(2,1)} %convert_element_type.337), channel_id=1, source_target_pairs={{1,0},{3,2},{5,4},{7,6},{9,8},{11,10},{13,12},{15,14},{17,16},{19,... | collective-permute-start | bytes 1769480 | tf_op jit(solution)/shard_map/while/body/eval_jaxpr/ppermute | solution.py:18
  417.7 13.2 copy-start.36
  431.6 11.4 copy-start.37
  431.6 11.4 copy-start.5
  467.2 18.9 %copy-start.2 = (bf16[2,384,768]{2,1,0:T(8,128)(2,1)}, bf16[2,384,768]{2,1,0:T(8,128)(2,1)S(1)}, u32[]{:S(2)}) copy-start(bf16[2,384,768]{2,1,0:T(8,128)(2,1)S(1)} %get-tuple-element.1246) | copy-start | bytes 3538948 | tf_op jit(solution)/shard_map/while/body/eval_jaxpr/cond
  487.2 15.5 %copy-start.49 = (f32[1,768]{1,0:T(1,128)S(1)}, f32[1,768]{1,0:T(1,128)}, u32[]{:S(2)}) copy-start(f32[1,768]{1,0:T(1,128)} %get-tuple-element.1270) | copy-start | bytes 9220 | tf_op jit(solution)/shard_map/while/body/eval_jaxpr/cond
  577.4 16.5 %copy-start.40 = (f32[768]{0:T(1024)}, f32[768]{0:T(1024)S(1)}, u32[]{:S(2)}) copy-start(f32[768]{0:T(1024)S(1)} %get-tuple-element.2164) | copy-start | bytes 9220 | tf_op jit(solution)/shard_map/while
  578.3 44.2 %collective-permute-start.1 = (bf16[384,768]{1,0:T(8,128)(2,1)}, bf16[384,768]{1,0:T(8,128)(2,1)}, u32[]{:S(2)}, u32[]{:S(2)}) collective-permute-start(bf16[384,768]{1,0:T(8,128)(2,1)} %convert_element_type.337), channel_id=1, source_target_pairs={{1,0},{3,2},{5,4},{7,6},{9,8},{11,10},{13,12},{15,14},{17,16},{19,... | collective-permute-start | bytes 1769480 | tf_op jit(solution)/shard_map/while/body/eval_jaxpr/ppermute | solution.py:18
  580.7 13.2 copy-start.36
  594.7 11.4 copy-start.37
  594.7 11.4 copy-start.5
  624.6 265.2 %reduce-scatter.9.cloned.1.call-start = ((), (), s32[]{:S(2)}) async-start(), calls=%async_computation.7 | async-start | bytes 2506752 | tf_op jit(solution)/shard_map/reduce_scatter | solution.py:394
  625.3 396.6 %reduce-scatter.11.cloned.1.call-start = ((), (), s32[]{:S(2)}) async-start(), calls=%async_computation.8 | async-start | bytes 2506752 | tf_op jit(solution)/shard_map/reduce_scatter | solution.py:394
  626.1 528.4 %reduce-scatter.13.cloned.1.call-start = ((), (), s32[]{:S(2)}) async-start(), calls=%async_computation.9 | async-start | bytes 2506752 | tf_op jit(solution)/shard_map/reduce_scatter | solution.py:394
  626.7 703.4 %reduce-scatter.15.cloned.1.call-start = ((), (), s32[]{:S(2)}) async-start(), calls=%async_computation.10 | async-start | bytes 10027008 | tf_op jit(solution)/shard_map/reduce_scatter | solution.py:394
  627.2 879.8 %reduce-scatter.17.cloned.1.call-start = ((), (), s32[]{:S(2)}) async-start(), calls=%async_computation.11 | async-start | bytes 10027008 | tf_op jit(solution)/shard_map/reduce_scatter | solution.py:394
  627.3 92.4 %copy-start.30 = (f32[3,384,768]{2,1,0:T(8,128)S(1)}, f32[3,384,768]{2,1,0:T(8,128)}, u32[]{:S(2)}) copy-start(f32[3,384,768]{2,1,0:T(8,128)} %get-tuple-element.2492) | copy-start | bytes 10616836
  (167 other events, 763.3 us)
Sparse Core Ops, SparseCore 0:
  624.7 132.0 reduce-scatter.6
  763.0 126.7 reduce-scatter.8
  895.3 126.5 reduce-scatter.10
  1028.0 126.3 reduce-scatter.12
  1160.5 169.4 reduce-scatter.14
  1337.1 169.9 reduce-scatter.16
where the time goes:
time: 1530 us; the launch traced here: 1510 us
  waiting for transfers between devices  844 us (55%)
  matrix products  235 us (15%)
  other arithmetic  178 us (12%)
  local copies, waits for them, and re-layouts  91.7 us (6%)
  blocking collectives  80.3 us (5%)
  starting transfers between devices  50.5 us (3%)
  loops' own time  18.5 us (1%)
  between operations  16.2 us (1%)
    reduce_scatter x6, waiting for transfers between devices, per_device(): summed = lax.psum_scatter(totals, 'dp', scatter_dimension=0, tiled=True)  786 us
    add x27, other arithmetic, backward_tick(): totals = tuple((total + piece for total, piece in zip(totals, grads)))  115 us
    dot_general x36, matrix products, contract(): return jnp.einsum(pattern, left, right, preferred_element_type=jnp.float32)  113 us
    dot_general x22, matrix products, product(): return jnp.dot(left, right, preferred_element_type=jnp.float32)  98.7 us
    unnamed x1, blocking collectives  80.3 us
    ppermute x6, waiting for transfers between devices, from_behind(): lax.ppermute(value, axis, [(source, source + steps) for source in range(i...  54.9 us
    ppermute x6, starting transfers between devices, from_behind(): lax.ppermute(value, axis, [(source, source + steps) for source in range(i...  50.3 us
  transfers between devices with their start and end apart: 12, of which 10 were waited for; matrix products, arithmetic and copies ran while one was open for 9% of the time, Pallas kernels for 0%

commit v1 on v0

v1 whole, which is shorter than its diff:
```python
import functools
import jax
import jax.numpy as jnp
from jax import lax
from jax.experimental import pallas as pl
from jax.experimental.pallas import tpu as pltpu

HEADS = 12
HEAD_DIM = 64
BUCKET = 64
PAIR = 2 * HEAD_DIM
masked_score = -1000000000.0
norm_epsilon = 1e-06
F32 = jnp.float32
BF16 = jnp.bfloat16
CHUNK = 16
FFN_TILE = 512
ATT_UNROLL = 3


def rows_times(left, right):
    return lax.dot_general(left, right, (((1,), (0,)), ((), ())), preferred_element_type=F32)


def rows_times_transposed(left, right):
    return lax.dot_general(left, right, (((1,), (1,)), ((), ())), preferred_element_type=F32)


def transposed_times(left, right):
    return lax.dot_general(left, right, (((0,), (0,)), ((), ())), preferred_element_type=F32)


def slot_facts(block, span_rows, place, info, base):
    bucket = info[base]
    count = info[base + 1]

    def length_of(slot):
        return jnp.where(slot < count, info[base + 2 + slot], 0)

    if span_rows == 2 * BUCKET:
        return (jnp.full_like(place, block), place, jnp.full_like(place, length_of(block)))
    short = bucket == 0
    first = 3 * block
    slot_short = first + place // BUCKET
    length_short = jnp.where(
        place < BUCKET,
        length_of(first),
        jnp.where(place < 2 * BUCKET, length_of(first + 1), length_of(first + 2)),
    )
    slot = jnp.where(short, slot_short, block)
    inner = jnp.where(short, place % BUCKET, place)
    length = jnp.where(short, length_short, length_of(block))
    return (slot, inner, length)


def fill_masks(span_rows, row_count, info, base, bias_ref, valid_ref, row_base):
    for block in range(row_count // span_rows):
        row_place = lax.broadcasted_iota(jnp.int32, (span_rows, 1), 0)
        key_place = lax.broadcasted_iota(jnp.int32, (1, span_rows), 1)
        row_slot, row_inner, row_length = slot_facts(block, span_rows, row_place, info, base)
        key_slot, key_inner, key_length = slot_facts(block, span_rows, key_place, info, base)
        key_tag = jnp.where(key_inner < key_length, key_slot, -1)
        allowed = (row_slot == key_tag) | (row_place == key_place)
        rows = slice(row_base + block * span_rows, row_base + (block + 1) * span_rows)
        bias_ref[rows, 0:span_rows] = jnp.where(allowed, 0.0, masked_score)
        if valid_ref is not None:
            valid_ref[rows, :] = jnp.where(row_inner < row_length, 1.0, 0.0)


def softmax_rows(scores):
    top = jnp.max(scores, axis=-1, keepdims=True)
    weight = jnp.exp(scores - top)
    return weight * (1.0 / jnp.sum(weight, axis=-1, keepdims=True))


def attend_forward(span_rows, row_count, q_ref, k_ref, v_ref, bias_ref, c_ref):
    blocks = row_count // span_rows

    def one_pair(pair, carry):
        columns = pl.ds(pl.multiple_of(pair * PAIR, PAIR), PAIR)
        lane = lax.broadcasted_iota(jnp.int32, (span_rows, PAIR), 1)
        first_half = lane < HEAD_DIM
        weights = []
        for block in range(blocks):
            rows = slice(block * span_rows, (block + 1) * span_rows)
            query = q_ref[rows, columns] * jnp.asarray(HEAD_DIM ** (-0.5), BF16)
            keys = k_ref[rows, columns]
            zero = jnp.zeros_like(keys)
            bias = bias_ref[rows, 0:span_rows]
            for mine in (first_half, jnp.logical_not(first_half)):
                scores = rows_times_transposed(query, jnp.where(mine, keys, zero)) + bias
                top = jnp.max(scores, axis=-1, keepdims=True)
                weights.append(jnp.exp(scores - top).astype(BF16))
        for block in range(blocks):
            rows = slice(block * span_rows, (block + 1) * span_rows)
            value = v_ref[rows, columns]
            one = jnp.ones_like(value)
            left = rows_times(weights[2 * block], jnp.where(first_half, value, one))
            right = rows_times(weights[2 * block + 1], jnp.where(first_half, one, value))
            above = jnp.where(first_half, left, right)
            below = pltpu.roll(jnp.where(first_half, right, left), HEAD_DIM, 1)
            c_ref[rows, columns] = (above / below).astype(BF16)
        return carry

    lax.fori_loop(0, HEADS // 2, one_pair, 0, unroll=ATT_UNROLL)


def row_moments(values):
    center = jnp.mean(values, axis=-1, keepdims=True)
    centred = values - center
    spread = jnp.mean(centred * centred, axis=-1, keepdims=True)
    return centred, lax.rsqrt(spread + norm_epsilon)


def over_chunks(row_count, body, rows=CHUNK, group=6):
    def step(index, carry):
        for inner in range(group):
            start = pl.multiple_of(index * (rows * group) + inner * rows, rows)
            body(pl.ds(start, rows))
        return carry

    lax.fori_loop(0, row_count // (rows * group), step, 0)


def gelu_with_slope(values):
    cumulative = 0.5 + 0.5 * lax.erf(values * (0.5 ** 0.5))
    density = jnp.exp(values * values * -0.5) * 0.3989422804014327
    return values * cumulative, cumulative + values * density


def at_index(ref, index):
    return ref if index is None else ref.at[index]


def forward_kernel(
    tok_index, info, tok, rx, wq, wk, wv, wm, wi, wo, bq, bv, bm, g1, s1, bi, bo, g2, s2,
    y_o, q_o, k_o, v_o, c_o, a1_o, ml_o, u_o, gp_o, a2_o,
    h_s, wq_s, wk_s, wv_s, wm_s, wi_s, wo_s,
    q_s, k_s, v_s, c_s, a1_s, m_s, ml_s, u_s, gp_s, a2_s, y_s, f0_s, e0_s, e1_s, bias_s, valid_s,
    in_sem, out_sem,
):
    rows, width = h_s.shape
    hidden = wi_s.shape[1]

    @pl.when(info[0] == 1)
    def _():
        loads = []
        for index, (source, target) in enumerate(
            ((wq, wq_s), (wk, wk_s), (wv, wv_s), (wm, wm_s), (wi, wi_s), (wo, wo_s))
        ):
            loads.append(pltpu.make_async_copy(source.at[0], target, in_sem.at[index]))
        own = pltpu.make_async_copy(at_index(tok, tok_index), h_s, in_sem.at[6])
        other = pltpu.make_async_copy(rx, h_s, in_sem.at[6])

        @pl.when(info[1] == 0)
        def _():
            own.start()

        @pl.when(info[1] == 1)
        def _():
            other.start()

        for load in loads[:3]:
            load.start()
        stores = []

        def store(source, target):
            copy = pltpu.make_async_copy(source, target, out_sem.at[len(stores)])
            copy.start()
            stores.append(copy)

        even = info[2] == 1

        @pl.when(even)
        def _():
            fill_masks(2 * BUCKET, rows, info, 2, bias_s, valid_s, 0)

        @pl.when(jnp.logical_not(even))
        def _():
            fill_masks(3 * BUCKET, rows, info, 2, bias_s, valid_s, 0)

        own.wait()
        loads[0].wait()
        loads[3].start()
        q_s[...] = (rows_times(h_s[...], wq_s[...]) + bq[...]).astype(BF16)
        store(q_s, q_o)
        loads[1].wait()
        loads[4].start()
        k_s[...] = rows_times(h_s[...], wk_s[...]).astype(BF16)
        store(k_s, k_o)
        loads[2].wait()
        loads[5].start()
        v_s[...] = (rows_times(h_s[...], wv_s[...]) + bv[...]).astype(BF16)
        store(v_s, v_o)

        @pl.when(even)
        def _():
            attend_forward(2 * BUCKET, rows, q_s, k_s, v_s, bias_s, c_s)

        @pl.when(jnp.logical_not(even))
        def _():
            attend_forward(3 * BUCKET, rows, q_s, k_s, v_s, bias_s, c_s)

        store(c_s, c_o)
        loads[3].wait()
        f0_s[...] = rows_times(c_s[...], wm_s[...])

        def first_norm(part):
            total = h_s[part, :].astype(F32) + (f0_s[part, :] + bm[...])
            a1_s[part, :] = total
            centred, scale = row_moments(total)
            middle = centred * scale * g1[...] + s1[...]
            m_s[part, :] = middle
            ml_s[part, :] = middle.astype(BF16)

        over_chunks(rows, first_norm)
        store(a1_s, a1_o)
        store(ml_s, ml_o)
        loads[4].wait()
        tile = FFN_TILE
        tiles = hidden // tile

        def project(buffer, which):
            columns = pl.ds(pl.multiple_of(which * tile, tile), tile)
            buffer[...] = rows_times(ml_s[...], wi_s[:, columns])

        def activate(buffer, which):
            columns = pl.ds(pl.multiple_of(which * tile, tile), tile)
            offset = bi[:, columns]
            for start in range(0, rows, 32):
                part = slice(start, start + 32)
                value, slope = gelu_with_slope(buffer[part, :] + offset)
                u_s[part, columns] = value.astype(BF16)
                gp_s[part, columns] = slope.astype(BF16)

        project(e0_s, 0)

        def two_tiles(index, carry):
            project(e1_s, 2 * index + 1)
            activate(e0_s, 2 * index)
            project(e0_s, jnp.minimum(2 * index + 2, tiles - 1))
            activate(e1_s, 2 * index + 1)
            return carry

        lax.fori_loop(0, tiles // 2, two_tiles, 0)
        store(u_s, u_o)
        store(gp_s, gp_o)
        loads[5].wait()
        f0_s[...] = rows_times(u_s[...], wo_s[...])

        def second_norm(part):
            total = m_s[part, :] + (f0_s[part, :] + bo[...])
            a2_s[part, :] = total
            centred, scale = row_moments(total)
            y_s[part, :] = ((centred * scale * g2[...] + s2[...]) * valid_s[part, :]).astype(BF16)

        over_chunks(rows, second_norm)
        store(y_s, y_o)
        store(a2_s, a2_o)
        for copy in stores:
            copy.wait()


ANY = pl.BlockSpec(memory_space=pl.ANY)
VM = pl.BlockSpec(memory_space=pltpu.VMEM)
SM = pl.BlockSpec(memory_space=pltpu.SMEM)
VMEM_LIMIT = 63_000 * 1024


def forward_layer(info, tok, tok_index, rx, params):
    wq, bq, wk, wv, bv, wm, bm, g1, s1, wi, bi, wo, bo, g2, s2 = params
    rows, width = rx.shape
    hidden = wi.shape[-1]
    S = jax.ShapeDtypeStruct
    flat = (rows, width)
    wide = (rows, hidden)
    outs = (
        S(flat, BF16), S(flat, BF16), S(flat, BF16), S(flat, BF16), S(flat, BF16),
        S(flat, F32), S(flat, BF16), S(wide, BF16), S(wide, BF16), S(flat, F32),
    )
    V = pltpu.VMEM
    square = (width, width)
    scratch = [
        V(flat, BF16), V(square, BF16), V(square, BF16), V(square, BF16), V(square, BF16),
        V((width, hidden), BF16), V((hidden, width), BF16),
        V(flat, BF16), V(flat, BF16), V(flat, BF16), V(flat, BF16),
        V(flat, F32), V(flat, F32), V(flat, BF16), V(wide, BF16), V(wide, BF16), V(flat, F32), V(flat, BF16),
        V(flat, F32), V((rows, FFN_TILE), F32), V((rows, FFN_TILE), F32), V((rows, 3 * BUCKET), F32), V((rows, 1), F32),
        pltpu.SemaphoreType.DMA((7,)), pltpu.SemaphoreType.DMA((10,)),
    ]
    return pl.pallas_call(
        functools.partial(forward_kernel, tok_index),
        out_shape=outs,
        in_specs=[SM, ANY, ANY] + [ANY] * 6 + [VM] * 9,
        out_specs=[ANY] * 10,
        scratch_shapes=scratch,
        compiler_params=pltpu.CompilerParams(vmem_limit_bytes=VMEM_LIMIT),
        cost_estimate=pl.CostEstimate(flops=2 * rows * width * (4 * width + 2 * hidden), bytes_accessed=30_000_000, transcendentals=rows * hidden * 2),
        name="layer_forward",
    )(info, tok, rx, wq, wk, wv, wm, wi, wo, bq, bv, bm, g1, s1, bi, bo, g2, s2)


def norm_backward(grad, total, gain):
    centred, scale = row_moments(total)
    unit = centred * scale
    spread = grad * gain
    first = jnp.mean(spread, axis=-1, keepdims=True)
    second = jnp.mean(spread * unit, axis=-1, keepdims=True)
    return (spread - first - unit * second) * scale, grad * unit


def fold_rows(values):
    return jnp.sum(values.reshape(values.shape[0] // 8, 8, values.shape[1]), axis=0)


def add_rows(total_ref, values):
    total_ref[...] += fold_rows(values)


def put_blocks(target, product, tile, place, orders, spread_units):
    count = target.shape[1]
    height = product.shape[0] // count
    for block in range(count):
        if spread_units and count > 1:
            unit = block % 4
            dest = tile * (count // 4) + block // 4
        else:
            unit = tile
            dest = block
        if count > 1:
            spot = place[orders[unit % 2] * count + dest]
        else:
            spot = 0
        target[unit, spot] = product[block * height : (block + 1) * height, :].astype(BF16)


def outer_kernel(
    orders, info, place, g, a2a, a2b, ua, ub, g2,
    da2_o, dz_o, away_o, home_o, small_o,
    g_s, a2_s, u_s, da2_s, dz_s, w_s, valid_s, sums_s, in_sem, out_sem,
):
    rows = a2a.shape[0]
    width = a2_s.shape[1]
    hidden = u_s.shape[1]

    @pl.when(info[0] == 1)
    def _():
        loads = []
        for index, (source, target) in enumerate(((g.at[0], g_s), (a2a, a2_s), (ua, u_s))):
            loads.append(pltpu.make_async_copy(source, target.at[0:rows], in_sem.at[index]))
        for index, (source, target) in enumerate(((g.at[1], g_s), (a2b, a2_s), (ub, u_s))):
            loads.append(pltpu.make_async_copy(source, target.at[rows : 2 * rows], in_sem.at[3 + index]))
        for load in (loads[0], loads[1], loads[3], loads[4]):
            load.start()
        for micro in range(2):
            base = 2 + 8 * micro
            for span in (2, 3):
                @pl.when((info[base] == 1) == (span == 2))
                def _(span=span, micro=micro, base=base):
                    fill_valid(span * BUCKET, rows, info, base, valid_s, micro * rows)
        sums_s[...] = jnp.zeros_like(sums_s)
        for load in (loads[0], loads[1], loads[3], loads[4]):
            load.wait()
        loads[2].start()
        loads[5].start()

        def second_norm(part):
            grad = g_s[part, :].astype(F32) * valid_s[part, :]
            moved, gained = norm_backward(grad, a2_s[part, :], g2[...])
            da2_s[part, :] = moved
            low = moved.astype(BF16)
            dz_s[part, :] = low
            add_rows(sums_s.at[0], gained)
            add_rows(sums_s.at[1], grad)
            add_rows(sums_s.at[2], low.astype(F32))

        over_chunks(2 * rows, second_norm)
        stores = [
            pltpu.make_async_copy(da2_s, da2_o, out_sem.at[0]),
            pltpu.make_async_copy(dz_s, dz_o, out_sem.at[1]),
        ]
        for copy in stores:
            copy.start()
        for index in range(3):
            small_o[index : index + 1, :] = jnp.sum(sums_s[index], axis=0, keepdims=True)
        loads[2].wait()
        loads[5].wait()
        for tile in range(hidden // width):
            columns = slice(tile * width, (tile + 1) * width)
            put_blocks(w_s, transposed_times(u_s[:, columns], dz_s[...]), tile, place, orders, True)
        stores.append(pltpu.make_async_copy(w_s.at[0:2], away_o, out_sem.at[2]))
        stores.append(pltpu.make_async_copy(w_s.at[2:4], home_o, out_sem.at[3]))
        for copy in stores[2:]:
            copy.start()
        for copy in stores:
            copy.wait()


def fill_valid(span_rows, row_count, info, base, valid_ref, row_base):
    for block in range(row_count // span_rows):
        row_place = lax.broadcasted_iota(jnp.int32, (span_rows, 1), 0)
        row_slot, row_inner, row_length = slot_facts(block, span_rows, row_place, info, base)
        rows = slice(row_base + block * span_rows, row_base + (block + 1) * span_rows)
        valid_ref[rows, :] = jnp.where(row_inner < row_length, 1.0, 0.0)


def inner_kernel(
    orders, info, place, dz, gpa, gpb, mla, mlb, wo,
    df_o, away_o, home_o, small_o,
    dz_s, gp_s, ml_s, wo_s, df_s, w_s, e0_s, e1_s, sums_s, in_sem, out_sem,
):
    rows = mla.shape[0]
    width = dz_s.shape[1]
    hidden = df_s.shape[1]

    @pl.when(info[0] == 1)
    def _():
        loads = [
            pltpu.make_async_copy(dz, dz_s, in_sem.at[0]),
            pltpu.make_async_copy(wo.at[0], wo_s, in_sem.at[1]),
            pltpu.make_async_copy(gpa, gp_s.at[0:rows], in_sem.at[2]),
            pltpu.make_async_copy(gpb, gp_s.at[rows : 2 * rows], in_sem.at[3]),
            pltpu.make_async_copy(mla, ml_s.at[0:rows], in_sem.at[4]),
            pltpu.make_async_copy(mlb, ml_s.at[rows : 2 * rows], in_sem.at[5]),
        ]
        loads[0].start()
        loads[1].start()
        loads[0].wait()
        loads[1].wait()
        for load in loads[2:]:
            load.start()
        tile = FFN_TILE
        tiles = hidden // tile
        sums_s[...] = jnp.zeros_like(sums_s)

        def project(buffer, which):
            columns = pl.ds(pl.multiple_of(which * tile, tile), tile)
            buffer[...] = rows_times_transposed(dz_s[...], wo_s[columns, :])

        def slope(buffer, which):
            columns = pl.ds(pl.multiple_of(which * tile, tile), tile)
            for start in range(0, 2 * rows, 32):
                part = slice(start, start + 32)
                low = (buffer[part, :] * gp_s[part, columns].astype(F32)).astype(BF16)
                df_s[part, columns] = low
                sums_s[:, columns] += fold_rows(low.astype(F32))

        project(e0_s, 0)
        for load in loads[2:]:
            load.wait()

        def two_tiles(index, carry):
            project(e1_s, 2 * index + 1)
            slope(e0_s, 2 * index)
            project(e0_s, jnp.minimum(2 * index + 2, tiles - 1))
            slope(e1_s, 2 * index + 1)
            return carry

        lax.fori_loop(0, tiles // 2, two_tiles, 0)
        stores = [pltpu.make_async_copy(df_s, df_o, out_sem.at[0])]
        stores[0].start()
        small_o[...] = jnp.sum(sums_s[...], axis=0, keepdims=True)
        for which in range(hidden // width):
            columns = slice(which * width, (which + 1) * width)
            put_blocks(w_s, transposed_times(ml_s[...], df_s[:, columns]), which, place, orders, False)
        stores.append(pltpu.make_async_copy(w_s.at[0:2], away_o, out_sem.at[1]))
        stores.append(pltpu.make_async_copy(w_s.at[2:4], home_o, out_sem.at[2]))
        for copy in stores[1:]:
            copy.start()
        for copy in stores:
            copy.wait()


def mixer_kernel(
    orders, info, place, df, wi, da2, a1a, a1b, ca, cb, wm, g1,
    da1_o, dc_o, mix_o, small_o,
    df_s, wi_s, da2_s, a1_s, c_s, wm_s, dm_s, da1_s, da_s, dc_s, w_s, sums_s, in_sem, out_sem,
):
    rows = a1a.shape[0]

    @pl.when(info[0] == 1)
    def _():
        loads = [
            pltpu.make_async_copy(df, df_s, in_sem.at[0]),
            pltpu.make_async_copy(wi.at[0], wi_s, in_sem.at[1]),
            pltpu.make_async_copy(da2, da2_s, in_sem.at[2]),
            pltpu.make_async_copy(a1a, a1_s.at[0:rows], in_sem.at[3]),
            pltpu.make_async_copy(a1b, a1_s.at[rows : 2 * rows], in_sem.at[4]),
            pltpu.make_async_copy(ca, c_s.at[0:rows], in_sem.at[5]),
            pltpu.make_async_copy(cb, c_s.at[rows : 2 * rows], in_sem.at[6]),
            pltpu.make_async_copy(wm.at[0], wm_s, in_sem.at[7]),
        ]
        for load in loads[:2]:
            load.start()
        for load in loads[:2]:
            load.wait()
        for load in loads[2:]:
            load.start()
        sums_s[...] = jnp.zeros_like(sums_s)
        dm_s[...] = rows_times_transposed(df_s[...], wi_s[...])
        for load in loads[2:5]:
            load.wait()

        def first_norm(part):
            grad = dm_s[part, :] + da2_s[part, :]
            moved, gained = norm_backward(grad, a1_s[part, :], g1[...])
            da1_s[part, :] = moved
            low = moved.astype(BF16)
            da_s[part, :] = low
            add_rows(sums_s.at[0], gained)
            add_rows(sums_s.at[1], grad)
            add_rows(sums_s.at[2], low.astype(F32))

        over_chunks(2 * rows, first_norm)
        stores = [pltpu.make_async_copy(da1_s, da1_o, out_sem.at[0])]
        stores[0].start()
        for index in range(3):
            small_o[index : index + 1, :] = jnp.sum(sums_s[index], axis=0, keepdims=True)
        for load in loads[5:]:
            load.wait()
        dc_s[...] = rows_times_transposed(da_s[...], wm_s[...]).astype(BF16)
        stores.append(pltpu.make_async_copy(dc_s, dc_o, out_sem.at[1]))
        stores[1].start()
        put_blocks(w_s, transposed_times(c_s[...], da_s[...]), 0, place, orders[1:], False)
        stores.append(pltpu.make_async_copy(w_s.at[0], mix_o, out_sem.at[2]))
        stores[2].start()
        for copy in stores:
            copy.wait()


def attend_backward(span_rows, row_count, row_base, q_ref, k_ref, v_ref, dc_ref, bias_ref, dq_ref, dk_ref, dv_ref):
    blocks = row_count // span_rows
    scale = HEAD_DIM ** (-0.5)

    def one_pair(pair, carry):
        columns = pl.ds(pl.multiple_of(pair * PAIR, PAIR), PAIR)
        lane = lax.broadcasted_iota(jnp.int32, (span_rows, PAIR), 1)
        halves = (lane < HEAD_DIM, lane >= HEAD_DIM)
        for block in range(blocks):
            rows = pl.ds(pl.multiple_of(row_base + block * span_rows, BUCKET), span_rows)
            query = q_ref[rows, columns] * jnp.asarray(scale, BF16)
            keys = k_ref[rows, columns]
            value = v_ref[rows, columns]
            grad = dc_ref[rows, columns]
            zero = jnp.zeros_like(keys)
            bias = bias_ref[rows, 0:span_rows]
            dq = dk = dv = None
            for mine in halves:
                keys_own = jnp.where(mine, keys, zero)
                scores = rows_times_transposed(query, keys_own) + bias
                grad_part = rows_times_transposed(grad, jnp.where(mine, value, zero))
                top = jnp.max(scores, axis=-1, keepdims=True)
                weight = jnp.exp(scores - top)
                part = weight * (1.0 / jnp.sum(weight, axis=-1, keepdims=True))
                mean = jnp.sum(grad_part * part, axis=-1, keepdims=True)
                grad_scores = (part * (grad_part - mean)).astype(BF16)
                terms = (
                    rows_times(grad_scores, keys_own),
                    transposed_times(grad_scores, jnp.where(mine, query, zero)),
                    transposed_times(part.astype(BF16), jnp.where(mine, grad, zero)),
                )
                if dq is None:
                    dq, dk, dv = terms
                else:
                    dq, dk, dv = (dq + terms[0], dk + terms[1], dv + terms[2])
            dq_ref[rows, columns] = (dq * scale).astype(BF16)
            dk_ref[rows, columns] = dk.astype(BF16)
            dv_ref[rows, columns] = dv.astype(BF16)
        return carry

    lax.fori_loop(0, HEADS // 2, one_pair, 0)


def attend_kernel(
    orders, stacked, info, place, qa, qb, ka, kb, va, vb, dc, ha, hb, da1, wq, wk, wv, dh_in,
    dh_o, low_o, away_o, home_o, small_o,
    q_s, k_s, v_s, dc_s, h_s, dh_s, low_s, wq_s, wk_s, wv_s, dq_s, dk_s, dv_s, w_s, bias_s, sums_s, in_sem, out_sem,
):
    rows = qa.shape[0]

    @pl.when(info[0] == 1)
    def _():
        first = [
            pltpu.make_async_copy(source, target.at[part], in_sem.at[index])
            for index, (source, target, part) in enumerate(
                (
                    (qa, q_s, slice(0, rows)),
                    (ka, k_s, slice(0, rows)),
                    (va, v_s, slice(0, rows)),
                    (qb, q_s, slice(rows, 2 * rows)),
                    (kb, k_s, slice(rows, 2 * rows)),
                    (vb, v_s, slice(rows, 2 * rows)),
                    (dc, dc_s, slice(0, 2 * rows)),
                )
            )
        ]
        later = [
            pltpu.make_async_copy(da1, dh_s, in_sem.at[9]),
            pltpu.make_async_copy(wq.at[0], wq_s, in_sem.at[10]),
            pltpu.make_async_copy(wk.at[0], wk_s, in_sem.at[11]),
            pltpu.make_async_copy(wv.at[0], wv_s, in_sem.at[12]),
        ]
        for copy in first:
            copy.start()
        for micro, source in enumerate((ha, hb)):
            part = slice(micro * rows, (micro + 1) * rows)
            later.append(pltpu.make_async_copy(at_index(source, micro if stacked else None), h_s.at[part], in_sem.at[7 + micro]))
        for micro in range(2):
            base = 2 + 8 * micro
            for span in (2, 3):
                @pl.when((info[base] == 1) == (span == 2))
                def _(span=span, micro=micro, base=base):
                    fill_masks(span * BUCKET, rows, info, base, bias_s, None, micro * rows)
        for copy in first:
            copy.wait()
        for copy in later:
            copy.start()

        def one_micro(micro, carry):
            base = 2 + 8 * micro
            for span in (2, 3):
                @pl.when((info[base] == 1) == (span == 2))
                def _(span=span):
                    attend_backward(span * BUCKET, rows, micro * rows, q_s, k_s, v_s, dc_s, bias_s, dq_s, dk_s, dv_s)
            return carry

        lax.fori_loop(0, 2, one_micro, 0)
        for copy in later:
            copy.wait()
        stores = []
        for unit, grad in enumerate((dq_s, dk_s, dv_s)):
            put_blocks(w_s, transposed_times(h_s[...], grad[...]), unit, place, orders, False)
        stores.append(pltpu.make_async_copy(w_s.at[0:2], away_o, out_sem.at[0]))
        stores.append(pltpu.make_async_copy(w_s.at[2], home_o, out_sem.at[1]))
        for copy in stores:
            copy.start()
        dh_s[...] += rows_times_transposed(dq_s[...], wq_s[...])
        dh_s[...] += rows_times_transposed(dk_s[...], wk_s[...])
        dh_s[...] += rows_times_transposed(dv_s[...], wv_s[...])
        sums_s[...] = jnp.zeros_like(sums_s)

        def finish(part):
            low_s[part, :] = dh_s[part, :].astype(BF16)
            add_rows(sums_s.at[0], dq_s[part, :].astype(F32))
            add_rows(sums_s.at[1], dv_s[part, :].astype(F32))

        over_chunks(2 * rows, finish)
        for index in range(2):
            small_o[index : index + 1, :] = jnp.sum(sums_s[index], axis=0, keepdims=True)
        for micro in range(2):
            part = slice(micro * rows, (micro + 1) * rows)
            stores.append(pltpu.make_async_copy(dh_s.at[part], dh_o.at[micro], out_sem.at[2 + micro]))
            stores.append(pltpu.make_async_copy(low_s.at[part], low_o.at[micro], out_sem.at[4 + micro]))
        for copy in stores[2:]:
            copy.start()
        for copy in stores:
            copy.wait()


def run_kernel(kernel, outs, out_specs, in_specs, scratch, loads, stores, flops, bytes_moved, name, aliases=None):
    return pl.pallas_call(
        kernel,
        out_shape=outs,
        in_specs=in_specs,
        out_specs=out_specs,
        scratch_shapes=list(scratch) + [pltpu.SemaphoreType.DMA((loads,)), pltpu.SemaphoreType.DMA((stores,))],
        compiler_params=pltpu.CompilerParams(vmem_limit_bytes=VMEM_LIMIT),
        cost_estimate=pl.CostEstimate(flops=flops, bytes_accessed=bytes_moved, transcendentals=0),
        input_output_aliases=aliases or {},
        name=name,
    )


S = jax.ShapeDtypeStruct
V = pltpu.VMEM


def outer_gradient(info, place, orders, count, g, a2a, a2b, ua, ub, g2):
    rows, width = a2a.shape
    hidden = ua.shape[1]
    both = (2 * rows, width)
    block = (count, width // count, width)
    return run_kernel(
        functools.partial(outer_kernel, orders),
        (S(both, F32), S(both, BF16), S((2,) + block, BF16), S((2,) + block, BF16), S((3, width), F32)),
        [ANY] * 4 + [VM],
        [SM, SM] + [ANY] * 5 + [VM],
        [V(both, g.dtype), V(both, F32), V((2 * rows, hidden), BF16), V(both, F32), V(both, BF16), V((4,) + block, BF16), V((2 * rows, 1), F32), V((3, 8, width), F32)],
        6, 4, 4 * rows * width * hidden, 20_000_000, "outer_gradient",
    )(info, place, g, a2a, a2b, ua, ub, g2)


def inner_gradient(info, place, orders, count, dz, gpa, gpb, mla, mlb, wo):
    rows, width = mla.shape
    hidden = gpa.shape[1]
    both = (2 * rows, width)
    wide = (2 * rows, hidden)
    block = (count, width // count, width)
    return run_kernel(
        functools.partial(inner_kernel, orders),
        (S(wide, BF16), S((2,) + block, BF16), S((2,) + block, BF16), S((1, hidden), F32)),
        [ANY] * 3 + [VM],
        [SM, SM] + [ANY] * 6,
        [V(both, BF16), V(wide, BF16), V(both, BF16), V((hidden, width), BF16), V(wide, BF16), V((4,) + block, BF16), V((2 * rows, FFN_TILE), F32), V((2 * rows, FFN_TILE), F32), V((8, hidden), F32)],
        6, 3, 8 * rows * width * hidden, 25_000_000, "inner_gradient",
    )(info, place, dz, gpa, gpb, mla, mlb, wo)


def mixer_gradient(info, place, orders, count, df, wi, da2, a1a, a1b, ca, cb, wm, g1):
    rows, width = a1a.shape
    hidden = df.shape[1]
    both = (2 * rows, width)
    wide = (2 * rows, hidden)
    block = (count, width // count, width)
    return run_kernel(
        functools.partial(mixer_kernel, orders),
        (S(both, F32), S(both, BF16), S(block, BF16), S((3, width), F32)),
        [ANY] * 3 + [VM],
        [SM, SM] + [ANY] * 8 + [VM],
        [V(wide, BF16), V((width, hidden), BF16), V(both, F32), V(both, F32), V(both, BF16), V((width, width), BF16), V(both, F32), V(both, F32), V(both, BF16), V(both, BF16), V((1,) + block, BF16), V((3, 8, width), F32)],
        8, 3, 4 * rows * width * (hidden + 2 * width), 22_000_000, "mixer_gradient",
    )(info, place, df, wi, da2, a1a, a1b, ca, cb, wm, g1)


def attend_gradient(info, place, orders, count, qa, qb, ka, kb, va, vb, dc, ha, hb, da1, wq, wk, wv, dh_in):
    rows, width = qa.shape
    both = (2 * rows, width)
    block = (count, width // count, width)
    square = (width, width)
    return run_kernel(
        functools.partial(attend_kernel, orders, len(ha.shape) == 3),
        (S((2, rows, width), F32), S((2, rows, width), BF16), S((2,) + block, BF16), S(block, BF16), S((2, width), F32)),
        [ANY] * 4 + [VM],
        [SM, SM] + [ANY] * 14,
        [V(both, BF16)] * 5 + [V(both, F32), V(both, BF16)] + [V(square, BF16)] * 3 + [V(both, BF16)] * 3 + [V((3,) + block, BF16), V((2 * rows, 3 * BUCKET), F32), V((2, 8, width), F32)],
        13, 6, 24 * rows * width * width, 20_000_000, "attend_gradient",
        {15: 0},
    )(info, place, qa, qb, ka, kb, va, vb, dc, ha, hb, da1, wq, wk, wv, dh_in)


EXCHANGES = ((1, 2, 4, 8), (2, 1, 4, 8), (4, 1, 2, 8), (4, 2, 1, 8))


def exchange(value, bit):
    count = lax.axis_size("dp")
    return lax.ppermute(value, "dp", [(index, index ^ bit) for index in range(count)])


def reduce_units(orders, owned, away, home, extra):
    received = lax.ppermute(away, "section", [(owned[1], 1 - owned[1])])
    count = away.shape[1]
    sends, keeps = ([], [])
    for color in range(2):
        mine = home[color]
        other = received[color]
        if extra is not None and color == 1:
            mine = jnp.concatenate([mine, extra], axis=1)
            other = jnp.concatenate([other, jnp.zeros_like(extra)], axis=1)
        half = count // 2
        sends.append(jnp.where(owned[0], mine[half:], other[half:]))
        keeps.append(jnp.where(owned[0], mine[:half], other[:half]))
    paths = [EXCHANGES[order] for order in orders]
    for step in range(4):
        bits = [path[step] for path in paths]
        if bits[0] == bits[1] and sends[0].shape == sends[1].shape:
            both = exchange(jnp.stack(sends), bits[0])
            arrived = [both[0], both[1]]
        elif bits[0] == bits[1]:
            joined = exchange(jnp.concatenate(sends, axis=1), bits[0])
            height = sends[0].shape[1]
            arrived = [joined[:, :height], joined[:, height:]]
        else:
            arrived = [exchange(value, bit) for value, bit in zip(sends, bits)]
        totals = [keep.astype(F32) + part.astype(F32) for keep, part in zip(keeps, arrived)]
        if step == 3:
            return [total[0] for total in totals]
        half = totals[0].shape[0] // 2
        sends = [total[half:].astype(BF16) for total in totals]
        keeps = [total[:half].astype(BF16) for total in totals]


def layer_backward(live, metas, place, orders, count, saved, inputs, grad, params, grad_buffer):
    wq, bq, wk, wv, bv, wm, bm, g1, s1, wi, bi, wo, bo, g2, s2 = params
    (ya, qa, ka, va, ca, a1a, mla, ua, gpa, a2a), (yb, qb, kb, vb, cb, a1b, mlb, ub, gpb, a2b) = saved
    info = jnp.concatenate([jnp.stack([live, live]), metas[0], metas[1]])
    da2, dz, outer_away, outer_home, small_two = outer_gradient(info, place, orders[0], count, grad, a2a, a2b, ua, ub, g2)
    df, inner_away, inner_home, small_inner = inner_gradient(info, place, orders[1], count, dz, gpa, gpb, mla, mlb, wo)
    da1, dc, mix_home, small_one = mixer_gradient(info, place, orders[2], count, df, wi, da2, a1a, a1b, ca, cb, wm, g1)
    dh, low, attend_away, value_home, small_attend = attend_gradient(
        info, place, orders[2], count, qa, qb, ka, kb, va, vb, dc, inputs[0], inputs[1], da1, wq, wk, wv, grad_buffer
    )
    smalls = (small_attend[0], small_attend[1], small_one[2], small_one[0], small_one[1], small_two[2], small_two[0], small_two[1])
    return (dh, low, (outer_away, outer_home), (inner_away, inner_home), (attend_away, (value_home, mix_home)), smalls, small_inner[0])


def per_device(
    tokens, cotangent, bucket, batch_size, lengths, query_weight, query_offset, keys_weight, value_weight, value_offset,
    mixer_weight, mixer_offset, first_gain, first_shift, inner_weight, inner_offset, outer_weight, outer_offset,
    second_gain, second_shift,
):
    params = (
        query_weight, query_offset, keys_weight, value_weight, value_offset, mixer_weight, mixer_offset, first_gain,
        first_shift, inner_weight, inner_offset, outer_weight, outer_offset, second_gain, second_shift,
    )
    section = lax.axis_index("section")
    group = lax.axis_index("dp")
    groups = lax.axis_size("dp")
    width = tokens.shape[2]
    hidden = inner_offset.shape[1]
    hypercube = groups == 16 and width % (16 * groups) == 0
    count = groups if hypercube else 1
    one = jnp.ones((), jnp.int32)
    at_first = (section == 0).astype(jnp.int32)
    at_second = (section == 1).astype(jnp.int32)
    metas = [jnp.concatenate([bucket[m : m + 1], batch_size[m : m + 1], lengths[m]]) for m in range(2)]

    def forward_info(live, source, meta):
        return jnp.concatenate([jnp.stack([live, source]), meta])

    down = [(0, 1)]
    slot_a = forward_layer(forward_info(at_first, 0 * one, metas[0]), tokens, 0, tokens[0], params)
    received_a = lax.ppermute(slot_a[0], "section", down)
    meta_b = jnp.where(section == 0, metas[1], metas[0])
    slot_b = forward_layer(forward_info(one, at_second, meta_b), tokens, 1, received_a, params)
    received_b = lax.ppermute(slot_b[0], "section", down)
    slot_c = forward_layer(forward_info(at_second, one, metas[1]), tokens, 0, received_b, params)
    layer_out = jnp.stack([jnp.where(section == 0, slot_a[0], slot_b[0]), jnp.where(section == 0, slot_b[0], slot_c[0])])

    dest = jnp.arange(groups, dtype=jnp.int32)
    relative = jnp.bitwise_xor(dest, group)
    if hypercube:
        spots = []
        for path in EXCHANGES:
            spot = jnp.zeros_like(dest)
            for index, bit in enumerate(path):
                spot = spot + jnp.bitwise_and(relative // bit, 1) * (8 >> index)
            spots.append(spot)
        place = jnp.concatenate(spots)
    else:
        place = dest
    orders = ((0, 1), (2, 3), (0, 1))
    buffer = jnp.zeros(tokens.shape, F32)
    second = layer_backward(
        at_second, metas, place, orders, count, (slot_b, slot_c), (received_a, received_b), cotangent, params, buffer
    )
    received_grad = lax.ppermute(second[1], "section", [(1, 0)])
    first = layer_backward(
        at_first, metas, place, orders, count, (slot_a, slot_b), (tokens, tokens), received_grad, params, second[0]
    )
    input_grad = first[0]
    at_owner = section == 1

    def small_blocks(smalls, small_inner):
        flat = jnp.stack(smalls).reshape(8, groups, width // groups).transpose(1, 0, 2).reshape(groups, -1)
        return jnp.concatenate([flat, small_inner.reshape(groups, -1)], axis=1)

    if hypercube:
        summed = []
        for layer, parts in ((1, second), (0, first)):
            owned = (section == layer, layer)
            dh, low, outer, inner, attend, smalls, small_inner = parts
            blocks = small_blocks(smalls, small_inner)
            blocks = jnp.pad(blocks, ((0, 0), (0, width - blocks.shape[1]))).astype(BF16)
            order = jnp.argsort(place[groups : 2 * groups])
            blocks = jnp.where(owned[0], blocks[order], jnp.zeros_like(blocks))
            extra = jnp.pad(blocks[:, None, :], ((0, 0), (0, 7), (0, 0)))
            results = [
                reduce_units(orders[0], owned, outer[0], outer[1], None),
                reduce_units(orders[1], owned, inner[0], inner[1], None),
                reduce_units(orders[2], owned, attend[0], attend[1], extra),
            ]
            summed.append(results)
        final = []
        for second_part, first_part in zip(summed[0], summed[1]):
            height = width // groups
            send = jnp.stack([jnp.where(section == 0, a[:height], b[:height]) for a, b in zip(second_part, first_part)])
            back = lax.ppermute(send, "section", [(0, 1), (1, 0)])
            mine = [jnp.where(at_owner, a, b) for a, b in zip(second_part, first_part)]
            final.append((back[0], back[1], mine[0], mine[1]))
        height = width // groups
        outer_grad = jnp.concatenate(final[0], axis=0)
        inner_grad = jnp.concatenate(final[1], axis=1)
        query_grad, keys_grad, value_grad, mixed = final[2]
        mixer_grad = mixed[:height]
        line = mixed[height]
        small = [line[index * height : (index + 1) * height] for index in range(8)]
        small_wide = line[8 * height : 8 * height + hidden // groups]
    else:
        def scatter(value):
            return lax.psum_scatter(value, "dp", scatter_dimension=0, tiled=True)

        final = []
        for dh, low, outer, inner, attend, smalls, small_inner in (second, first):
            outer_full = jnp.concatenate([outer[0], outer[1]]).reshape(hidden, width)
            inner_full = jnp.concatenate([inner[0][0, 0], inner[0][1, 0], inner[1][0, 0], inner[1][1, 0]], axis=1)
            squares = [attend[0][0, 0], attend[0][1, 0], attend[1][0][0], attend[1][1][0]]
            final.append([scatter(outer_full), scatter(inner_full)] + [scatter(square) for square in squares] + [scatter(value) for value in smalls] + [scatter(small_inner)])
        chosen = [jnp.where(at_owner, a, b).astype(F32) for a, b in zip(final[0], final[1])]
        outer_grad, inner_grad, query_grad, keys_grad, value_grad, mixer_grad = chosen[:6]
        small = chosen[6:14]
        small_wide = chosen[14]
    outputs = (
        layer_out, input_grad, query_grad, small[0], keys_grad, value_grad, small[1], mixer_grad, small[2], small[3],
        small[4], inner_grad, small_wide, outer_grad, small[5], small[6], small[7],
    )
    return tuple(piece[None] for piece in outputs)


def solution(mesh):
    from jax.sharding import PartitionSpec as P

    matrix = P("section", None, None)
    vector = P("section", None)
    in_specs = (
        P("dp", None, None), P("dp", None, None), P("dp"), P("dp"), P("dp", None), matrix, vector, matrix, matrix, vector,
        matrix, vector, vector, vector, matrix, vector, matrix, vector, vector, vector,
    )
    rows = P("section", "dp", None, None)
    grad = P("section", "dp", None)
    small = P("section", "dp")
    out_specs = (rows, rows, grad, small, grad, grad, small, grad, small, small, small, grad, small, grad, small, small, small)
    return jax.shard_map(per_device, mesh=mesh, in_specs=in_specs, out_specs=out_specs, check_vma=False)
```

time: 1530 us -> 440 us (0.29)
  waiting for transfers between devices: 844 us -> 186 us
  matrix products: 235 us -> 0 us
  other arithmetic: 178 us -> 29 us
  Pallas kernels: 0 us -> 136 us
  blocking collectives: 80.3 us -> 0 us
  local copies, waits for them, and re-layouts: 91.7 us -> 28.2 us
  loops' own time: 18.5 us -> 0 us
    reduce_scatter x6 -> x0, waiting for transfers between devices: 786 us -> none  [per_device(): summed = lax.psum_scatter(totals, 'dp', scatter_dimension=0, tiled=True)]
    dot_general x58 -> x0, matrix products: 212 us -> none  [the longest x36 113 us: contract(): return jnp.einsum(pattern, left, right, preferred_element_type=jnp.float32)]
    pallas_call x0 -> x11, Pallas kernels: none -> 136 us  [the longest x2 35.7 us: attend_gradient(): run_kernel(functools.partial(attend_kernel, orders, len(ha.shape) == 3),...]
    ppermute x6 -> x48, waiting for transfers between devices: 54.9 us -> 186 us  [the longest x36 104 us: exchange(): lax.ppermute(value, 'dp', [(index, index ^ bit) for index in range(count)])]
    add x27 -> x2, other arithmetic: 115 us -> 0.03 us  [per_device(): spot = spot + jnp.bitwise_and(relative // bit, 1) * (8 >> index)]
    unnamed x1 -> x0, blocking collectives: 80.3 us -> none
    dynamic_slice x19 -> x0, local copies, waits for them, and re-layouts: 24.1 us -> none  [the longest x6 7.88 us: per_device(): lax.scan(forward_tick, start_rows, jnp.arange(micro_count + 1))]
    sub x4 -> x0, matrix products: 23.9 us -> none  [forward_pieces(): attention = jax.nn.softmax(scores, axis=-1)]
  transfers between devices with their start and end apart: 12 -> 48, of which waited for: 10 -> 25; matrix products, arithmetic and copies ran while one was open for 9% -> 10% of each run, Pallas kernels for 0% -> 18%
where the time goes in v1:
time: 440 us; the launch traced here: 437 us
  waiting for transfers between devices  186 us (42%)
  Pallas kernels  136 us (31%)
  starting transfers between devices  56 us (13%)
  other arithmetic  29 us (7%)
  local copies, waits for them, and re-layouts  28.2 us (6%)
    ppermute x36, waiting for transfers between devices, exchange(): lax.ppermute(value, 'dp', [(index, index ^ bit) for index in range(count)])  104 us
    ppermute x1, waiting for transfers between devices, per_device(): received_grad = lax.ppermute(second[1], 'section', [(1, 0)])  81.6 us
    ppermute x36, starting transfers between devices, exchange(): lax.ppermute(value, 'dp', [(index, index ^ bit) for index in range(count)])  42.3 us
    pallas_call x2, Pallas kernels, attend_gradient(): run_kernel(functools.partial(attend_kernel, orders, len(ha.shape) == 3),...  35.7 us
    pallas_call x3, Pallas kernels, forward_layer(): pl.pallas_call(functools.partial(forward_kernel, tok_index), out_shape=ou...  35.5 us
    pallas_call x2, Pallas kernels, inner_gradient(): run_kernel(functools.partial(inner_kernel, orders), (S(wide, BF16), S((2,...  31.9 us
    pallas_call x2, Pallas kernels, mixer_gradient(): run_kernel(functools.partial(mixer_kernel, orders), (S(both, F32), S(both...  18.8 us
    pallas_call x2, Pallas kernels, outer_gradient(): run_kernel(functools.partial(outer_kernel, orders), (S(both, F32), S(both...  13.7 us
  transfers between devices with their start and end apart: 48, of which 25 were waited for; matrix products, arithmetic and copies ran while one was open for 10% of the time, Pallas kernels for 18%

profile of v1, /device:TPU:0, one launch (start us, length us, event | category | flops | bytes accessed | tf_op | source)
XLA Modules:
  0.0 436.6 jit_solution(6087331698643634947)
XLA Ops:
  6.6 17.1 %layer_forward.3 = (bf16[384,768]{1,0:T(8,128)(2,1)}, bf16[384,768]{1,0:T(8,128)(2,1)}, bf16[384,768]{1,0:T(8,128)(2,1)}, bf16[384,768]{1,0:T(8,128)(2,1)}, bf16...) custom-call(s32[10]{0:T(128)} %concatenate.66.info, ...), custom_call_target="tpu_custom_call" | custom-call | flops 5435817984 | bytes 30000000 | tf_op jit(solution)/shard_map/layer_forward/pallas_call | solution.py:291
  25.0 2.7 broadcast_select_fusion.1
  29.0 17.5 %layer_forward.4 = (bf16[384,768]{1,0:T(8,128)(2,1)}, bf16[384,768]{1,0:T(8,128)(2,1)}, bf16[384,768]{1,0:T(8,128)(2,1)}, bf16[384,768]{1,0:T(8,128)(2,1)}, bf16...) custom-call(s32[10]{0:T(128)} %pad_add_fusion.info, ...), custom_call_target="tpu_custom_call" | custom-call | flops 5435817984 | bytes 30000000 | tf_op jit(solution)/shard_map/layer_forward/pallas_call | solution.py:291
  47.8 3.2 concatenate.73.info
  51.0 3.2 concatenate.71.info
  61.2 13.4 %inner_gradient.2 = (bf16[768,3072]{1,0:T(8,128)(2,1)}, bf16[2,16,48,768]{3,2,1,0:T(8,128)(2,1)}, bf16[2,16,48,768]{3,2,1,0:T(8,128)(2,1)}, f32[1,3072]{1,0:T(1,128)}) custom-call(s32[18]{0:T(128)} %concatenate.73.info, s32[64]{0:T(128)} %pad_add_fusion.1.place, bf16[768,768]{1,0:T(8,128)(2,1)} %get-tuple-element.99.dz, ...), custom_call_target="tpu_custom_call" | custom-call | flops 7247757312 | bytes 25000000 | tf_op jit(solution)/shard_map/inner_gradient/pallas_call | solution.py:699
  77.6 4.1 attend_gradient.2
  90.8 81.6 %collective-permute-done.2.g = bf16[2,384,768]{2,1,0:T(8,128)(2,1)} collective-permute-done((bf16[2,384,768]{2,1,0:T(8,128)(2,1)}, bf16[2,384,768]{2,1,0:T(8,128)(2,1)}, u32[]{:S(2)}, u32[]{:S(2)}) %collective-permute-start.2) | collective-permute-done | bytes 1179680 | tf_op jit(solution)/shard_map/ppermute | solution.py:846
  172.4 12.3 %outer_gradient.3 = (f32[768,768]{1,0:T(8,128)}, bf16[768,768]{1,0:T(8,128)(2,1)}, bf16[2,16,48,768]{3,2,1,0:T(8,128)(2,1)}, bf16[2,16,48,768]{3,2,1,0:T(8,128)(2,1)}, f32[3,768]{1,0:T(4,128)}) custom-call(s32[18]{0:T(128)} %concatenate.71.info, s32[64]{0:T(128)} %pad_add_fusion.1.place, bf16[2,384,768]{2,1,0:T(8,128)(2,1)} %collective-permute-done.2.g, ...), custom_call_target="tpu_custom_call" | custom-call | flops 3623878656 | bytes 20000000 | tf_op jit(solution)/shard_map/outer_gradient/pallas_call | solution.py:683
  185.5 18.5 %inner_gradient.3 = (bf16[768,3072]{1,0:T(8,128)(2,1)}, bf16[2,16,48,768]{3,2,1,0:T(8,128)(2,1)}, bf16[2,16,48,768]{3,2,1,0:T(8,128)(2,1)}, f32[1,3072]{1,0:T(1,128)}) custom-call(s32[18]{0:T(128)} %concatenate.71.info, s32[64]{0:T(128)} %pad_add_fusion.1.place, bf16[768,768]{1,0:T(8,128)(2,1)} %get-tuple-element.115.dz, ...), custom_call_target="tpu_custom_call" | custom-call | flops 7247757312 | bytes 25000000 | tf_op jit(solution)/shard_map/inner_gradient/pallas_call | solution.py:699
  204.0 17.3 %mixer_gradient.3 = (f32[768,768]{1,0:T(8,128)}, bf16[768,768]{1,0:T(8,128)(2,1)}, bf16[16,48,768]{2,1,0:T(8,128)(2,1)}, f32[3,768]{1,0:T(4,128)}) custom-call(s32[18]{0:T(128)} %concatenate.71.info, s32[64]{0:T(128)} %pad_add_fusion.1.place, bf16[768,3072]{1,0:T(8,128)(2,1)} %get-tuple-element.118.df, bf16[1,768,3072]{2,1,0:T(8,128)(2,1)} %wi.9, ...), custom_call_target="tpu_custom_call" | custom-call | flops 5435817984 | bytes 22000000 | tf_op jit(solution)/shard_map/mixer_gradient/pallas_call | solution.py:715
  222.1 2.7 collective-permute-start.40
  224.9 31.5 %attend_gradient.3 = (f32[2,384,768]{2,1,0:T(8,128)}, bf16[2,384,768]{2,1,0:T(8,128)(2,1)}, bf16[2,16,48,768]{3,2,1,0:T(8,128)(2,1)}, bf16[16,48,768]{2,1,0:T(8,128)(2,1)}, f32[2,768]{1,0:T(2,128)}) custom-call(s32[18]{0:T(128)} %concatenate.71.info, s32[64]{0:T(128)} %pad_add_fusion.1.place, ...), custom_call_target="tpu_custom_call", output_to_operand_aliasing={{0}: (15, {})} | custom-call | flops 5435817984 | bytes 20000000 | tf_op jit(solution)/shard_map/attend_gradient/pallas_call | solution.py:730
  261.6 3.0 collective-permute-start.34
  283.1 2.4 collective-permute-done.37
  287.2 5.1 %collective-permute-done.5 = bf16[4,48,768]{2,1,0:T(8,128)(2,1)S(1)} collective-permute-done((bf16[4,48,768]{2,1,0:T(8,128)(2,1)S(1)}, bf16[4,48,768]{2,1,0:T(8,128)(2,1)S(1)}, u32[]{:S(2)}, u32[]{:S(2)}) %collective-permute-start.5) | collective-permute-done | bytes 294944 | tf_op jit(solution)/shard_map/ppermute | solution.py:746
  292.9 6.1 %collective-permute-done.35 = bf16[4,48,768]{2,1,0:T(8,128)(2,1)S(1)} collective-permute-done((bf16[4,48,768]{2,1,0:T(8,128)(2,1)S(1)}, bf16[4,48,768]{2,1,0:T(8,128)(2,1)S(1)}, u32[]{:S(2)}, u32[]{:S(2)}) %collective-permute-start.35) | collective-permute-done | bytes 294944 | tf_op jit(solution)/shard_map/ppermute | solution.py:746
  299.1 9.7 %collective-permute-done.7 = bf16[4,56,768]{2,1,0:T(8,128)(2,1)S(1)} collective-permute-done((bf16[4,56,768]{2,1,0:T(8,128)(2,1)S(1)}, bf16[4,56,768]{2,1,0:T(8,128)(2,1)S(1)}, u32[]{:S(2)}, u32[]{:S(2)}) %collective-permute-start.7) | collective-permute-done | bytes 344096 | tf_op jit(solution)/shard_map/ppermute | solution.py:746
  310.6 5.0 %collective-permute-done.38 = bf16[2,2,48,768]{3,2,1,0:T(8,128)(2,1)S(1)} collective-permute-done((bf16[2,2,48,768]{3,2,1,0:T(8,128)(2,1)S(1)}, bf16[2,2,48,768]{3,2,1,0:T(8,128)(2,1)S(1)}, u32[]{:S(2)}, u32[]{:S(2)}) %collective-permute-start.38) | collective-permute-done | bytes 294944 | tf_op jit(solution)/shard_map/ppermute | solution.py:746
  331.7 8.5 %collective-permute-done.22 = bf16[4,48,768]{2,1,0:T(8,128)(2,1)S(1)} collective-permute-done((bf16[4,48,768]{2,1,0:T(8,128)(2,1)S(1)}, bf16[4,48,768]{2,1,0:T(8,128)(2,1)S(1)}, u32[]{:S(2)}, u32[]{:S(2)}) %collective-permute-start.22) | collective-permute-done | bytes 294944 | tf_op jit(solution)/shard_map/ppermute | solution.py:746
  342.9 10.3 %collective-permute-done.23 = bf16[2,48,768]{2,1,0:T(8,128)(2,1)S(1)} collective-permute-done((bf16[2,48,768]{2,1,0:T(8,128)(2,1)S(1)}, bf16[2,48,768]{2,1,0:T(8,128)(2,1)S(1)}, u32[]{:S(2)}, u32[]{:S(2)}) %collective-permute-start.23) | collective-permute-done | bytes 147488 | tf_op jit(solution)/shard_map/ppermute | solution.py:746
  353.8 4.5 %collective-permute-done.21 = bf16[2,48,768]{2,1,0:T(8,128)(2,1)S(1)} collective-permute-done((bf16[2,48,768]{2,1,0:T(8,128)(2,1)S(1)}, bf16[2,48,768]{2,1,0:T(8,128)(2,1)S(1)}, u32[]{:S(2)}, u32[]{:S(2)}) %collective-permute-start.21) | collective-permute-done | bytes 147488 | tf_op jit(solution)/shard_map/ppermute | solution.py:746
  360.5 4.8 %collective-permute-start.9 = (bf16[1,104,768]{2,1,0:T(8,128)(2,1)S(1)}, bf16[1,104,768]{2,1,0:T(8,128)(2,1)S(1)}, u32[]{:S(2)}, u32[]{:S(2)}) collective-permute-start(bf16[1,104,768]{2,1,0:T(8,128)(2,1)S(1)} %pad_maximum_fusion.9), channel_id=1, source_target_pairs={{0,16},{2,18},{4,20},{6,22},{8,24},{10,26},{12,28},{14,30},{16,0},... | collective-permute-start | bytes 479240 | tf_op jit(solution)/shard_map/ppermute | solution.py:746
  369.0 3.4 collective-permute-done.13
  374.0 5.2 %collective-permute-done.12 = bf16[4,48,768]{2,1,0:T(8,128)(2,1)S(1)} collective-permute-done((bf16[4,48,768]{2,1,0:T(8,128)(2,1)S(1)}, bf16[4,48,768]{2,1,0:T(8,128)(2,1)S(1)}, u32[]{:S(2)}, u32[]{:S(2)}) %collective-permute-start.12) | collective-permute-done | bytes 294944 | tf_op jit(solution)/shard_map/ppermute | solution.py:746
  379.5 6.3 %collective-permute-done.42 = bf16[4,48,768]{2,1,0:T(8,128)(2,1)S(1)} collective-permute-done((bf16[4,48,768]{2,1,0:T(8,128)(2,1)S(1)}, bf16[4,48,768]{2,1,0:T(8,128)(2,1)S(1)}, u32[]{:S(2)}, u32[]{:S(2)}) %collective-permute-start.42) | collective-permute-done | bytes 294944 | tf_op jit(solution)/shard_map/ppermute | solution.py:746
  386.0 7.1 %collective-permute-done.14 = bf16[4,56,768]{2,1,0:T(8,128)(2,1)S(1)} collective-permute-done((bf16[4,56,768]{2,1,0:T(8,128)(2,1)S(1)}, bf16[4,56,768]{2,1,0:T(8,128)(2,1)S(1)}, u32[]{:S(2)}, u32[]{:S(2)}) %collective-permute-start.14) | collective-permute-done | bytes 344096 | tf_op jit(solution)/shard_map/ppermute | solution.py:746
  393.5 6.3 %collective-permute-done.45 = bf16[2,2,48,768]{3,2,1,0:T(8,128)(2,1)S(1)} collective-permute-done((bf16[2,2,48,768]{3,2,1,0:T(8,128)(2,1)S(1)}, bf16[2,2,48,768]{3,2,1,0:T(8,128)(2,1)S(1)}, u32[]{:S(2)}, u32[]{:S(2)}) %collective-permute-start.45) | collective-permute-done | bytes 294944 | tf_op jit(solution)/shard_map/ppermute | solution.py:746
  400.3 3.3 collective-permute-start.46
  404.4 2.4 collective-permute-done.46
  415.5 4.9 %collective-permute-done.16 = bf16[1,104,768]{2,1,0:T(8,128)(2,1)S(1)} collective-permute-done((bf16[1,104,768]{2,1,0:T(8,128)(2,1)S(1)}, bf16[1,104,768]{2,1,0:T(8,128)(2,1)S(1)}, u32[]{:S(2)}, u32[]{:S(2)}) %collective-permute-start.16) | collective-permute-done | bytes 159776 | tf_op jit(solution)/shard_map/ppermute | solution.py:746
  424.8 8.8 %collective-permute-done.31 = bf16[2,1,48,768]{3,2,1,0:T(8,128)(2,1)S(1)} collective-permute-done((bf16[2,1,48,768]{3,2,1,0:T(8,128)(2,1)S(1)}, bf16[2,1,48,768]{3,2,1,0:T(8,128)(2,1)S(1)}, u32[]{:S(2)}, u32[]{:S(2)}) %collective-permute-start.31) | collective-permute-done | bytes 147488 | tf_op jit(solution)/shard_map/ppermute | solution.py:746
  (273 shorter events, 102.3 us)
Async XLA Ops:
  46.5 11.5 %collective-permute-start.1 = (bf16[384,768]{1,0:T(8,128)(2,1)}, bf16[384,768]{1,0:T(8,128)(2,1)S(1)}, u32[]{:S(2)}, u32[]{:S(2)}) collective-permute-start(bf16[384,768]{1,0:T(8,128)(2,1)} %get-tuple-element.84), channel_id=1, source_target_pairs={{0,1},{2,3},{4,5},{6,7},{8,9},{10,11},{12,13},{14,15},{16,17},{18,... | collective-permute-start | bytes 1769480 | tf_op jit(solution)/shard_map/ppermute | solution.py:825
  81.8 90.7 %collective-permute-start.2 = (bf16[2,384,768]{2,1,0:T(8,128)(2,1)}, bf16[2,384,768]{2,1,0:T(8,128)(2,1)}, u32[]{:S(2)}, u32[]{:S(2)}) collective-permute-start(bf16[2,384,768]{2,1,0:T(8,128)(2,1)} %get-tuple-element.112), channel_id=1, source_target_pairs={{1,0},{3,2},{5,4},{7,6},{9,8},{11,10},{13,12},{15,14},{17,16},{19,... | collective-permute-start | bytes 3538952 | tf_op jit(solution)/shard_map/ppermute | solution.py:846
  83.2 176.5 %collective-permute-start.33 = (bf16[2,16,48,768]{3,2,1,0:T(8,128)(2,1)}, bf16[2,16,48,768]{3,2,1,0:T(8,128)(2,1)}, u32[]{:S(2)}, u32[]{:S(2)}) collective-permute-start(bf16[2,16,48,768]{3,2,1,0:T(8,128)(2,1)} %get-tuple-element.146), channel_id=1, source_target_pairs={{1,0},{3,2},{5,4},{7,6},{9,8},{11,10},{13,12},{15,14},{17,16},{19,... | collective-permute-start | bytes 7077896 | tf_op jit(solution)/shard_map/ppermute | solution.py:750
  86.2 178.9 %collective-permute-start.3 = (bf16[2,16,48,768]{3,2,1,0:T(8,128)(2,1)}, bf16[2,16,48,768]{3,2,1,0:T(8,128)(2,1)}, u32[]{:S(2)}, u32[]{:S(2)}) collective-permute-start(bf16[2,16,48,768]{3,2,1,0:T(8,128)(2,1)} %get-tuple-element.127), channel_id=1, source_target_pairs={{1,0},{3,2},{5,4},{7,6},{9,8},{11,10},{13,12},{15,14},{17,16},{19,... | collective-permute-start | bytes 7077896 | tf_op jit(solution)/shard_map/ppermute | solution.py:750
  87.5 181.8 %collective-permute-start.18 = (bf16[2,16,48,768]{3,2,1,0:T(8,128)(2,1)}, bf16[2,16,48,768]{3,2,1,0:T(8,128)(2,1)}, u32[]{:S(2)}, u32[]{:S(2)}) collective-permute-start(bf16[2,16,48,768]{3,2,1,0:T(8,128)(2,1)} %get-tuple-element.142), channel_id=1, source_target_pairs={{1,0},{3,2},{5,4},{7,6},{9,8},{11,10},{13,12},{15,14},{17,16},{19,... | collective-permute-start | bytes 7077896 | tf_op jit(solution)/shard_map/ppermute | solution.py:750
  222.1 95.4 %collective-permute-start.40 = (bf16[2,16,48,768]{3,2,1,0:T(8,128)(2,1)}, bf16[2,16,48,768]{3,2,1,0:T(8,128)(2,1)}, u32[]{:S(2)}, u32[]{:S(2)}) collective-permute-start(bf16[2,16,48,768]{3,2,1,0:T(8,128)(2,1)} %get-tuple-element.148), channel_id=1, source_target_pairs={{0,1},{2,3},{4,5},{6,7},{8,9},{10,11},{12,13},{14,15},{16,17},{18,... | collective-permute-start | bytes 7077896 | tf_op jit(solution)/shard_map/ppermute | solution.py:750
  261.6 10.9 %collective-permute-start.34 = (bf16[8,48,768]{2,1,0:T(8,128)(2,1)S(1)}, bf16[8,48,768]{2,1,0:T(8,128)(2,1)S(1)}, u32[]{:S(2)}, u32[]{:S(2)}) collective-permute-start(bf16[8,48,768]{2,1,0:T(8,128)(2,1)S(1)} %get-tuple-element.159), channel_id=1, source_target_pairs={{0,2},{2,0},{4,6},{6,4},{8,10},{10,8},{12,14},{14,12},{16,18},{18,... | collective-permute-start | bytes 1769480 | tf_op jit(solution)/shard_map/ppermute | solution.py:746
  264.6 9.9 %collective-permute-start.36 = (bf16[8,48,768]{2,1,0:T(8,128)(2,1)S(1)}, bf16[8,48,768]{2,1,0:T(8,128)(2,1)S(1)}, u32[]{:S(2)}, u32[]{:S(2)}) collective-permute-start(bf16[8,48,768]{2,1,0:T(8,128)(2,1)S(1)} %get-tuple-element.160), channel_id=1, source_target_pairs={{0,4},{2,6},{4,0},{6,2},{8,12},{10,14},{12,8},{14,10},{16,20},{18,... | collective-permute-start | bytes 1769480 | tf_op jit(solution)/shard_map/ppermute | solution.py:746
  266.3 12.5 %collective-permute-start.4 = (bf16[8,48,768]{2,1,0:T(8,128)(2,1)S(1)}, bf16[8,48,768]{2,1,0:T(8,128)(2,1)S(1)}, u32[]{:S(2)}, u32[]{:S(2)}) collective-permute-start(bf16[8,48,768]{2,1,0:T(8,128)(2,1)S(1)} %fusion.22), channel_id=1, source_target_pairs={{0,2},{2,0},{4,6},{6,4},{8,10},{10,8},{12,14},{14,12},{16,18},{18,... | collective-permute-start | bytes 1769480 | tf_op jit(solution)/shard_map/ppermute | solution.py:746
  269.4 12.9 %collective-permute-start.6 = (bf16[8,56,768]{2,1,0:T(8,128)(2,1)S(1)}, bf16[8,56,768]{2,1,0:T(8,128)(2,1)S(1)}, u32[]{:S(2)}, u32[]{:S(2)}) collective-permute-start(bf16[8,56,768]{2,1,0:T(8,128)(2,1)S(1)} %fusion.9), channel_id=1, source_target_pairs={{0,4},{2,6},{4,0},{6,2},{8,12},{10,14},{12,8},{14,10},{16,20},{18,... | collective-permute-start | bytes 2064392 | tf_op jit(solution)/shard_map/ppermute | solution.py:746
  272.9 50.7 %collective-permute-start.10 = (bf16[2,16,48,768]{3,2,1,0:T(8,128)(2,1)S(1)}, bf16[2,16,48,768]{3,2,1,0:T(8,128)(2,1)S(1)}, u32[]{:S(2)}, u32[]{:S(2)}) collective-permute-start(bf16[2,16,48,768]{3,2,1,0:T(8,128)(2,1)S(1)} %copy-done.16), channel_id=1, source_target_pairs={{0,1},{2,3},{4,5},{6,7},{8,9},{10,11},{12,13},{14,15},{16,17},{18,... | collective-permute-start | bytes 7077896 | tf_op jit(solution)/shard_map/ppermute | solution.py:750
  274.5 50.5 %collective-permute-start.25 = (bf16[2,16,48,768]{3,2,1,0:T(8,128)(2,1)S(1)}, bf16[2,16,48,768]{3,2,1,0:T(8,128)(2,1)S(1)}, u32[]{:S(2)}, u32[]{:S(2)}) collective-permute-start(bf16[2,16,48,768]{3,2,1,0:T(8,128)(2,1)S(1)} %copy-done.15), channel_id=1, source_target_pairs={{0,1},{2,3},{4,5},{6,7},{8,9},{10,11},{12,13},{14,15},{16,17},{18,... | collective-permute-start | bytes 7077896 | tf_op jit(solution)/shard_map/ppermute | solution.py:750
  282.3 9.9 %collective-permute-start.5 = (bf16[4,48,768]{2,1,0:T(8,128)(2,1)S(1)}, bf16[4,48,768]{2,1,0:T(8,128)(2,1)S(1)}, u32[]{:S(2)}, u32[]{:S(2)}) collective-permute-start(bf16[4,48,768]{2,1,0:T(8,128)(2,1)S(1)} %slice.949), channel_id=1, source_target_pairs={{0,4},{2,6},{4,0},{6,2},{8,12},{10,14},{12,8},{14,10},{16,20},{18,... | collective-permute-start | bytes 884744 | tf_op jit(solution)/shard_map/ppermute | solution.py:746
  285.5 35.3 %collective-permute-start.19 = (bf16[2,8,48,768]{3,2,1,0:T(8,128)(2,1)S(1)}, bf16[2,8,48,768]{3,2,1,0:T(8,128)(2,1)S(1)}, u32[]{:S(2)}, u32[]{:S(2)}) collective-permute-start(bf16[2,8,48,768]{3,2,1,0:T(8,128)(2,1)S(1)} %pad_maximum_fusion), channel_id=1, source_target_pairs={{0,8},{2,10},{4,12},{6,14},{8,0},{10,2},{12,4},{14,6},{16,24},{18,... | collective-permute-start | bytes 3538952 | tf_op jit(solution)/shard_map/ppermute | solution.py:746
  299.0 9.8 %collective-permute-start.7 = (bf16[4,56,768]{2,1,0:T(8,128)(2,1)S(1)}, bf16[4,56,768]{2,1,0:T(8,128)(2,1)S(1)}, u32[]{:S(2)}, u32[]{:S(2)}) collective-permute-start(bf16[4,56,768]{2,1,0:T(8,128)(2,1)S(1)} %slice.960), channel_id=1, source_target_pairs={{0,2},{2,0},{4,6},{6,4},{8,10},{10,8},{12,14},{14,12},{16,18},{18,... | collective-permute-start | bytes 1032200 | tf_op jit(solution)/shard_map/ppermute | solution.py:746
  315.5 13.7 %collective-permute-start.8 = (bf16[2,104,768]{2,1,0:T(8,128)(2,1)S(1)}, bf16[2,104,768]{2,1,0:T(8,128)(2,1)S(1)}, u32[]{:S(2)}, u32[]{:S(2)}) collective-permute-start(bf16[2,104,768]{2,1,0:T(8,128)(2,1)S(1)} %pad_maximum_fusion.2), channel_id=1, source_target_pairs={{0,8},{2,10},{4,12},{6,14},{8,0},{10,2},{12,4},{14,6},{16,24},{18,... | collective-permute-start | bytes 958472 | tf_op jit(solution)/shard_map/ppermute | solution.py:746
  317.6 86.4 %collective-permute-start.39 = (bf16[2,1,48,768]{3,2,1,0:T(8,128)(2,1)S(1)}, bf16[2,1,48,768]{3,2,1,0:T(8,128)(2,1)S(1)}, u32[]{:S(2)}, u32[]{:S(2)}) collective-permute-start(bf16[2,1,48,768]{3,2,1,0:T(8,128)(2,1)S(1)} %pad_maximum_fusion.13), channel_id=1, source_target_pairs={{0,16},{2,18},{4,20},{6,22},{8,24},{10,26},{12,28},{14,30},{16,0},... | collective-permute-start | bytes 442376 | tf_op jit(solution)/shard_map/ppermute | solution.py:746
  320.9 38.1 %collective-permute-start.41 = (bf16[8,48,768]{2,1,0:T(8,128)(2,1)S(1)}, bf16[8,48,768]{2,1,0:T(8,128)(2,1)S(1)}, u32[]{:S(2)}, u32[]{:S(2)}) collective-permute-start(bf16[8,48,768]{2,1,0:T(8,128)(2,1)S(1)} %get-tuple-element.155), channel_id=1, source_target_pairs={{0,2},{2,0},{4,6},{6,4},{8,10},{10,8},{12,14},{14,12},{16,18},{18,... | collective-permute-start | bytes 1769480 | tf_op jit(solution)/shard_map/ppermute | solution.py:746
  323.6 36.9 %collective-permute-start.43 = (bf16[8,48,768]{2,1,0:T(8,128)(2,1)S(1)}, bf16[8,48,768]{2,1,0:T(8,128)(2,1)S(1)}, u32[]{:S(2)}, u32[]{:S(2)}) collective-permute-start(bf16[8,48,768]{2,1,0:T(8,128)(2,1)S(1)} %get-tuple-element.156), channel_id=1, source_target_pairs={{0,4},{2,6},{4,0},{6,2},{8,12},{10,14},{12,8},{14,10},{16,20},{18,... | collective-permute-start | bytes 1769480 | tf_op jit(solution)/shard_map/ppermute | solution.py:746
  325.1 15.2 %collective-permute-start.22 = (bf16[4,48,768]{2,1,0:T(8,128)(2,1)S(1)}, bf16[4,48,768]{2,1,0:T(8,128)(2,1)S(1)}, u32[]{:S(2)}, u32[]{:S(2)}) collective-permute-start(bf16[4,48,768]{2,1,0:T(8,128)(2,1)S(1)} %slice_bitcast_fusion.11), channel_id=1, source_target_pairs={{0,4},{2,6},{4,0},{6,2},{8,12},{10,14},{12,8},{14,10},{16,20},{18,... | collective-permute-start | bytes 884744 | tf_op jit(solution)/shard_map/ppermute | solution.py:746
  329.2 13.5 %collective-permute-start.20 = (bf16[4,48,768]{2,1,0:T(8,128)(2,1)S(1)}, bf16[4,48,768]{2,1,0:T(8,128)(2,1)S(1)}, u32[]{:S(2)}, u32[]{:S(2)}) collective-permute-start(bf16[4,48,768]{2,1,0:T(8,128)(2,1)S(1)} %slice_bitcast_fusion.13), channel_id=1, source_target_pairs={{0,2},{2,0},{4,6},{6,4},{8,10},{10,8},{12,14},{14,12},{16,18},{18,... | collective-permute-start | bytes 884744 | tf_op jit(solution)/shard_map/ppermute | solution.py:746
  340.3 26.8 %collective-permute-start.11 = (bf16[8,48,768]{2,1,0:T(8,128)(2,1)S(1)}, bf16[8,48,768]{2,1,0:T(8,128)(2,1)S(1)}, u32[]{:S(2)}, u32[]{:S(2)}) collective-permute-start(bf16[8,48,768]{2,1,0:T(8,128)(2,1)S(1)} %fusion.20), channel_id=1, source_target_pairs={{0,2},{2,0},{4,6},{6,4},{8,10},{10,8},{12,14},{14,12},{16,18},{18,... | collective-permute-start | bytes 1769480 | tf_op jit(solution)/shard_map/ppermute | solution.py:746
  342.7 10.5 %collective-permute-start.23 = (bf16[2,48,768]{2,1,0:T(8,128)(2,1)S(1)}, bf16[2,48,768]{2,1,0:T(8,128)(2,1)S(1)}, u32[]{:S(2)}, u32[]{:S(2)}) collective-permute-start(bf16[2,48,768]{2,1,0:T(8,128)(2,1)S(1)} %slice.1021), channel_id=1, source_target_pairs={{0,2},{2,0},{4,6},{6,4},{8,10},{10,8},{12,14},{14,12},{16,18},{18,... | collective-permute-start | bytes 442376 | tf_op jit(solution)/shard_map/ppermute | solution.py:746
  358.3 14.1 %collective-permute-start.13 = (bf16[8,56,768]{2,1,0:T(8,128)(2,1)S(1)}, bf16[8,56,768]{2,1,0:T(8,128)(2,1)S(1)}, u32[]{:S(2)}, u32[]{:S(2)}) collective-permute-start(bf16[8,56,768]{2,1,0:T(8,128)(2,1)S(1)} %fusion.11), channel_id=1, source_target_pairs={{0,4},{2,6},{4,0},{6,2},{8,12},{10,14},{12,8},{14,10},{16,20},{18,... | collective-permute-start | bytes 2064392 | tf_op jit(solution)/shard_map/ppermute | solution.py:746
  358.9 41.3 %collective-permute-start.26 = (bf16[2,8,48,768]{3,2,1,0:T(8,128)(2,1)S(1)}, bf16[2,8,48,768]{3,2,1,0:T(8,128)(2,1)S(1)}, u32[]{:S(2)}, u32[]{:S(2)}) collective-permute-start(bf16[2,8,48,768]{3,2,1,0:T(8,128)(2,1)S(1)} %pad_maximum_fusion.1), channel_id=1, source_target_pairs={{0,8},{2,10},{4,12},{6,14},{8,0},{10,2},{12,4},{14,6},{16,24},{18,... | collective-permute-start | bytes 3538952 | tf_op jit(solution)/shard_map/ppermute | solution.py:746
  360.5 54.1 %collective-permute-start.9 = (bf16[1,104,768]{2,1,0:T(8,128)(2,1)S(1)}, bf16[1,104,768]{2,1,0:T(8,128)(2,1)S(1)}, u32[]{:S(2)}, u32[]{:S(2)}) collective-permute-start(bf16[1,104,768]{2,1,0:T(8,128)(2,1)S(1)} %pad_maximum_fusion.9), channel_id=1, source_target_pairs={{0,16},{2,18},{4,20},{6,22},{8,24},{10,26},{12,28},{14,30},{16,0},... | collective-permute-start | bytes 479240 | tf_op jit(solution)/shard_map/ppermute | solution.py:746
  373.9 50.9 %collective-permute-start.24 = (bf16[2,1,48,768]{3,2,1,0:T(8,128)(2,1)S(1)}, bf16[2,1,48,768]{3,2,1,0:T(8,128)(2,1)S(1)}, u32[]{:S(2)}, u32[]{:S(2)}) collective-permute-start(bf16[2,1,48,768]{3,2,1,0:T(8,128)(2,1)S(1)} %pad_maximum_fusion.11), channel_id=1, source_target_pairs={{0,16},{2,18},{4,20},{6,22},{8,24},{10,26},{12,28},{14,30},{16,0},... | collective-permute-start | bytes 442376 | tf_op jit(solution)/shard_map/ppermute | solution.py:746
  408.4 16.4 %collective-permute-start.47 = (f32[2,48,768]{2,1,0:T(8,128)S(1)}, f32[2,48,768]{2,1,0:T(8,128)S(1)}, u32[]{:S(2)}, u32[]{:S(2)}) collective-permute-start(f32[2,48,768]{2,1,0:T(8,128)S(1)} %pad_maximum_fusion.8), channel_id=1, source_target_pairs={{0,1},{1,0},{2,3},{3,2},{4,5},{5,4},{6,7},{7,6},{8,9},{9,8},{10,11... | collective-permute-start | bytes 884744 | tf_op jit(solution)/shard_map/ppermute | solution.py:877
  410.8 9.6 %collective-permute-start.16 = (bf16[1,104,768]{2,1,0:T(8,128)(2,1)S(1)}, bf16[1,104,768]{2,1,0:T(8,128)(2,1)S(1)}, u32[]{:S(2)}, u32[]{:S(2)}) collective-permute-start(bf16[1,104,768]{2,1,0:T(8,128)(2,1)S(1)} %pad_maximum_fusion.10), channel_id=1, source_target_pairs={{0,16},{2,18},{4,20},{6,22},{8,24},{10,26},{12,28},{14,30},{16,0},... | collective-permute-start | bytes 479240 | tf_op jit(solution)/shard_map/ppermute | solution.py:746
  413.5 9.7 %collective-permute-start.30 = (bf16[2,48,768]{2,1,0:T(8,128)(2,1)S(1)}, bf16[2,48,768]{2,1,0:T(8,128)(2,1)S(1)}, u32[]{:S(2)}, u32[]{:S(2)}) collective-permute-start(bf16[2,48,768]{2,1,0:T(8,128)(2,1)S(1)} %slice.1039), channel_id=1, source_target_pairs={{0,2},{2,0},{4,6},{6,4},{8,10},{10,8},{12,14},{14,12},{16,18},{18,... | collective-permute-start | bytes 442376 | tf_op jit(solution)/shard_map/ppermute | solution.py:746
  422.4 12.3 %collective-permute-start.17 = (f32[2,48,768]{2,1,0:T(8,128)S(1)}, f32[2,48,768]{2,1,0:T(8,128)S(1)}, u32[]{:S(2)}, u32[]{:S(2)}) collective-permute-start(f32[2,48,768]{2,1,0:T(8,128)S(1)} %pad_maximum_fusion.4), channel_id=1, source_target_pairs={{0,1},{1,0},{2,3},{3,2},{4,5},{5,4},{6,7},{7,6},{8,9},{9,8},{10,11... | collective-permute-start | bytes 884744 | tf_op jit(solution)/shard_map/ppermute | solution.py:877
  423.3 10.4 %collective-permute-start.31 = (bf16[2,1,48,768]{3,2,1,0:T(8,128)(2,1)S(1)}, bf16[2,1,48,768]{3,2,1,0:T(8,128)(2,1)S(1)}, u32[]{:S(2)}, u32[]{:S(2)}) collective-permute-start(bf16[2,1,48,768]{3,2,1,0:T(8,128)(2,1)S(1)} %pad_maximum_fusion.12), channel_id=1, source_target_pairs={{0,16},{2,18},{4,20},{6,22},{8,24},{10,26},{12,28},{14,30},{16,0},... | collective-permute-start | bytes 442376 | tf_op jit(solution)/shard_map/ppermute | solution.py:746
  (36 other events, 266.7 us)

commit v2 on v0

v2 whole, which is shorter than its diff:
```python
import functools
import jax
import jax.numpy as jnp
from jax import lax
from jax.experimental import pallas as pl
from jax.experimental.pallas import tpu as pltpu
from jax.sharding import PartitionSpec as P

HEADS = 12
HEAD_DIM = 64
BUCKET = 64
PAIR = 2 * HEAD_DIM
masked_score = -1000000000.0
norm_epsilon = 1e-06
F32 = jnp.float32
BF16 = jnp.bfloat16
CHUNK = 16
FFN_TILE = 512
ATT_UNROLL = 3


def rows_times(left, right):
    return lax.dot_general(left, right, (((1,), (0,)), ((), ())), preferred_element_type=F32)


def rows_times_transposed(left, right):
    return lax.dot_general(left, right, (((1,), (1,)), ((), ())), preferred_element_type=F32)


def transposed_times(left, right):
    return lax.dot_general(left, right, (((0,), (0,)), ((), ())), preferred_element_type=F32)


def slot_facts(block, span_rows, place, meta, micro):
    bucket_ref, count_ref, lengths_ref = meta
    bucket = bucket_ref[micro]
    count = count_ref[micro]

    def length_of(slot):
        return jnp.where(slot < count, lengths_ref[micro, slot], 0)

    if span_rows == 2 * BUCKET:
        return (jnp.full_like(place, block), place, jnp.full_like(place, length_of(block)))
    short = bucket == 0
    first = 3 * block
    slot_short = first + place // BUCKET
    length_short = jnp.where(
        place < BUCKET,
        length_of(first),
        jnp.where(place < 2 * BUCKET, length_of(first + 1), length_of(first + 2)),
    )
    slot = jnp.where(short, slot_short, block)
    inner = jnp.where(short, place % BUCKET, place)
    length = jnp.where(short, length_short, length_of(block))
    return (slot, inner, length)


def fill_masks(span_rows, row_count, meta, micro, bias_ref, valid_ref):
    for block in range(row_count // span_rows):
        row_place = lax.broadcasted_iota(jnp.int32, (span_rows, 1), 0)
        row_slot, row_inner, row_length = slot_facts(block, span_rows, row_place, meta, micro)
        rows = slice(block * span_rows, (block + 1) * span_rows)
        if bias_ref is not None:
            key_place = lax.broadcasted_iota(jnp.int32, (1, span_rows), 1)
            key_slot, key_inner, key_length = slot_facts(block, span_rows, key_place, meta, micro)
            key_tag = jnp.where(key_inner < key_length, key_slot, -1)
            allowed = (row_slot == key_tag) | (row_place == key_place)
            bias_ref[rows, 0:span_rows] = jnp.where(allowed, 0.0, masked_score)
        if valid_ref is not None:
            valid_ref[rows, :] = jnp.where(row_inner < row_length, 1.0, 0.0)


def by_span(meta, micro, body):
    even = meta[0][micro] == 1

    @pl.when(even)
    def _():
        body(2 * BUCKET)

    @pl.when(jnp.logical_not(even))
    def _():
        body(3 * BUCKET)


def attend_forward(span_rows, row_count, q_ref, k_ref, v_ref, bias_ref, c_ref):
    blocks = row_count // span_rows

    def one_pair(pair, carry):
        columns = pl.ds(pl.multiple_of(pair * PAIR, PAIR), PAIR)
        lane = lax.broadcasted_iota(jnp.int32, (span_rows, PAIR), 1)
        first_half = lane < HEAD_DIM
        weights = []
        for block in range(blocks):
            rows = slice(block * span_rows, (block + 1) * span_rows)
            query = q_ref[rows, columns] * jnp.asarray(HEAD_DIM ** (-0.5), BF16)
            keys = k_ref[rows, columns]
            zero = jnp.zeros_like(keys)
            bias = bias_ref[rows, 0:span_rows]
            for mine in (first_half, jnp.logical_not(first_half)):
                scores = rows_times_transposed(query, jnp.where(mine, keys, zero)) + bias
                top = jnp.max(scores, axis=-1, keepdims=True)
                weights.append(jnp.exp(scores - top).astype(BF16))
        for block in range(blocks):
            rows = slice(block * span_rows, (block + 1) * span_rows)
            value = v_ref[rows, columns]
            one = jnp.ones_like(value)
            left = rows_times(weights[2 * block], jnp.where(first_half, value, one))
            right = rows_times(weights[2 * block + 1], jnp.where(first_half, one, value))
            above = jnp.where(first_half, left, right)
            below = pltpu.roll(jnp.where(first_half, right, left), HEAD_DIM, 1)
            c_ref[rows, columns] = (above / below).astype(BF16)
        return carry

    lax.fori_loop(0, HEADS // 2, one_pair, 0, unroll=ATT_UNROLL)


def row_moments(values):
    center = jnp.mean(values, axis=-1, keepdims=True)
    centred = values - center
    spread = jnp.mean(centred * centred, axis=-1, keepdims=True)
    return centred, lax.rsqrt(spread + norm_epsilon)


def over_chunks(row_count, body, rows=CHUNK, group=6):
    def step(index, carry):
        for inner in range(group):
            start = pl.multiple_of(index * (rows * group) + inner * rows, rows)
            body(pl.ds(start, rows))
        return carry

    lax.fori_loop(0, row_count // (rows * group), step, 0)


def gelu_with_slope(values):
    cumulative = 0.5 + 0.5 * lax.erf(values * (0.5 ** 0.5))
    density = jnp.exp(values * values * -0.5) * 0.3989422804014327
    return values * cumulative, cumulative + values * density


ANY = pl.BlockSpec(memory_space=pl.ANY)
VM = pl.BlockSpec(memory_space=pltpu.VMEM)
SM = pl.BlockSpec(memory_space=pltpu.SMEM)
VMEM_LIMIT = 63_000 * 1024
S = jax.ShapeDtypeStruct
V = pltpu.VMEM
B_QUERY, B_VALUE, B_MIXER, GAIN_ONE, SHIFT_ONE, B_OUTER, GAIN_TWO, SHIFT_TWO = range(8)
QUERY, KEYS, VALUE, CONTEXT, MIDDLE, RESULT = range(6)
EXCHANGES = ((1, 2, 4, 8), (2, 1, 4, 8), (4, 1, 2, 8), (4, 2, 1, 8))


class Loads:
    def __init__(self, semaphores):
        self.semaphores = semaphores
        self.copies = {}

    def start(self, name, source, target, other=None, take_other=None):
        semaphore = self.semaphores.at[len(self.copies)]
        copy = pltpu.make_async_copy(source, target, semaphore)
        self.copies[name] = copy
        if other is None:
            copy.start()
            return
        second = pltpu.make_async_copy(other, target, semaphore)

        @pl.when(take_other)
        def _():
            second.start()

        @pl.when(jnp.logical_not(take_other))
        def _():
            copy.start()

    def wait(self, *names):
        for name in names:
            self.copies[name].wait()


class Stores:
    def __init__(self, semaphores):
        self.semaphores = semaphores
        self.copies = []

    def start(self, source, target):
        copy = pltpu.make_async_copy(source, target, self.semaphores.at[len(self.copies)])
        copy.start()
        self.copies.append(copy)

    def wait(self):
        for copy in self.copies:
            copy.wait()


def spot_of(order, dest, me):
    relative = jnp.bitwise_xor(dest, me)
    spot = 0
    for index, bit in enumerate(EXCHANGES[order]):
        one = jnp.bitwise_and(lax.shift_right_logical(relative, bit.bit_length() - 1), 1)
        spot = spot + one * (8 >> index)
    return spot


def put_blocks(target, product, unit_at, tile, orders, me, spread_units):
    count = target.shape[1]
    height = product.shape[0] // count
    for block in range(count):
        if spread_units and count > 1:
            unit = block % 4
            dest = tile * (count // 4) + block // 4
        else:
            unit = tile
            dest = block
        spot = 0 if count == 1 else spot_of(orders[unit % 2], dest, me)
        target[unit_at + unit, spot] = product[block * height : (block + 1) * height, :].astype(BF16)


def forward_body(load, store, meta, micro, vec, bi, outs, refs):
    h_s, wq_s, wk_s, wv_s, wm_s, wi_s, wo_s, low_s, total_s, wide_s, m_s, f0_s, e0_s, e1_s, bias_s, valid_s = refs
    y_o, low_o, total_o, wide_o = outs
    rows, width = h_s.shape
    hidden = wi_s.shape[1]
    q_s, k_s, v_s, c_s, ml_s, y_s = (low_s.at[index] for index in (QUERY, KEYS, VALUE, CONTEXT, MIDDLE, RESULT))
    a1_s, a2_s = (total_s.at[0], total_s.at[1])
    u_s, gp_s = (wide_s.at[0], wide_s.at[1])
    load(0)
    by_span(meta, micro, lambda span: fill_masks(span, rows, meta, micro, bias_s, valid_s))
    load(1)
    q_s[...] = (rows_times(h_s[...], wq_s[...]) + vec(B_QUERY)).astype(BF16)
    load(2)
    k_s[...] = rows_times(h_s[...], wk_s[...]).astype(BF16)
    load(3)
    v_s[...] = (rows_times(h_s[...], wv_s[...]) + vec(B_VALUE)).astype(BF16)
    by_span(meta, micro, lambda span: attend_forward(span, rows, q_s, k_s, v_s, bias_s, c_s))
    store.start(low_s.at[0:4], low_o.at[0:4])
    load(4)
    f0_s[...] = rows_times(c_s[...], wm_s[...])
    offset_mixer, gain_one, shift_one = (vec(B_MIXER), vec(GAIN_ONE), vec(SHIFT_ONE))

    def first_norm(part):
        total = h_s[part, :].astype(F32) + (f0_s[part, :] + offset_mixer)
        a1_s[part, :] = total
        centred, scale = row_moments(total)
        middle = centred * scale * gain_one + shift_one
        m_s[part, :] = middle
        ml_s[part, :] = middle.astype(BF16)

    over_chunks(rows, first_norm)
    store.start(a1_s, total_o.at[0])
    store.start(ml_s, low_o.at[MIDDLE])
    load(5)
    tile = FFN_TILE
    tiles = hidden // tile

    def project(buffer, which):
        columns = pl.ds(pl.multiple_of(which * tile, tile), tile)
        buffer[...] = rows_times(ml_s[...], wi_s[:, columns])

    def activate(buffer, which):
        columns = pl.ds(pl.multiple_of(which * tile, tile), tile)
        offset = bi(columns)
        for start in range(0, rows, 32):
            part = slice(start, start + 32)
            value, slope = gelu_with_slope(buffer[part, :] + offset)
            u_s[part, columns] = value.astype(BF16)
            gp_s[part, columns] = slope.astype(BF16)

    project(e0_s, 0)

    def two_tiles(index, carry):
        project(e1_s, 2 * index + 1)
        activate(e0_s, 2 * index)
        project(e0_s, jnp.minimum(2 * index + 2, tiles - 1))
        activate(e1_s, 2 * index + 1)
        return carry

    lax.fori_loop(0, tiles // 2, two_tiles, 0)
    store.start(wide_s, wide_o)
    load(6)
    f0_s[...] = rows_times(u_s[...], wo_s[...])
    offset_outer, gain_two, shift_two = (vec(B_OUTER), vec(GAIN_TWO), vec(SHIFT_TWO))

    def second_norm(part):
        total = m_s[part, :] + (f0_s[part, :] + offset_outer)
        a2_s[part, :] = total
        centred, scale = row_moments(total)
        y_s[part, :] = ((centred * scale * gain_two + shift_two) * valid_s[part, :]).astype(BF16)

    over_chunks(rows, second_norm)
    store.start(y_s, y_o)
    store.start(a2_s, total_o.at[1])
    store.wait()


def forward_loads(loads, hidden_start, weights, others, take_other, targets):
    names = ("wq", "wk", "wv", "wm", "wi", "wo")

    def begin(index):
        other = None if others is None else others[index].at[0]
        loads.start(names[index], weights[index].at[0], targets[index], other, take_other)

    def load(step):
        if step == 0:
            hidden_start()
            for index in range(3):
                begin(index)
            return
        if step == 1:
            loads.wait("h")
        loads.wait(names[step - 1])
        if step <= 3:
            begin(step + 2)

    return load


def first_forward_kernel(
    index, bucket, count, lengths, tok, wq, wk, wv, wm, wi, wo, bq, bv, bm, g1, s1, bo, g2, s2, bi,
    y_o, low_o, total_o, wide_o, vec_o,
    h_s, wq_s, wk_s, wv_s, wm_s, wi_s, wo_s, low_s, total_s, wide_s, m_s, f0_s, e0_s, e1_s, bias_s, valid_s, in_sem, out_sem,
):
    vectors = (bq, bv, bm, g1, s1, bo, g2, s2)
    for place, vector in enumerate(vectors):
        vec_o[place : place + 1, :] = vector[...]

    @pl.when(lax.axis_index("section") == 0)
    def _():
        loads = Loads(in_sem)
        load = forward_loads(
            loads, lambda: loads.start("h", tok.at[index], h_s), (wq, wk, wv, wm, wi, wo), None, None,
            (wq_s, wk_s, wv_s, wm_s, wi_s, wo_s),
        )
        forward_body(
            load, Stores(out_sem), (bucket, count, lengths), index, lambda place: vectors[place][...], lambda columns: bi[:, columns],
            (y_o, low_o, total_o, wide_o),
            (h_s, wq_s, wk_s, wv_s, wm_s, wi_s, wo_s, low_s, total_s, wide_s, m_s, f0_s, e0_s, e1_s, bias_s, valid_s),
        )


def second_forward_kernel(
    bucket, count, lengths, y_own, y_other, wq, wk, wv, wm, wi, wo, xq, xk, xv, xm, xi, xo, vec_own, vec_other, bi_own, bi_other,
    y_o, low_o, total_o, wide_o,
    h_s, wq_s, wk_s, wv_s, wm_s, wi_s, wo_s, low_s, total_s, wide_s, m_s, f0_s, e0_s, e1_s, bias_s, valid_s, in_sem, out_sem,
):
    section = lax.axis_index("section")
    first = section == 0
    loads = Loads(in_sem)
    load = forward_loads(
        loads, lambda: loads.start("h", y_other, h_s, y_own, first), (wq, wk, wv, wm, wi, wo), (xq, xk, xv, xm, xi, xo), first,
        (wq_s, wk_s, wv_s, wm_s, wi_s, wo_s),
    )

    def vec(place):
        return jnp.where(first, vec_other[place : place + 1, :], vec_own[place : place + 1, :])

    forward_body(
        load, Stores(out_sem), (bucket, count, lengths), section, vec,
        lambda columns: jnp.where(first, bi_other[:, columns], bi_own[:, columns]),
        (y_o, low_o, total_o, wide_o),
        (h_s, wq_s, wk_s, wv_s, wm_s, wi_s, wo_s, low_s, total_s, wide_s, m_s, f0_s, e0_s, e1_s, bias_s, valid_s),
    )


def run_kernel(kernel, outs, out_specs, in_specs, scratch, loads, stores, flops, bytes_moved, name):
    return pl.pallas_call(
        kernel,
        out_shape=outs,
        in_specs=in_specs,
        out_specs=out_specs,
        scratch_shapes=list(scratch) + [pltpu.SemaphoreType.DMA((loads,)), pltpu.SemaphoreType.DMA((stores,))],
        compiler_params=pltpu.CompilerParams(vmem_limit_bytes=VMEM_LIMIT),
        cost_estimate=pl.CostEstimate(flops=flops, bytes_accessed=bytes_moved, transcendentals=0),
        name=name,
    )


def forward_shapes(rows, width, hidden):
    flat = (rows, width)
    square = (width, width)
    outs = (S(flat, BF16), S((5,) + flat, BF16), S((2,) + flat, F32), S((2, rows, hidden), BF16))
    scratch = [
        V(flat, BF16), V(square, BF16), V(square, BF16), V(square, BF16), V(square, BF16), V((width, hidden), BF16),
        V((hidden, width), BF16), V((6,) + flat, BF16), V((2,) + flat, F32), V((2, rows, hidden), BF16), V(flat, F32),
        V(flat, F32), V((rows, FFN_TILE), F32), V((rows, FFN_TILE), F32), V((rows, 3 * BUCKET), F32), V((rows, 1), F32),
    ]
    flops = 2 * rows * width * (4 * width + 2 * hidden)
    return outs, scratch, flops


def first_forward(meta, tokens, index, weights, vectors, bi):
    rows, width = tokens.shape[1:]
    outs, scratch, flops = forward_shapes(rows, width, bi.shape[1])
    return run_kernel(
        functools.partial(first_forward_kernel, index), outs + (S((8, width), F32),), [ANY] * 4 + [VM],
        [SM] * 3 + [ANY] * 7 + [VM] * 9, scratch, 7, 6, flops, 25_000_000, "first_forward",
    )(*meta, tokens, *weights, *vectors, bi)


def second_forward(meta, y_own, y_other, weights, others, vec_own, vec_other, bi_own, bi_other):
    rows, width = y_own.shape
    outs, scratch, flops = forward_shapes(rows, width, bi_own.shape[1])
    return run_kernel(
        second_forward_kernel, outs, [ANY] * 4, [SM] * 3 + [ANY] * 14 + [VM] * 4, scratch, 7, 6, flops, 25_000_000,
        "second_forward",
    )(*meta, y_own, y_other, *weights, *others, vec_own, vec_other, bi_own, bi_other)


def norm_backward(grad, total, gain):
    centred, scale = row_moments(total)
    unit = centred * scale
    spread = grad * gain
    first = jnp.mean(spread, axis=-1, keepdims=True)
    second = jnp.mean(spread * unit, axis=-1, keepdims=True)
    return (spread - first - unit * second) * scale, grad * unit


def fold_rows(values):
    return jnp.sum(values.reshape(values.shape[0] // 8, 8, values.shape[1]), axis=0)


def layer_of(layer):
    return lax.axis_index("section") != layer


def taken(layer, own, other, place):
    return jnp.where(layer_of(layer), other[place : place + 1, :], own[place : place + 1, :])


def send_units(store, w_s, away_o, home_o):
    section = lax.axis_index("section")
    store.start(w_s.at[pl.ds(2 * (1 - section), 2)], away_o)
    store.start(w_s.at[pl.ds(2 * section, 2)], home_o)


def outer_kernel(
    layer, orders, bucket, count, lengths, g, total, total_x, wide, wide_x, vec_own, vec_other,
    da2_o, dz_o, away_o, home_o, small_o,
    g_s, a2_s, u_s, da2_s, dz_s, w_s, valid_s, sums_s, in_sem, out_sem,
):
    section = lax.axis_index("section")
    rows, width = a2_s.shape
    hidden = u_s.shape[1]
    second = section == 1
    loads = Loads(in_sem)
    store = Stores(out_sem)
    other = (lambda ref: ref) if layer == 0 else (lambda ref: None)
    loads.start("g", g.at[section] if layer == 1 else g, g_s)
    loads.start("a2", total.at[1], a2_s, other(total_x.at[1]), second)
    loads.start("u", wide.at[0], u_s, other(wide_x.at[0]), second)
    meta = (bucket, count, lengths)
    by_span(meta, section, lambda span: fill_masks(span, rows, meta, section, None, valid_s))
    sums_s[...] = jnp.zeros_like(sums_s)
    gain = taken(layer, vec_own, vec_other, GAIN_TWO)
    loads.wait("g", "a2")

    def second_norm(part):
        grad = g_s[part, :].astype(F32) * valid_s[part, :]
        moved, gained = norm_backward(grad, a2_s[part, :], gain)
        da2_s[part, :] = moved
        low = moved.astype(BF16)
        dz_s[part, :] = low
        sums_s[0] += fold_rows(gained)
        sums_s[1] += fold_rows(grad)
        sums_s[2] += fold_rows(low.astype(F32))

    over_chunks(rows, second_norm)
    store.start(da2_s, da2_o)
    store.start(dz_s, dz_o)
    for index in range(3):
        small_o[index : index + 1, :] = jnp.sum(sums_s[index], axis=0, keepdims=True)
    loads.wait("u")
    me = lax.axis_index("dp")
    for tile in range(hidden // width):
        columns = slice(tile * width, (tile + 1) * width)
        put_blocks(w_s, transposed_times(u_s[:, columns], dz_s[...]), 0, tile, orders, me, True)
    send_units(store, w_s, away_o, home_o)
    store.wait()


def inner_kernel(
    layer, orders, dz, wide, wide_x, low, low_x, wo, wo_x,
    df_o, away_o, home_o, small_o,
    dz_s, gp_s, ml_s, wo_s, df_s, w_s, e0_s, e1_s, sums_s, in_sem, out_sem,
):
    section = lax.axis_index("section")
    rows, width = dz_s.shape
    hidden = df_s.shape[1]
    second = section == 1
    loads = Loads(in_sem)
    store = Stores(out_sem)
    other = (lambda ref: ref) if layer == 0 else (lambda ref: None)
    loads.start("dz", dz, dz_s)
    loads.start("wo", wo.at[0], wo_s, wo_x.at[0], layer_of(layer))
    loads.start("gp", wide.at[1], gp_s, other(wide_x.at[1]), second)
    loads.start("ml", low.at[MIDDLE], ml_s, other(low_x.at[MIDDLE]), second)
    tile = FFN_TILE
    tiles = hidden // tile
    sums_s[...] = jnp.zeros_like(sums_s)

    def project(buffer, which):
        columns = pl.ds(pl.multiple_of(which * tile, tile), tile)
        buffer[...] = rows_times_transposed(dz_s[...], wo_s[columns, :])

    def slope(buffer, which):
        columns = pl.ds(pl.multiple_of(which * tile, tile), tile)
        total = None
        for start in range(0, rows, 32):
            part = slice(start, start + 32)
            low_part = (buffer[part, :] * gp_s[part, columns].astype(F32)).astype(BF16)
            df_s[part, columns] = low_part
            term = fold_rows(low_part.astype(F32))
            total = term if total is None else total + term
        sums_s[:, columns] = total

    loads.wait("dz", "wo")
    project(e0_s, 0)
    loads.wait("gp")

    def two_tiles(index, carry):
        project(e1_s, 2 * index + 1)
        slope(e0_s, 2 * index)
        project(e0_s, jnp.minimum(2 * index + 2, tiles - 1))
        slope(e1_s, 2 * index + 1)
        return carry

    lax.fori_loop(0, tiles // 2, two_tiles, 0)
    store.start(df_s, df_o)
    small_o[...] = jnp.sum(sums_s[...], axis=0, keepdims=True)
    loads.wait("ml")
    me = lax.axis_index("dp")
    for which in range(hidden // width):
        columns = slice(which * width, (which + 1) * width)
        put_blocks(w_s, transposed_times(ml_s[...], df_s[:, columns]), 0, which, orders, me, False)
    send_units(store, w_s, away_o, home_o)
    store.wait()


def mixer_kernel(
    layer, orders, df, wi, wi_x, da2, total, total_x, low, low_x, wm, wm_x, vec_own, vec_other,
    da1_o, dc_o, mix_o, small_o,
    df_s, wi_s, da2_s, a1_s, c_s, wm_s, dm_s, da1_s, da_s, dc_s, w_s, sums_s, in_sem, out_sem,
):
    section = lax.axis_index("section")
    rows, width = dm_s.shape
    second = section == 1
    loads = Loads(in_sem)
    store = Stores(out_sem)
    other = (lambda ref: ref) if layer == 0 else (lambda ref: None)
    loads.start("df", df, df_s)
    loads.start("wi", wi.at[0], wi_s, wi_x.at[0], layer_of(layer))
    loads.start("da2", da2, da2_s)
    loads.start("a1", total.at[0], a1_s, other(total_x.at[0]), second)
    loads.start("c", low.at[CONTEXT], c_s, other(low_x.at[CONTEXT]), second)
    loads.start("wm", wm.at[0], wm_s, wm_x.at[0], layer_of(layer))
    sums_s[...] = jnp.zeros_like(sums_s)
    gain = taken(layer, vec_own, vec_other, GAIN_ONE)
    loads.wait("df", "wi")
    dm_s[...] = rows_times_transposed(df_s[...], wi_s[...])
    loads.wait("da2", "a1")

    def first_norm(part):
        grad = dm_s[part, :] + da2_s[part, :]
        moved, gained = norm_backward(grad, a1_s[part, :], gain)
        da1_s[part, :] = moved
        low_part = moved.astype(BF16)
        da_s[part, :] = low_part
        sums_s[0] += fold_rows(gained)
        sums_s[1] += fold_rows(grad)
        sums_s[2] += fold_rows(low_part.astype(F32))

    over_chunks(rows, first_norm)
    store.start(da1_s, da1_o)
    for index in range(3):
        small_o[index : index + 1, :] = jnp.sum(sums_s[index], axis=0, keepdims=True)
    loads.wait("c", "wm")
    dc_s[...] = rows_times_transposed(da_s[...], wm_s[...]).astype(BF16)
    store.start(dc_s, dc_o)
    put_blocks(w_s, transposed_times(c_s[...], da_s[...]), 0, 0, orders[1:], lax.axis_index("dp"), False)
    store.start(w_s.at[0], mix_o)
    store.wait()


def attend_backward(span_rows, row_count, q_ref, k_ref, v_ref, dc_ref, bias_ref, dq_ref, dk_ref, dv_ref):
    blocks = row_count // span_rows
    scale = HEAD_DIM ** (-0.5)

    def one_pair(pair, carry):
        columns = pl.ds(pl.multiple_of(pair * PAIR, PAIR), PAIR)
        lane = lax.broadcasted_iota(jnp.int32, (span_rows, PAIR), 1)
        halves = (lane < HEAD_DIM, lane >= HEAD_DIM)
        for block in range(blocks):
            rows = slice(block * span_rows, (block + 1) * span_rows)
            query = q_ref[rows, columns] * jnp.asarray(scale, BF16)
            keys = k_ref[rows, columns]
            value = v_ref[rows, columns]
            grad = dc_ref[rows, columns]
            zero = jnp.zeros_like(keys)
            bias = bias_ref[rows, 0:span_rows]
            dq = dk = dv = None
            for mine in halves:
                keys_own = jnp.where(mine, keys, zero)
                scores = rows_times_transposed(query, keys_own) + bias
                grad_part = rows_times_transposed(grad, jnp.where(mine, value, zero))
                top = jnp.max(scores, axis=-1, keepdims=True)
                weight = jnp.exp(scores - top)
                part = weight * (1.0 / jnp.sum(weight, axis=-1, keepdims=True))
                mean = jnp.sum(grad_part * part, axis=-1, keepdims=True)
                grad_scores = (part * (grad_part - mean)).astype(BF16)
                terms = (
                    rows_times(grad_scores, keys_own),
                    transposed_times(grad_scores, jnp.where(mine, query, zero)),
                    transposed_times(part.astype(BF16), jnp.where(mine, grad, zero)),
                )
                if dq is None:
                    dq, dk, dv = terms
                else:
                    dq, dk, dv = (dq + terms[0], dk + terms[1], dv + terms[2])
            dq_ref[rows, columns] = (dq * scale).astype(BF16)
            dk_ref[rows, columns] = dk.astype(BF16)
            dv_ref[rows, columns] = dv.astype(BF16)
        return carry

    lax.fori_loop(0, HEADS // 2, one_pair, 0)


def attend_kernel(
    layer, orders, bucket, count, lengths, low, low_x, dc, h_one, h_two, da1, wq, wk, wv, xq, xk, xv, mix,
    dh_o, dlow_o, away_o, home_o, small_o,
    q_s, k_s, v_s, dc_s, h_s, dh_s, dlow_s, wq_s, wk_s, wv_s, dq_s, dk_s, dv_s, w_s, bias_s, sums_s, in_sem, out_sem,
):
    section = lax.axis_index("section")
    rows, width = q_s.shape
    second = section == 1
    loads = Loads(in_sem)
    store = Stores(out_sem)
    other = (lambda ref: ref) if layer == 0 else (lambda ref: None)
    for name, index, target in (("q", QUERY, q_s), ("k", KEYS, k_s), ("v", VALUE, v_s)):
        loads.start(name, low.at[index], target, other(low_x.at[index]), second)
    loads.start("dc", dc, dc_s)
    meta = (bucket, count, lengths)
    by_span(meta, section, lambda span: fill_masks(span, rows, meta, section, bias_s, None))
    loads.wait("q", "k", "v", "dc")
    if layer == 0:
        loads.start("h", h_one.at[section], h_s)
    else:
        loads.start("h", h_one, h_s, h_two, second)
    loads.start("mix", mix, w_s.at[3])
    loads.start("da1", da1, dh_s)
    for name, own, received, target in (("wq", wq, xq, wq_s), ("wk", wk, xk, wk_s), ("wv", wv, xv, wv_s)):
        loads.start(name, own.at[0], target, received.at[0], layer_of(layer))
    by_span(meta, section, lambda span: attend_backward(span, rows, q_s, k_s, v_s, dc_s, bias_s, dq_s, dk_s, dv_s))
    loads.wait("h", "mix")
    me = lax.axis_index("dp")
    for unit, grad in enumerate((dq_s, dk_s, dv_s)):
        put_blocks(w_s, transposed_times(h_s[...], grad[...]), 0, unit, orders, me, False)
    send_units(store, w_s, away_o, home_o)
    loads.wait("da1", "wq", "wk", "wv")
    dh_s[...] += rows_times_transposed(dq_s[...], wq_s[...])
    dh_s[...] += rows_times_transposed(dk_s[...], wk_s[...])
    dh_s[...] += rows_times_transposed(dv_s[...], wv_s[...])
    store.start(dh_s, dh_o)
    sums_s[...] = jnp.zeros_like(sums_s)

    def finish(part):
        dlow_s[part, :] = dh_s[part, :].astype(BF16)
        sums_s[0] += fold_rows(dq_s[part, :].astype(F32))
        sums_s[1] += fold_rows(dv_s[part, :].astype(F32))

    over_chunks(rows, finish)
    store.start(dlow_s, dlow_o)
    for index in range(2):
        small_o[index : index + 1, :] = jnp.sum(sums_s[index], axis=0, keepdims=True)
    store.wait()


def unit_shapes(count, width):
    block = (count, width // count, width)
    return block, S((2,) + block, BF16)


def outer_gradient(layer, orders, count, meta, g, total, total_x, wide, wide_x, vec_own, vec_other):
    rows, width = total.shape[1:]
    hidden = wide.shape[2]
    flat = (rows, width)
    block, units = unit_shapes(count, width)
    return run_kernel(
        functools.partial(outer_kernel, layer, orders), (S(flat, F32), S(flat, BF16), units, units, S((3, width), F32)),
        [ANY] * 4 + [VM], [SM] * 3 + [ANY] * 5 + [VM] * 2,
        [V(flat, g.dtype), V(flat, F32), V((rows, hidden), BF16), V(flat, F32), V(flat, BF16), V((4,) + block, BF16), V((rows, 1), F32), V((3, 8, width), F32)],
        3, 4, 2 * rows * width * hidden, 12_000_000, "outer_gradient",
    )(*meta, g, total, total_x, wide, wide_x, vec_own, vec_other)


def inner_gradient(layer, orders, count, dz, wide, wide_x, low, low_x, wo, wo_x):
    rows, width = dz.shape
    hidden = wide.shape[2]
    flat = (rows, width)
    block, units = unit_shapes(count, width)
    return run_kernel(
        functools.partial(inner_kernel, layer, orders), (S((rows, hidden), BF16), units, units, S((1, hidden), F32)),
        [ANY] * 3 + [VM], [ANY] * 7,
        [V(flat, BF16), V((rows, hidden), BF16), V(flat, BF16), V((hidden, width), BF16), V((rows, hidden), BF16), V((4,) + block, BF16), V((rows, FFN_TILE), F32), V((rows, FFN_TILE), F32), V((8, hidden), F32)],
        4, 3, 4 * rows * width * hidden, 18_000_000, "inner_gradient",
    )(dz, wide, wide_x, low, low_x, wo, wo_x)


def mixer_gradient(layer, orders, count, df, wi, wi_x, da2, total, total_x, low, low_x, wm, wm_x, vec_own, vec_other):
    rows, width = da2.shape
    hidden = df.shape[1]
    flat = (rows, width)
    block, _ = unit_shapes(count, width)
    return run_kernel(
        functools.partial(mixer_kernel, layer, orders), (S(flat, F32), S(flat, BF16), S(block, BF16), S((3, width), F32)),
        [ANY] * 3 + [VM], [ANY] * 10 + [VM] * 2,
        [V((rows, hidden), BF16), V((width, hidden), BF16), V(flat, F32), V(flat, F32), V(flat, BF16), V((width, width), BF16), V(flat, F32), V(flat, F32), V(flat, BF16), V(flat, BF16), V((1,) + block, BF16), V((3, 8, width), F32)],
        6, 3, 2 * rows * width * (hidden + 2 * width), 15_000_000, "mixer_gradient",
    )(df, wi, wi_x, da2, total, total_x, low, low_x, wm, wm_x, vec_own, vec_other)


def attend_gradient(layer, orders, count, meta, low, low_x, dc, h_one, h_two, da1, weights, others, mix):
    rows, width = da1.shape
    flat = (rows, width)
    square = (width, width)
    block, units = unit_shapes(count, width)
    return run_kernel(
        functools.partial(attend_kernel, layer, orders), (S(flat, F32), S(flat, BF16), units, units, S((2, width), F32)),
        [ANY] * 4 + [VM], [SM] * 3 + [ANY] * 13,
        [V(flat, BF16)] * 5 + [V(flat, F32), V(flat, BF16)] + [V(square, BF16)] * 3 + [V(flat, BF16)] * 3 + [V((4,) + block, BF16), V((rows, 3 * BUCKET), F32), V((2, 8, width), F32)],
        10, 4, 12 * rows * width * width, 15_000_000, "attend_gradient",
    )(*meta, low, low_x, dc, h_one, h_two, da1, *weights, *others, mix)


def exchange(value, bit):
    count = lax.axis_size("dp")
    return lax.ppermute(value, "dp", [(index, index ^ bit) for index in range(count)])


def swap(value):
    return lax.ppermute(value, "section", [(0, 1), (1, 0)])


def hand_over(value, source):
    return lax.ppermute(value, "section", [(source, 1 - source)])


def widen(value):
    return value.astype(F32)


class UnitSum:
    def __init__(self, orders, away, home, extra=None):
        self.paths = [EXCHANGES[order] for order in orders]
        self.home = home
        self.extra = extra
        self.flying = swap(away)
        self.flying_extra = None if extra is None else swap(extra)
        self.step = -1
        self.result = None

    def arrive(self):
        if self.step == -1:
            totals = [widen(self.home[color]) + widen(self.flying[color]) for color in range(2)]
            if self.extra is not None:
                extra = widen(self.extra) + widen(self.flying_extra)
                totals[1] = jnp.concatenate([totals[1], extra], axis=1)
        else:
            totals = [widen(keep) + widen(part) for keep, part in zip(self.keeps, self.flying)]
        self.step += 1
        if self.step == 4:
            self.result = [total[0] for total in totals]
            return self.result
        half = totals[0].shape[0] // 2
        self.keeps = [total[:half].astype(BF16) for total in totals]
        self.sends = [total[half:].astype(BF16) for total in totals]
        return self.sends

    def depart(self):
        bits = [path[self.step] for path in self.paths]
        if bits[0] == bits[1]:
            height = self.sends[0].shape[1]
            both = exchange(jnp.concatenate(self.sends, axis=1), bits[0])
            self.flying = [both[:, :height], both[:, height:]]
        else:
            self.flying = [exchange(value, bit) for value, bit in zip(self.sends, bits)]


def per_device(
    tokens, cotangent, bucket, batch_size, lengths, query_weight, query_offset, keys_weight, value_weight, value_offset,
    mixer_weight, mixer_offset, first_gain, first_shift, inner_weight, inner_offset, outer_weight, outer_offset,
    second_gain, second_shift,
):
    section = lax.axis_index("section")
    groups = lax.axis_size("dp")
    width = tokens.shape[2]
    hidden = inner_offset.shape[1]
    height = width // groups
    hypercube = groups == 16 and width % (16 * groups) == 0
    count = groups if hypercube else 1
    meta = (bucket, batch_size, lengths)
    weights = (query_weight, keys_weight, value_weight, mixer_weight, inner_weight, outer_weight)
    vectors = (query_offset, value_offset, mixer_offset, first_gain, first_shift, outer_offset, second_gain, second_shift)
    others = tuple(swap(weight) for weight in weights)
    bi_other = swap(inner_offset)
    y_a, low_a, total_a, wide_a, vec_own = first_forward(meta, tokens, 0, weights, vectors, inner_offset)
    vec_other = swap(vec_own)
    y_b, low_b, total_b, wide_b, _ = first_forward(meta, tokens, 1, weights, vectors, inner_offset)
    y_x = hand_over(y_b, 0)
    y_c, low_c, total_c, wide_c = second_forward(
        meta, y_a, y_x, weights, others, vec_own, vec_other, inner_offset, bi_other
    )
    low_x, total_x, wide_x = (hand_over(value, 0) for value in (low_b, total_b, wide_b))
    y_cx = hand_over(y_c, 0)
    kept = {1: (low_c, low_c, total_c, total_c, wide_c, wide_c), 0: (low_a, low_x, total_a, total_x, wide_a, wide_x)}
    entries = {1: (y_a, y_x), 0: (tokens, tokens)}
    orders = ((0, 1), (2, 3), (0, 1))
    sums = {}
    pending = []

    def boundary(value, moves):
        ready = []
        for name in moves:
            ready.extend(sums[name].arrive())
        if not ready:
            return value
        held = lax.optimization_barrier((value, *ready))
        ready = list(held[1:])
        for name in moves:
            unit = sums[name]
            if unit.step == 4:
                unit.result = [ready.pop(0), ready.pop(0)]
            else:
                unit.sends = [ready.pop(0), ready.pop(0)]
                unit.depart()
        return held[0]

    grad = cotangent
    moves = SCHEDULE if hypercube else ((),) * 9
    raw = {}
    dh = {}
    for layer in (1, 0):
        low, lowx, total, totalx, wide, widex = kept[layer]
        turn = 4 * (1 - layer)
        grad = boundary(grad, moves[turn])
        da2, dz, outer_away, outer_home, small_two = outer_gradient(
            layer, orders[0], count, meta, grad, total, totalx, wide, widex, vec_own, vec_other
        )
        if hypercube:
            sums["o", layer] = UnitSum(orders[0], outer_away, outer_home)
        dz = boundary(dz, moves[turn + 1])
        df, inner_away, inner_home, small_inner = inner_gradient(
            layer, orders[1], count, dz, wide, widex, low, lowx, outer_weight, others[5]
        )
        if hypercube:
            sums["i", layer] = UnitSum(orders[1], inner_away, inner_home)
        df = boundary(df, moves[turn + 2])
        da1, dc, mix, small_one = mixer_gradient(
            layer, orders[2], count, df, inner_weight, others[4], da2, total, totalx, low, lowx, mixer_weight, others[3],
            vec_own, vec_other,
        )
        dc = boundary(dc, moves[turn + 3])
        dh[layer], grad, attend_away, attend_home, small_attend = attend_gradient(
            layer, orders[2], count, meta, low, lowx, dc, entries[layer][0], entries[layer][1], da1, weights[:3],
            others[:3], mix,
        )
        smalls = jnp.concatenate([small_attend, small_one, small_two], axis=0)
        if hypercube:
            flat = smalls.reshape(8, groups, height).transpose(1, 0, 2).reshape(groups, 8 * height)
            blocks = jnp.concatenate([flat, small_inner.reshape(groups, hidden // groups)], axis=1)
            blocks = jnp.pad(blocks, ((0, 0), (0, width - blocks.shape[1])))
            dest = jnp.arange(groups, dtype=jnp.int32)
            spot = spot_of(orders[2][1], dest, lax.axis_index("dp"))
            picked = (spot[None, :] == dest[:, None]).astype(F32)
            blocks = jnp.sum(picked[:, :, None] * blocks[None, :, :], axis=1)
            extra = jnp.pad(blocks[:, None, :], ((0, 0), (0, 7), (0, 0))).astype(BF16)
            sums["t", layer] = UnitSum(orders[2], attend_away, attend_home, extra)
        else:
            raw[layer] = [(outer_away, outer_home), (inner_away, inner_home), (attend_away, attend_home), smalls, small_inner]
    dh_x1 = hand_over(dh[1], 0)
    dh_x0 = hand_over(dh[0], 1)
    first = section == 0
    layer_out = jnp.stack([jnp.where(first, y_a, y_cx), jnp.where(first, y_b, y_c)])
    input_grad = jnp.stack([jnp.where(first, dh[0], dh_x1), jnp.where(first, dh_x0, dh[1])])
    if hypercube:
        dependent = jnp.zeros((), F32)
        for names in moves[8:]:
            dependent = boundary(dependent, names)
        found = {name: unit.result for name, unit in sums.items()}
    else:
        found = {}

        def scatter(value, dimension=0):
            return lax.psum_scatter(value, "dp", scatter_dimension=dimension, tiled=True)

        for layer in (1, 0):
            for name, (away, home) in zip("oit", raw[layer][:3]):
                total = (widen(home) + widen(swap(away))).astype(BF16)[:, 0]
                found[name, layer] = [widen(scatter(total[color])) for color in range(2)]
    finals = []
    for name in "oit":
        early, late = (found[name, 1], found[name, 0])
        send = jnp.stack([jnp.where(first, a[:height], b[:height]) for a, b in zip(early, late)])
        back = swap(send)
        mine = [jnp.where(first, b, a) for a, b in zip(early, late)]
        low_units = [jnp.where(first, mine[color][:height], back[color]) for color in range(2)]
        high_units = [jnp.where(first, back[color], mine[color][:height]) for color in range(2)]
        finals.append(low_units + high_units)
        if name == "t":
            mixed = mine[1]
    query_grad, keys_grad, value_grad, mixer_grad = finals[2]
    inner_grad = jnp.concatenate(finals[1], axis=1)
    if hypercube:
        outer_grad = jnp.concatenate(finals[0], axis=0)
        line = mixed[height]
        small = [line[index * height : (index + 1) * height] for index in range(8)]
        small_wide = line[8 * height : 8 * height + hidden // groups]
    else:
        parts = [[], []]
        for layer in (1, 0):
            smalls, small_inner = raw[layer][3:]
            smalls = smalls + swap(smalls)
            small_inner = small_inner + swap(small_inner)
            parts[layer] = [scatter(smalls[index]) for index in range(8)] + [scatter(small_inner[0])]
        chosen = [jnp.where(first, a, b) for a, b in zip(parts[0], parts[1])]
        small, small_wide = (chosen[:8], chosen[8])
        wholes = []
        for layer in (1, 0):
            away, home = raw[layer][0]
            whole = (widen(home) + widen(swap(away))).astype(BF16)[:, 0]
            pair = swap(whole)
            ordered = jnp.where(first, jnp.concatenate([whole, pair]), jnp.concatenate([pair, whole]))
            wholes.append(scatter(ordered.reshape(hidden, width)))
        outer_grad = widen(jnp.where(first, wholes[1], wholes[0]))
    grad_query_offset, grad_value_offset, grad_first_gain, grad_first_shift, grad_mixer_offset = small[:5]
    grad_second_gain, grad_second_shift, grad_outer_offset = small[5:8]
    outputs = (
        layer_out, input_grad, query_grad, grad_query_offset, keys_grad, value_grad, grad_value_offset, mixer_grad,
        grad_mixer_offset, grad_first_gain, grad_first_shift, inner_grad, small_wide, outer_grad, grad_outer_offset,
        grad_second_gain, grad_second_shift,
    )
    return tuple(piece[None] for piece in outputs)


O1, I1, T1, O0, I0, T0 = (("o", 1), ("i", 1), ("t", 1), ("o", 0), ("i", 0), ("t", 0))
SCHEDULE = (
    (),
    (),
    (O1,),
    (I1,),
    (O1,),
    (I1, T1),
    (O1, O0),
    (T1, I1, I0),
    (O1, O0, T1, T0),
    (I1, O1),
    (I0, O0, T0),
    (T1, I1),
    (O0, I0, T0),
    (T1, O0),
    (I0, T0),
    (I0, T0),
)


def solution(mesh):
    matrix = P("section", None, None)
    vector = P("section", None)
    in_specs = (
        P("dp", None, None), P("dp", None, None), P("dp"), P("dp"), P("dp", None), matrix, vector, matrix, matrix, vector,
        matrix, vector, vector, vector, matrix, vector, matrix, vector, vector, vector,
    )
    rows = P("section", "dp", None, None)
    grad = P("section", "dp", None)
    small = P("section", "dp")
    out_specs = (rows, rows, grad, small, grad, grad, small, grad, small, small, small, grad, small, grad, small, small, small)
    return jax.shard_map(per_device, mesh=mesh, in_specs=in_specs, out_specs=out_specs, check_vma=False)
```

time: 1530 us -> 422 us (0.28)
  waiting for transfers between devices: 844 us -> 122 us
  matrix products: 235 us -> 0 us
  Pallas kernels: 0 us -> 157 us
  other arithmetic: 178 us -> 43.2 us
  blocking collectives: 80.3 us -> 0 us
  local copies, waits for them, and re-layouts: 91.7 us -> 26.6 us
  loops' own time: 18.5 us -> 0 us
    reduce_scatter x6 -> x0, waiting for transfers between devices: 786 us -> none  [per_device(): summed = lax.psum_scatter(totals, 'dp', scatter_dimension=0, tiled=True)]
    dot_general x58 -> x0, matrix products: 212 us -> none  [the longest x36 113 us: contract(): return jnp.einsum(pattern, left, right, preferred_element_type=jnp.float32)]
    pallas_call x0 -> x11, Pallas kernels: none -> 157 us  [the longest x2 37.5 us: first_forward(): run_kernel(functools.partial(first_forward_kernel, index), outs + (S((8,...]
    add x27 -> x5, other arithmetic: 115 us -> 3.32 us  [the longest x2 3.18 us: arrive(): widen(self.home[color]) + widen(self.flying[color])]
    unnamed x1 -> x0, blocking collectives: 80.3 us -> none
    ppermute x6 -> x62, waiting for transfers between devices: 54.9 us -> 122 us  [the longest x36 113 us: exchange(): lax.ppermute(value, 'dp', [(index, index ^ bit) for index in range(count)])]
    dynamic_slice x19 -> x0, local copies, waits for them, and re-layouts: 24.1 us -> none  [the longest x6 7.88 us: per_device(): lax.scan(forward_tick, start_rows, jnp.arange(micro_count + 1))]
    sub x4 -> x0, matrix products: 23.9 us -> none  [forward_pieces(): attention = jax.nn.softmax(scores, axis=-1)]
  transfers between devices with their start and end apart: 12 -> 62, of which waited for: 10 -> 24; matrix products, arithmetic and copies ran while one was open for 9% -> 14% of each run, Pallas kernels for 0% -> 31%
where the time goes in v2:
time: 422 us; the launch traced here: 414 us
  Pallas kernels  157 us (37%)
  waiting for transfers between devices  122 us (29%)
  starting transfers between devices  62.7 us (15%)
  other arithmetic  43.2 us (10%)
  local copies, waits for them, and re-layouts  26.6 us (6%)
    ppermute x36, waiting for transfers between devices, exchange(): lax.ppermute(value, 'dp', [(index, index ^ bit) for index in range(count)])  113 us
    ppermute x36, starting transfers between devices, exchange(): lax.ppermute(value, 'dp', [(index, index ^ bit) for index in range(count)])  39.2 us
    pallas_call x2, Pallas kernels, first_forward(): run_kernel(functools.partial(first_forward_kernel, index), outs + (S((8,...  37.5 us
    pallas_call x2, Pallas kernels, attend_gradient(): run_kernel(functools.partial(attend_kernel, layer, orders), (S(flat, F32)...  36.8 us
    pallas_call x2, Pallas kernels, mixer_gradient(): run_kernel(functools.partial(mixer_kernel, layer, orders), (S(flat, F32),...  23 us
    pallas_call x2, Pallas kernels, inner_gradient(): run_kernel(functools.partial(inner_kernel, layer, orders), (S((rows, hidd...  22.9 us
    another operation x40, other arithmetic  21.2 us
    pallas_call x2, Pallas kernels, outer_gradient(): run_kernel(functools.partial(outer_kernel, layer, orders), (S(flat, F32),...  18.3 us
  transfers between devices with their start and end apart: 62, of which 24 were waited for; matrix products, arithmetic and copies ran while one was open for 14% of the time, Pallas kernels for 31%

profile of v2, /device:TPU:0, one launch (start us, length us, event | category | flops | bytes accessed | tf_op | source)
XLA Modules:
  0.0 414.1 jit_solution(364893905873595408)
XLA Ops:
  1.7 18.4 %first_forward.3 = (bf16[384,768]{1,0:T(8,128)(2,1)}, bf16[5,384,768]{2,1,0:T(8,128)(2,1)}, f32[2,384,768]{2,1,0:T(8,128)}, bf16[2,384,3072]{2,1,0:T(8,128)(2,1)}, f32[8,768]{1,0:T(8,128)}) custom-call(s32[2]{0:T(128)} %bucket.13, s32[2]{0:T(128)} %count.13, s32[2,6]{1,0:T(2,128)} %lengths.13, bf16[2,384,768]{2,1,0:T(8,128)(2,1)} %h_two.1, ...), custom_call_target="tpu_custom_call" | custom-call | flops 5435817984 | bytes 25000000 | tf_op jit(solution)/shard_map/first_forward/pallas_call | solution.py:391
  22.4 19.1 %first_forward.2 = (bf16[384,768]{1,0:T(8,128)(2,1)}, bf16[5,384,768]{2,1,0:T(8,128)(2,1)}, f32[2,384,768]{2,1,0:T(8,128)}, bf16[2,384,3072]{2,1,0:T(8,128)(2,1)}, f32[8,768]{1,0:T(8,128)}) custom-call(s32[2]{0:T(128)} %bucket.13, s32[2]{0:T(128)} %count.13, s32[2,6]{1,0:T(2,128)} %lengths.13, bf16[2,384,768]{2,1,0:T(8,128)(2,1)} %h_two.1, ...), custom_call_target="tpu_custom_call" | custom-call | flops 5435817984 | bytes 25000000 | tf_op jit(solution)/shard_map/first_forward/pallas_call | solution.py:391
  45.9 3.6 collective-permute-done.3.xv
  50.9 18.0 %second_forward.1 = (bf16[384,768]{1,0:T(8,128)(2,1)}, bf16[5,384,768]{2,1,0:T(8,128)(2,1)}, f32[2,384,768]{2,1,0:T(8,128)}, bf16[2,384,3072]{2,1,0:T(8,128)(2,1)}) custom-call(s32[2]{0:T(128)} %bucket.13, s32[2]{0:T(128)} %count.13, s32[2,6]{1,0:T(2,128)} %lengths.13, bf16[384,768]{1,0:T(8,128)(2,1)} %get-tuple-element.131.y_own.h_one, ...), custom_call_target="tpu_custom_call" | custom-call | flops 5435817984 | bytes 25000000 | tf_op jit(solution)/shard_map/second_forward/pallas_call | solution.py:400
  68.9 9.2 %outer_gradient.2 = (f32[384,768]{1,0:T(8,128)}, bf16[384,768]{1,0:T(8,128)(2,1)}, bf16[2,16,48,768]{3,2,1,0:T(8,128)(2,1)}, bf16[2,16,48,768]{3,2,1,0:T(8,128)(2,1)}, f32[3,768]{1,0:T(4,128)}) custom-call(s32[2]{0:T(128)} %bucket.13, s32[2]{0:T(128)} %count.13, s32[2,6]{1,0:T(2,128)} %lengths.13, f32[2,384,768]{2,1,0:T(8,128)} %g.1, ...), custom_call_target="tpu_custom_call" | custom-call | flops 1811939328 | bytes 12000000 | tf_op jit(solution)/shard_map/outer_gradient/pallas_call | solution.py:684
  78.3 11.5 %inner_gradient.2 = (bf16[384,3072]{1,0:T(8,128)(2,1)}, bf16[2,16,48,768]{3,2,1,0:T(8,128)(2,1)}, bf16[2,16,48,768]{3,2,1,0:T(8,128)(2,1)}, f32[1,3072]{1,0:T(1,128)}) custom-call(bf16[384,768]{1,0:T(8,128)(2,1)} %get-tuple-element.140.dz, bf16[2,384,3072]{2,1,0:T(8,128)(2,1)} %get-tuple-element.139.wide.wide_x, ...), custom_call_target="tpu_custom_call" | custom-call | flops 3623878656 | bytes 18000000 | tf_op jit(solution)/shard_map/inner_gradient/pallas_call | solution.py:697
  90.3 4.2 %collective-permute-start.16 = (bf16[2,384,3072]{2,1,0:T(8,128)(2,1)}, bf16[2,384,3072]{2,1,0:T(8,128)(2,1)}, u32[]{:S(2)}, u32[]{:S(2)}) collective-permute-start(bf16[2,384,3072]{2,1,0:T(8,128)(2,1)} %get-tuple-element.159), channel_id=1, source_target_pairs={{0,1},{2,3},{4,5},{6,7},{8,9},{10,11},{12,13},{14,15},{16,17},{18,... | collective-permute-start | bytes 14155784 | tf_op jit(solution)/shard_map/ppermute | solution.py:741
  113.4 11.5 %mixer_gradient.2 = (f32[384,768]{1,0:T(8,128)}, bf16[384,768]{1,0:T(8,128)(2,1)}, bf16[16,48,768]{2,1,0:T(8,128)(2,1)}, f32[3,768]{1,0:T(4,128)}) custom-call(bf16[384,3072]{1,0:T(8,128)(2,1)} %get-tuple-element.144.df, bf16[1,768,3072]{2,1,0:T(8,128)(2,1)} %wi.9, bf16[1,768,3072]{2,1,0:T(8,128)(2,1)} %collective-permute-done.5.xi.wi_x, ...), custom_call_target="tpu_custom_call" | custom-call | flops 2717908992 | bytes 15000000 | tf_op jit(solution)/shard_map/mixer_gradient/pallas_call | solution.py:710
  124.8 18.4 %attend_gradient.2 = (f32[384,768]{1,0:T(8,128)}, bf16[384,768]{1,0:T(8,128)(2,1)}, bf16[2,16,48,768]{3,2,1,0:T(8,128)(2,1)}, bf16[2,16,48,768]{3,2,1,0:T(8,128)(2,1)}, f32[2,768]{1,0:T(2,128)}) custom-call(s32[2]{0:T(128)} %bucket.13, s32[2]{0:T(128)} %count.13, s32[2,6]{1,0:T(2,128)} %lengths.13, bf16[5,384,768]{2,1,0:T(8,128)(2,1)} %get-tuple-element.137.low.low_x, ...), custom_call_target="tpu_custom_call" | custom-call | flops 2717908992 | bytes 15000000 | tf_op jit(solution)/shard_map/attend_gradient/pallas_call | solution.py:723
  151.4 3.1 collective-permute-start.10
  157.0 4.4 %collective-permute-done.14 = bf16[8,48,768]{2,1,0:T(8,128)(2,1)} collective-permute-done((bf16[8,48,768]{2,1,0:T(8,128)(2,1)}, bf16[8,48,768]{2,1,0:T(8,128)(2,1)}, u32[]{:S(2)}, u32[]{:S(2)}) %collective-permute-start.14) | collective-permute-done | bytes 589856 | tf_op jit(solution)/shard_map/ppermute | solution.py:733
  169.5 9.1 %outer_gradient.3 = (f32[384,768]{1,0:T(8,128)}, bf16[384,768]{1,0:T(8,128)(2,1)}, bf16[2,16,48,768]{3,2,1,0:T(8,128)(2,1)}, bf16[2,16,48,768]{3,2,1,0:T(8,128)(2,1)}, f32[3,768]{1,0:T(4,128)}) custom-call(s32[2]{0:T(128)} %bucket.13, s32[2]{0:T(128)} %count.13, s32[2,6]{1,0:T(2,128)} %lengths.13, bf16[384,768]{1,0:T(8,128)(2,1)} %get-tuple-element.155.g, ...), custom_call_target="tpu_custom_call" | custom-call | flops 1811939328 | bytes 12000000 | tf_op jit(solution)/shard_map/outer_gradient/pallas_call | solution.py:684
  178.6 2.8 collective-permute-start.28
  181.8 7.5 %collective-permute-done.17 = bf16[8,96,768]{2,1,0:T(8,128)(2,1)} collective-permute-done((bf16[8,96,768]{2,1,0:T(8,128)(2,1)}, bf16[8,96,768]{2,1,0:T(8,128)(2,1)}, u32[]{:S(2)}, u32[]{:S(2)}) %collective-permute-start.17) | collective-permute-done | bytes 1179680 | tf_op jit(solution)/shard_map/ppermute | solution.py:733
  201.7 11.5 %inner_gradient.3 = (bf16[384,3072]{1,0:T(8,128)(2,1)}, bf16[2,16,48,768]{3,2,1,0:T(8,128)(2,1)}, bf16[2,16,48,768]{3,2,1,0:T(8,128)(2,1)}, f32[1,3072]{1,0:T(1,128)}) custom-call(bf16[384,768]{1,0:T(8,128)(2,1)} %get-tuple-element.169.dz, bf16[2,384,3072]{2,1,0:T(8,128)(2,1)} %get-tuple-element.158.wide, ...), custom_call_target="tpu_custom_call" | custom-call | flops 3623878656 | bytes 18000000 | tf_op jit(solution)/shard_map/inner_gradient/pallas_call | solution.py:697
  224.7 8.4 %collective-permute-done.23 = bf16[8,48,768]{2,1,0:T(8,128)(2,1)S(1)} collective-permute-done((bf16[8,48,768]{2,1,0:T(8,128)(2,1)}, bf16[8,48,768]{2,1,0:T(8,128)(2,1)S(1)}, u32[]{:S(2)}, u32[]{:S(2)}) %collective-permute-start.23) | collective-permute-done | bytes 589856 | tf_op jit(solution)/shard_map/ppermute | solution.py:733
  234.7 11.5 %mixer_gradient.3 = (f32[384,768]{1,0:T(8,128)}, bf16[384,768]{1,0:T(8,128)(2,1)}, bf16[16,48,768]{2,1,0:T(8,128)(2,1)}, f32[3,768]{1,0:T(4,128)}) custom-call(bf16[384,3072]{1,0:T(8,128)(2,1)} %get-tuple-element.175.df, bf16[1,768,3072]{2,1,0:T(8,128)(2,1)} %wi.9, bf16[1,768,3072]{2,1,0:T(8,128)(2,1)} %collective-permute-done.5.xi.wi_x, ...), custom_call_target="tpu_custom_call" | custom-call | flops 2717908992 | bytes 15000000 | tf_op jit(solution)/shard_map/mixer_gradient/pallas_call | solution.py:710
  253.1 8.5 %collective-permute-done.31 = bf16[8,48,768]{2,1,0:T(8,128)(2,1)S(1)} collective-permute-done((bf16[8,48,768]{2,1,0:T(8,128)(2,1)}, bf16[8,48,768]{2,1,0:T(8,128)(2,1)S(1)}, u32[]{:S(2)}, u32[]{:S(2)}) %collective-permute-start.31) | collective-permute-done | bytes 589856 | tf_op jit(solution)/shard_map/ppermute | solution.py:733
  266.7 18.4 %attend_gradient.3 = (f32[384,768]{1,0:T(8,128)}, bf16[384,768]{1,0:T(8,128)(2,1)}, bf16[2,16,48,768]{3,2,1,0:T(8,128)(2,1)}, bf16[2,16,48,768]{3,2,1,0:T(8,128)(2,1)}, f32[2,768]{1,0:T(2,128)}) custom-call(s32[2]{0:T(128)} %bucket.13, s32[2]{0:T(128)} %count.13, s32[2,6]{1,0:T(2,128)} %lengths.13, bf16[5,384,768]{2,1,0:T(8,128)(2,1)} %get-tuple-element.135.low, ...), custom_call_target="tpu_custom_call" | custom-call | flops 2717908992 | bytes 15000000 | tf_op jit(solution)/shard_map/attend_gradient/pallas_call | solution.py:723
  291.2 3.4 collective-permute-done.54
  296.3 3.5 collective-permute-done.53
  302.8 4.2 %collective-permute-done.34 = bf16[4,48,768]{2,1,0:T(8,128)(2,1)S(1)} collective-permute-done((bf16[4,48,768]{2,1,0:T(8,128)(2,1)S(1)}, bf16[4,48,768]{2,1,0:T(8,128)(2,1)S(1)}, u32[]{:S(2)}, u32[]{:S(2)}) %collective-permute-start.34) | collective-permute-done | bytes 294944 | tf_op jit(solution)/shard_map/ppermute | solution.py:733
  310.1 6.3 %collective-permute-done.30 = bf16[8,96,768]{2,1,0:T(8,128)(2,1)S(1)} collective-permute-done((bf16[8,96,768]{2,1,0:T(8,128)(2,1)S(1)}, bf16[8,96,768]{2,1,0:T(8,128)(2,1)S(1)}, u32[]{:S(2)}, u32[]{:S(2)}) %collective-permute-start.30) | collective-permute-done | bytes 1179680 | tf_op jit(solution)/shard_map/ppermute | solution.py:733
  332.3 16.4 %collective-permute-done.39 = bf16[4,48,768]{2,1,0:T(8,128)(2,1)S(1)} collective-permute-done((bf16[4,48,768]{2,1,0:T(8,128)(2,1)S(1)}, bf16[4,48,768]{2,1,0:T(8,128)(2,1)S(1)}, u32[]{:S(2)}, u32[]{:S(2)}) %collective-permute-start.39) | collective-permute-done | bytes 294944 | tf_op jit(solution)/shard_map/ppermute | solution.py:733
  350.2 6.5 %collective-permute-done.56 = bf16[1,96,768]{2,1,0:T(8,128)(2,1)S(1)} collective-permute-done((bf16[1,96,768]{2,1,0:T(8,128)(2,1)S(1)}, bf16[1,96,768]{2,1,0:T(8,128)(2,1)S(1)}, u32[]{:S(2)}, u32[]{:S(2)}) %collective-permute-start.56) | collective-permute-done | bytes 147488 | tf_op jit(solution)/shard_map/ppermute | solution.py:733
  358.6 7.0 %collective-permute-done.57 = bf16[1,104,768]{2,1,0:T(8,128)(2,1)S(1)} collective-permute-done((bf16[1,104,768]{2,1,0:T(8,128)(2,1)S(1)}, bf16[1,104,768]{2,1,0:T(8,128)(2,1)S(1)}, u32[]{:S(2)}, u32[]{:S(2)}) %collective-permute-start.57) | collective-permute-done | bytes 159776 | tf_op jit(solution)/shard_map/ppermute | solution.py:733
  368.0 6.9 %collective-permute-done.44 = bf16[4,48,768]{2,1,0:T(8,128)(2,1)S(1)} collective-permute-done((bf16[4,48,768]{2,1,0:T(8,128)(2,1)S(1)}, bf16[4,48,768]{2,1,0:T(8,128)(2,1)S(1)}, u32[]{:S(2)}, u32[]{:S(2)}) %collective-permute-start.44) | collective-permute-done | bytes 294944 | tf_op jit(solution)/shard_map/ppermute | solution.py:733
  375.0 7.0 %collective-permute-done.42 = bf16[4,48,768]{2,1,0:T(8,128)(2,1)S(1)} collective-permute-done((bf16[4,48,768]{2,1,0:T(8,128)(2,1)S(1)}, bf16[4,48,768]{2,1,0:T(8,128)(2,1)S(1)}, u32[]{:S(2)}, u32[]{:S(2)}) %collective-permute-start.42) | collective-permute-done | bytes 294944 | tf_op jit(solution)/shard_map/ppermute | solution.py:733
  386.6 4.1 collective-permute-done.58
  391.1 3.9 collective-permute-done.49
  395.3 3.0 collective-permute-start.50
  399.2 10.5 %collective-permute-done.50 = bf16[1,96,768]{2,1,0:T(8,128)(2,1)S(1)} collective-permute-done((bf16[1,96,768]{2,1,0:T(8,128)(2,1)S(1)}, bf16[1,96,768]{2,1,0:T(8,128)(2,1)S(1)}, u32[]{:S(2)}, u32[]{:S(2)}) %collective-permute-start.50) | collective-permute-done | bytes 147488 | tf_op jit(solution)/shard_map/ppermute | solution.py:733
  (421 shorter events, 129.5 us)
Async XLA Ops:
  0.7 48.8 %collective-permute-start.5 = (bf16[1,768,3072]{2,1,0:T(8,128)(2,1)}, bf16[1,768,3072]{2,1,0:T(8,128)(2,1)}, u32[]{:S(2)}, u32[]{:S(2)}) collective-permute-start(bf16[1,768,3072]{2,1,0:T(8,128)(2,1)} %wi.9), channel_id=1, source_target_pairs={{0,1},{1,0},{2,3},{3,2},{4,5},{5,4},{6,7},{7,6},{8,9},{9,8},{10,11... | collective-permute-start | bytes 14155784 | tf_op jit(solution)/shard_map/ppermute | solution.py:737
  1.2 49.4 %collective-permute-start.6 = (bf16[1,3072,768]{2,1,0:T(8,128)(2,1)}, bf16[1,3072,768]{2,1,0:T(8,128)(2,1)}, u32[]{:S(2)}, u32[]{:S(2)}) collective-permute-start(bf16[1,3072,768]{2,1,0:T(8,128)(2,1)} %wo.9), channel_id=1, source_target_pairs={{0,1},{1,0},{2,3},{3,2},{4,5},{5,4},{6,7},{7,6},{8,9},{9,8},{10,11... | collective-permute-start | bytes 14155784 | tf_op jit(solution)/shard_map/ppermute | solution.py:737
  1.3 42.3 %collective-permute-start.1 = (bf16[1,768,768]{2,1,0:T(8,128)(2,1)}, bf16[1,768,768]{2,1,0:T(8,128)(2,1)}, u32[]{:S(2)}, u32[]{:S(2)}) collective-permute-start(bf16[1,768,768]{2,1,0:T(8,128)(2,1)} %wq.9), channel_id=1, source_target_pairs={{0,1},{1,0},{2,3},{3,2},{4,5},{5,4},{6,7},{7,6},{8,9},{9,8},{10,11... | collective-permute-start | bytes 3538952 | tf_op jit(solution)/shard_map/ppermute | solution.py:737
  20.2 23.0 %collective-permute-start = (bf16[384,768]{1,0:T(8,128)(2,1)}, bf16[384,768]{1,0:T(8,128)(2,1)}, u32[]{:S(2)}, u32[]{:S(2)}) collective-permute-start(bf16[384,768]{1,0:T(8,128)(2,1)} %get-tuple-element.132), channel_id=1, source_target_pairs={{0,1},{2,3},{4,5},{6,7},{8,9},{10,11},{12,13},{14,15},{16,17},{18,... | collective-permute-start | bytes 1769480 | tf_op jit(solution)/shard_map/ppermute | solution.py:741
  22.4 19.1 %collective-permute-start.8 = (f32[1,3072]{1,0:T(1,128)S(1)}, f32[1,3072]{1,0:T(1,128)S(1)}, u32[]{:S(2)}, u32[]{:S(2)}) collective-permute-start(f32[1,3072]{1,0:T(1,128)S(1)} %copy-done.72), channel_id=1, source_target_pairs={{0,1},{1,0},{2,3},{3,2},{4,5},{5,4},{6,7},{7,6},{8,9},{9,8},{10,11... | collective-permute-start | bytes 36872 | tf_op jit(solution)/shard_map/ppermute | solution.py:737
  78.2 25.9 %collective-permute-start.11 = (bf16[2,16,48,768]{3,2,1,0:T(8,128)(2,1)}, bf16[2,16,48,768]{3,2,1,0:T(8,128)(2,1)}, u32[]{:S(2)}, u32[]{:S(2)}) collective-permute-start(bf16[2,16,48,768]{3,2,1,0:T(8,128)(2,1)} %get-tuple-element.143), channel_id=1, source_target_pairs={{0,1},{1,0},{2,3},{3,2},{4,5},{5,4},{6,7},{7,6},{8,9},{9,8},{10,11... | collective-permute-start | bytes 7077896 | tf_op jit(solution)/shard_map/ppermute | solution.py:737
  89.7 18.4 %collective-permute-start.12 = (bf16[2,16,48,768]{3,2,1,0:T(8,128)(2,1)}, bf16[2,16,48,768]{3,2,1,0:T(8,128)(2,1)}, u32[]{:S(2)}, u32[]{:S(2)}) collective-permute-start(bf16[2,16,48,768]{3,2,1,0:T(8,128)(2,1)} %get-tuple-element.148), channel_id=1, source_target_pairs={{0,1},{1,0},{2,3},{3,2},{4,5},{5,4},{6,7},{7,6},{8,9},{9,8},{10,11... | collective-permute-start | bytes 7077896 | tf_op jit(solution)/shard_map/ppermute | solution.py:737
  90.3 77.8 %collective-permute-start.16 = (bf16[2,384,3072]{2,1,0:T(8,128)(2,1)}, bf16[2,384,3072]{2,1,0:T(8,128)(2,1)}, u32[]{:S(2)}, u32[]{:S(2)}) collective-permute-start(bf16[2,384,3072]{2,1,0:T(8,128)(2,1)} %get-tuple-element.159), channel_id=1, source_target_pairs={{0,1},{2,3},{4,5},{6,7},{8,9},{10,11},{12,13},{14,15},{16,17},{18,... | collective-permute-start | bytes 14155784 | tf_op jit(solution)/shard_map/ppermute | solution.py:741
  94.5 56.9 %collective-permute-start.15 = (f32[2,384,768]{2,1,0:T(8,128)}, f32[2,384,768]{2,1,0:T(8,128)S(1)}, u32[]{:S(2)}, u32[]{:S(2)}) collective-permute-start(f32[2,384,768]{2,1,0:T(8,128)} %get-tuple-element.157), channel_id=1, source_target_pairs={{0,1},{2,3},{4,5},{6,7},{8,9},{10,11},{12,13},{14,15},{16,17},{18,... | collective-permute-start | bytes 7077896 | tf_op jit(solution)/shard_map/ppermute | solution.py:741
  143.2 49.3 %collective-permute-start.18 = (bf16[2,16,48,768]{3,2,1,0:T(8,128)(2,1)}, bf16[2,16,48,768]{3,2,1,0:T(8,128)(2,1)}, u32[]{:S(2)}, u32[]{:S(2)}) collective-permute-start(bf16[2,16,48,768]{3,2,1,0:T(8,128)(2,1)} %get-tuple-element.164), channel_id=1, source_target_pairs={{0,1},{1,0},{2,3},{3,2},{4,5},{5,4},{6,7},{7,6},{8,9},{9,8},{10,11... | collective-permute-start | bytes 7077896 | tf_op jit(solution)/shard_map/ppermute | solution.py:737
  145.3 16.1 %collective-permute-start.14 = (bf16[8,48,768]{2,1,0:T(8,128)(2,1)}, bf16[8,48,768]{2,1,0:T(8,128)(2,1)}, u32[]{:S(2)}, u32[]{:S(2)}) collective-permute-start(bf16[8,48,768]{2,1,0:T(8,128)(2,1)} %slice_bitcast_fusion.18), channel_id=1, source_target_pairs={{0,4},{2,6},{4,0},{6,2},{8,12},{10,14},{12,8},{14,10},{16,20},{18,... | collective-permute-start | bytes 1769480 | tf_op jit(solution)/shard_map/ppermute | solution.py:733
  150.1 15.3 %collective-permute-start.13 = (bf16[8,48,768]{2,1,0:T(8,128)(2,1)}, bf16[8,48,768]{2,1,0:T(8,128)(2,1)S(1)}, u32[]{:S(2)}, u32[]{:S(2)}) collective-permute-start(bf16[8,48,768]{2,1,0:T(8,128)(2,1)} %slice_bitcast_fusion.19), channel_id=1, source_target_pairs={{0,2},{2,0},{4,6},{6,4},{8,10},{10,8},{12,14},{14,12},{16,18},{18,... | collective-permute-start | bytes 1769480 | tf_op jit(solution)/shard_map/ppermute | solution.py:733
  151.4 50.3 %collective-permute-start.10 = (bf16[5,384,768]{2,1,0:T(8,128)(2,1)}, bf16[5,384,768]{2,1,0:T(8,128)(2,1)}, u32[]{:S(2)}, u32[]{:S(2)}) collective-permute-start(bf16[5,384,768]{2,1,0:T(8,128)(2,1)} %get-tuple-element.136), channel_id=1, source_target_pairs={{0,1},{2,3},{4,5},{6,7},{8,9},{10,11},{12,13},{14,15},{16,17},{18,... | collective-permute-start | bytes 8847368 | tf_op jit(solution)/shard_map/ppermute | solution.py:741
  161.4 27.8 %collective-permute-start.17 = (bf16[8,96,768]{2,1,0:T(8,128)(2,1)}, bf16[8,96,768]{2,1,0:T(8,128)(2,1)}, u32[]{:S(2)}, u32[]{:S(2)}) collective-permute-start(bf16[8,96,768]{2,1,0:T(8,128)(2,1)} %pad_maximum_fusion), channel_id=1, source_target_pairs={{0,8},{2,10},{4,12},{6,14},{8,0},{10,2},{12,4},{14,6},{16,24},{18,... | collective-permute-start | bytes 3538952 | tf_op jit(solution)/shard_map/ppermute | solution.py:733
  178.6 110.7 %collective-permute-start.28 = (f32[384,768]{1,0:T(8,128)}, f32[384,768]{1,0:T(8,128)}, u32[]{:S(2)}, u32[]{:S(2)}) collective-permute-start(f32[384,768]{1,0:T(8,128)} %get-tuple-element.188), channel_id=1, source_target_pairs={{0,1},{2,3},{4,5},{6,7},{8,9},{10,11},{12,13},{14,15},{16,17},{18,... | collective-permute-start | bytes 3538952 | tf_op jit(solution)/shard_map/ppermute | solution.py:741
  181.6 37.0 %collective-permute-start.22 = (bf16[2,16,48,768]{3,2,1,0:T(8,128)(2,1)}, bf16[2,16,48,768]{3,2,1,0:T(8,128)(2,1)}, u32[]{:S(2)}, u32[]{:S(2)}) collective-permute-start(bf16[2,16,48,768]{3,2,1,0:T(8,128)(2,1)} %get-tuple-element.174), channel_id=1, source_target_pairs={{0,1},{1,0},{2,3},{3,2},{4,5},{5,4},{6,7},{7,6},{8,9},{9,8},{10,11... | collective-permute-start | bytes 7077896 | tf_op jit(solution)/shard_map/ppermute | solution.py:737
  198.6 16.1 %collective-permute-start.26 = (bf16[4,48,768]{2,1,0:T(8,128)(2,1)}, bf16[4,48,768]{2,1,0:T(8,128)(2,1)}, u32[]{:S(2)}, u32[]{:S(2)}) collective-permute-start(bf16[4,48,768]{2,1,0:T(8,128)(2,1)} %slice.807), channel_id=1, source_target_pairs={{0,4},{2,6},{4,0},{6,2},{8,12},{10,14},{12,8},{14,10},{16,20},{18,... | collective-permute-start | bytes 884744 | tf_op jit(solution)/shard_map/ppermute | solution.py:733
  200.2 17.1 %collective-permute-start.25 = (bf16[4,48,768]{2,1,0:T(8,128)(2,1)}, bf16[4,48,768]{2,1,0:T(8,128)(2,1)S(1)}, u32[]{:S(2)}, u32[]{:S(2)}) collective-permute-start(bf16[4,48,768]{2,1,0:T(8,128)(2,1)} %slice.804), channel_id=1, source_target_pairs={{0,2},{2,0},{4,6},{6,4},{8,10},{10,8},{12,14},{14,12},{16,18},{18,... | collective-permute-start | bytes 884744 | tf_op jit(solution)/shard_map/ppermute | solution.py:733
  213.1 49.5 %collective-permute-start.27 = (bf16[2,16,48,768]{3,2,1,0:T(8,128)(2,1)}, bf16[2,16,48,768]{3,2,1,0:T(8,128)(2,1)}, u32[]{:S(2)}, u32[]{:S(2)}) collective-permute-start(bf16[2,16,48,768]{3,2,1,0:T(8,128)(2,1)} %get-tuple-element.183), channel_id=1, source_target_pairs={{0,1},{1,0},{2,3},{3,2},{4,5},{5,4},{6,7},{7,6},{8,9},{9,8},{10,11... | collective-permute-start | bytes 7077896 | tf_op jit(solution)/shard_map/ppermute | solution.py:737
  214.7 32.3 %collective-permute-start.24 = (bf16[8,56,768]{2,1,0:T(8,128)(2,1)}, bf16[8,56,768]{2,1,0:T(8,128)(2,1)}, u32[]{:S(2)}, u32[]{:S(2)}) collective-permute-start(bf16[8,56,768]{2,1,0:T(8,128)(2,1)} %slice.811), channel_id=1, source_target_pairs={{0,4},{2,6},{4,0},{6,2},{8,12},{10,14},{12,8},{14,10},{16,20},{18,... | collective-permute-start | bytes 2064392 | tf_op jit(solution)/shard_map/ppermute | solution.py:733
  217.3 15.8 %collective-permute-start.23 = (bf16[8,48,768]{2,1,0:T(8,128)(2,1)}, bf16[8,48,768]{2,1,0:T(8,128)(2,1)S(1)}, u32[]{:S(2)}, u32[]{:S(2)}) collective-permute-start(bf16[8,48,768]{2,1,0:T(8,128)(2,1)} %slice_bitcast_fusion.11), channel_id=1, source_target_pairs={{0,2},{2,0},{4,6},{6,4},{8,10},{10,8},{12,14},{14,12},{16,18},{18,... | collective-permute-start | bytes 1769480 | tf_op jit(solution)/shard_map/ppermute | solution.py:733
  222.6 28.4 %collective-permute-start.33 = (bf16[8,48,768]{2,1,0:T(8,128)(2,1)}, bf16[8,48,768]{2,1,0:T(8,128)(2,1)}, u32[]{:S(2)}, u32[]{:S(2)}) collective-permute-start(bf16[8,48,768]{2,1,0:T(8,128)(2,1)} %slice_bitcast_fusion.9), channel_id=1, source_target_pairs={{0,4},{2,6},{4,0},{6,2},{8,12},{10,14},{12,8},{14,10},{16,20},{18,... | collective-permute-start | bytes 1769480 | tf_op jit(solution)/shard_map/ppermute | solution.py:733
  233.1 16.5 %collective-permute-start.32 = (bf16[2,96,768]{2,1,0:T(8,128)(2,1)}, bf16[2,96,768]{2,1,0:T(8,128)(2,1)S(1)}, u32[]{:S(2)}, u32[]{:S(2)}) collective-permute-start(bf16[2,96,768]{2,1,0:T(8,128)(2,1)} %pad_maximum_fusion.4), channel_id=1, source_target_pairs={{0,8},{2,10},{4,12},{6,14},{8,0},{10,2},{12,4},{14,6},{16,24},{18,... | collective-permute-start | bytes 884744 | tf_op jit(solution)/shard_map/ppermute | solution.py:733
  285.1 31.8 %collective-permute-start.36 = (bf16[2,16,48,768]{3,2,1,0:T(8,128)(2,1)}, bf16[2,16,48,768]{3,2,1,0:T(8,128)(2,1)}, u32[]{:S(2)}, u32[]{:S(2)}) collective-permute-start(bf16[2,16,48,768]{3,2,1,0:T(8,128)(2,1)} %get-tuple-element.198), channel_id=1, source_target_pairs={{0,1},{1,0},{2,3},{3,2},{4,5},{5,4},{6,7},{7,6},{8,9},{9,8},{10,11... | collective-permute-start | bytes 7077896 | tf_op jit(solution)/shard_map/ppermute | solution.py:737
  288.2 28.1 %collective-permute-start.30 = (bf16[8,96,768]{2,1,0:T(8,128)(2,1)S(1)}, bf16[8,96,768]{2,1,0:T(8,128)(2,1)S(1)}, u32[]{:S(2)}, u32[]{:S(2)}) collective-permute-start(bf16[8,96,768]{2,1,0:T(8,128)(2,1)S(1)} %pad_maximum_fusion.1), channel_id=1, source_target_pairs={{0,8},{2,10},{4,12},{6,14},{8,0},{10,2},{12,4},{14,6},{16,24},{18,... | collective-permute-start | bytes 3538952 | tf_op jit(solution)/shard_map/ppermute | solution.py:733
  289.3 27.3 %collective-permute-start.29 = (f32[384,768]{1,0:T(8,128)S(1)}, f32[384,768]{1,0:T(8,128)S(1)}, u32[]{:S(2)}, u32[]{:S(2)}) collective-permute-start(f32[384,768]{1,0:T(8,128)S(1)} %copy-done.56), channel_id=1, source_target_pairs={{1,0},{3,2},{5,4},{7,6},{9,8},{11,10},{13,12},{15,14},{17,16},{19,... | collective-permute-start | bytes 3538952 | tf_op jit(solution)/shard_map/ppermute | solution.py:741
  327.0 30.3 %collective-permute-start.41 = (bf16[8,56,768]{2,1,0:T(8,128)(2,1)S(1)}, bf16[8,56,768]{2,1,0:T(8,128)(2,1)S(1)}, u32[]{:S(2)}, u32[]{:S(2)}) collective-permute-start(bf16[8,56,768]{2,1,0:T(8,128)(2,1)S(1)} %slice.857), channel_id=1, source_target_pairs={{0,4},{2,6},{4,0},{6,2},{8,12},{10,14},{12,8},{14,10},{16,20},{18,... | collective-permute-start | bytes 2064392 | tf_op jit(solution)/shard_map/ppermute | solution.py:733
  328.1 29.0 %collective-permute-start.40 = (bf16[8,48,768]{2,1,0:T(8,128)(2,1)S(1)}, bf16[8,48,768]{2,1,0:T(8,128)(2,1)S(1)}, u32[]{:S(2)}, u32[]{:S(2)}) collective-permute-start(bf16[8,48,768]{2,1,0:T(8,128)(2,1)S(1)} %slice_bitcast_fusion.1), channel_id=1, source_target_pairs={{0,2},{2,0},{4,6},{6,4},{8,10},{10,8},{12,14},{14,12},{16,18},{18,... | collective-permute-start | bytes 1769480 | tf_op jit(solution)/shard_map/ppermute | solution.py:733
  328.5 20.3 %collective-permute-start.39 = (bf16[4,48,768]{2,1,0:T(8,128)(2,1)S(1)}, bf16[4,48,768]{2,1,0:T(8,128)(2,1)S(1)}, u32[]{:S(2)}, u32[]{:S(2)}) collective-permute-start(bf16[4,48,768]{2,1,0:T(8,128)(2,1)S(1)} %copy-done.66), channel_id=1, source_target_pairs={{0,2},{2,0},{4,6},{6,4},{8,10},{10,8},{12,14},{14,12},{16,18},{18,... | collective-permute-start | bytes 884744 | tf_op jit(solution)/shard_map/ppermute | solution.py:733
  330.1 20.0 %collective-permute-start.38 = (bf16[4,48,768]{2,1,0:T(8,128)(2,1)S(1)}, bf16[4,48,768]{2,1,0:T(8,128)(2,1)S(1)}, u32[]{:S(2)}, u32[]{:S(2)}) collective-permute-start(bf16[4,48,768]{2,1,0:T(8,128)(2,1)S(1)} %copy-done.65), channel_id=1, source_target_pairs={{0,4},{2,6},{4,0},{6,2},{8,12},{10,14},{12,8},{14,10},{16,20},{18,... | collective-permute-start | bytes 884744 | tf_op jit(solution)/shard_map/ppermute | solution.py:733
  332.2 24.6 %collective-permute-start.52 = (bf16[2,104,768]{2,1,0:T(8,128)(2,1)S(1)}, bf16[2,104,768]{2,1,0:T(8,128)(2,1)S(1)}, u32[]{:S(2)}, u32[]{:S(2)}) collective-permute-start(bf16[2,104,768]{2,1,0:T(8,128)(2,1)S(1)} %pad_maximum_fusion.3), channel_id=1, source_target_pairs={{0,8},{2,10},{4,12},{6,14},{8,0},{10,2},{12,4},{14,6},{16,24},{18,... | collective-permute-start | bytes 958472 | tf_op jit(solution)/shard_map/ppermute | solution.py:733
  365.6 16.7 %collective-permute-start.46 = (bf16[4,56,768]{2,1,0:T(8,128)(2,1)S(1)}, bf16[4,56,768]{2,1,0:T(8,128)(2,1)S(1)}, u32[]{:S(2)}, u32[]{:S(2)}) collective-permute-start(bf16[4,56,768]{2,1,0:T(8,128)(2,1)S(1)} %slice.864), channel_id=1, source_target_pairs={{0,2},{2,0},{4,6},{6,4},{8,10},{10,8},{12,14},{14,12},{16,18},{18,... | collective-permute-start | bytes 1032200 | tf_op jit(solution)/shard_map/ppermute | solution.py:733
  (116 other events, 906.3 us)

commit v3 on v2

v3 whole, which is shorter than its diff:
```python
import functools
import jax
import jax.numpy as jnp
from jax import lax
from jax.experimental import pallas as pl
from jax.experimental.pallas import tpu as pltpu
from jax.sharding import PartitionSpec as P

HEADS = 12
HEAD_DIM = 64
BUCKET = 64
PAIR = 2 * HEAD_DIM
masked_score = -1000000000.0
norm_epsilon = 1e-06
F32 = jnp.float32
BF16 = jnp.bfloat16
CHUNK = 16
FFN_TILE = 512
ATT_UNROLL = 3


def rows_times(left, right):
    return lax.dot_general(left, right, (((1,), (0,)), ((), ())), preferred_element_type=F32)


def rows_times_transposed(left, right):
    return lax.dot_general(left, right, (((1,), (1,)), ((), ())), preferred_element_type=F32)


def transposed_times(left, right):
    return lax.dot_general(left, right, (((0,), (0,)), ((), ())), preferred_element_type=F32)


def slot_facts(block, span_rows, place, meta, micro):
    bucket_ref, count_ref, lengths_ref = meta
    bucket = bucket_ref[micro]
    count = count_ref[micro]

    def length_of(slot):
        return jnp.where(slot < count, lengths_ref[micro, slot], 0)

    if span_rows == 2 * BUCKET:
        return (jnp.full_like(place, block), place, jnp.full_like(place, length_of(block)))
    short = bucket == 0
    first = 3 * block
    slot_short = first + place // BUCKET
    length_short = jnp.where(
        place < BUCKET,
        length_of(first),
        jnp.where(place < 2 * BUCKET, length_of(first + 1), length_of(first + 2)),
    )
    slot = jnp.where(short, slot_short, block)
    inner = jnp.where(short, place % BUCKET, place)
    length = jnp.where(short, length_short, length_of(block))
    return (slot, inner, length)


def fill_masks(span_rows, row_count, meta, micro, bias_ref, valid_ref):
    for block in range(row_count // span_rows):
        row_place = lax.broadcasted_iota(jnp.int32, (span_rows, 1), 0)
        row_slot, row_inner, row_length = slot_facts(block, span_rows, row_place, meta, micro)
        rows = slice(block * span_rows, (block + 1) * span_rows)
        if bias_ref is not None:
            key_place = lax.broadcasted_iota(jnp.int32, (1, span_rows), 1)
            key_slot, key_inner, key_length = slot_facts(block, span_rows, key_place, meta, micro)
            key_tag = jnp.where(key_inner < key_length, key_slot, -1)
            allowed = (row_slot == key_tag) | (row_place == key_place)
            bias_ref[rows, 0:span_rows] = jnp.where(allowed, 0.0, masked_score)
        if valid_ref is not None:
            valid_ref[rows, :] = jnp.where(row_inner < row_length, 1.0, 0.0)


def by_span(meta, micro, body):
    even = meta[0][micro] == 1

    @pl.when(even)
    def _():
        body(2 * BUCKET)

    @pl.when(jnp.logical_not(even))
    def _():
        body(3 * BUCKET)


def attend_forward(span_rows, row_count, q_ref, k_ref, v_ref, bias_ref, c_ref):
    blocks = row_count // span_rows

    def one_pair(pair, carry):
        columns = pl.ds(pl.multiple_of(pair * PAIR, PAIR), PAIR)
        lane = lax.broadcasted_iota(jnp.int32, (span_rows, PAIR), 1)
        first_half = lane < HEAD_DIM
        weights = []
        for block in range(blocks):
            rows = slice(block * span_rows, (block + 1) * span_rows)
            query = q_ref[rows, columns] * jnp.asarray(HEAD_DIM ** (-0.5), BF16)
            keys = k_ref[rows, columns]
            zero = jnp.zeros_like(keys)
            bias = bias_ref[rows, 0:span_rows]
            for mine in (first_half, jnp.logical_not(first_half)):
                scores = rows_times_transposed(query, jnp.where(mine, keys, zero)) + bias
                top = jnp.max(scores, axis=-1, keepdims=True)
                weights.append(jnp.exp(scores - top).astype(BF16))
        for block in range(blocks):
            rows = slice(block * span_rows, (block + 1) * span_rows)
            value = v_ref[rows, columns]
            one = jnp.ones_like(value)
            left = rows_times(weights[2 * block], jnp.where(first_half, value, one))
            right = rows_times(weights[2 * block + 1], jnp.where(first_half, one, value))
            above = jnp.where(first_half, left, right)
            below = pltpu.roll(jnp.where(first_half, right, left), HEAD_DIM, 1)
            c_ref[rows, columns] = (above / below).astype(BF16)
        return carry

    lax.fori_loop(0, HEADS // 2, one_pair, 0, unroll=ATT_UNROLL)


def row_moments(values):
    center = jnp.mean(values, axis=-1, keepdims=True)
    centred = values - center
    spread = jnp.mean(centred * centred, axis=-1, keepdims=True)
    return centred, lax.rsqrt(spread + norm_epsilon)


def over_chunks(row_count, body, rows=CHUNK, group=6):
    def step(index, carry):
        for inner in range(group):
            start = pl.multiple_of(index * (rows * group) + inner * rows, rows)
            body(pl.ds(start, rows))
        return carry

    lax.fori_loop(0, row_count // (rows * group), step, 0)


def over_chunks_with_sums(row_count, body, sums_ref, rows=CHUNK, group=6):
    def step(index, carry):
        total = None
        for inner in range(group):
            start = pl.multiple_of(index * (rows * group) + inner * rows, rows)
            terms = [fold_rows(term) for term in body(pl.ds(start, rows))]
            total = terms if total is None else [a + b for a, b in zip(total, terms)]
        for place, term in enumerate(total):
            sums_ref[place] += term
        return carry

    lax.fori_loop(0, row_count // (rows * group), step, 0)


def fold_rows(values):
    return jnp.sum(values.reshape(values.shape[0] // 8, 8, values.shape[1]), axis=0)


def gelu_with_slope(values):
    cumulative = 0.5 + 0.5 * lax.erf(values * (0.5 ** 0.5))
    density = jnp.exp(values * values * -0.5) * 0.3989422804014327
    return values * cumulative, cumulative + values * density


ANY = pl.BlockSpec(memory_space=pl.ANY)
VM = pl.BlockSpec(memory_space=pltpu.VMEM)
SM = pl.BlockSpec(memory_space=pltpu.SMEM)
VMEM_LIMIT = 63_000 * 1024
S = jax.ShapeDtypeStruct
V = pltpu.VMEM
B_QUERY, B_VALUE, B_MIXER, GAIN_ONE, SHIFT_ONE, B_OUTER, GAIN_TWO, SHIFT_TWO = range(8)
X_BIT, Y_BIT, NEAR_BIT, FAR_BIT = (0, 1, 2, 3)
SMALL_ROWS = 16


class Loads:
    def __init__(self, semaphores):
        self.semaphores = semaphores
        self.copies = {}

    def start(self, name, source, target, other=None, take_other=None):
        semaphore = self.semaphores.at[len(self.copies)]
        copy = pltpu.make_async_copy(source, target, semaphore)
        self.copies[name] = copy
        if other is None:
            copy.start()
            return
        second = pltpu.make_async_copy(other, target, semaphore)

        @pl.when(take_other)
        def _():
            second.start()

        @pl.when(jnp.logical_not(take_other))
        def _():
            copy.start()

    def wait(self, *names):
        for name in names:
            self.copies[name].wait()


class Stores:
    def __init__(self, semaphores):
        self.semaphores = semaphores
        self.copies = []

    def start(self, source, target):
        copy = pltpu.make_async_copy(source, target, self.semaphores.at[len(self.copies)])
        copy.start()
        self.copies.append(copy)

    def wait(self):
        for copy in self.copies:
            copy.wait()


def run_kernel(kernel, outs, out_specs, in_specs, scratch, loads, stores, flops, bytes_moved, name):
    return pl.pallas_call(
        kernel,
        out_shape=outs,
        in_specs=in_specs,
        out_specs=out_specs,
        scratch_shapes=list(scratch) + [pltpu.SemaphoreType.DMA((loads,)), pltpu.SemaphoreType.DMA((stores,))],
        compiler_params=pltpu.CompilerParams(vmem_limit_bytes=VMEM_LIMIT),
        cost_estimate=pl.CostEstimate(flops=flops, bytes_accessed=bytes_moved, transcendentals=0),
        name=name,
    )


def spot_of(near_first, dest):
    relative = jnp.bitwise_xor(dest, lax.axis_index("dp"))

    def bit(index):
        return jnp.bitwise_and(lax.shift_right_logical(relative, index), 1)

    first = lax.axis_index("section") == 0
    lead = jnp.where(first, bit(X_BIT), bit(Y_BIT))
    follow = jnp.where(first, bit(Y_BIT), bit(X_BIT))
    if near_first:
        return bit(NEAR_BIT) * 8 + lead * 4 + follow * 2 + bit(FAR_BIT)
    return lead * 8 + follow * 4 + bit(NEAR_BIT) * 2 + bit(FAR_BIT)


def step_bits(near_first):
    cross = [(X_BIT, Y_BIT), (Y_BIT, X_BIT)]
    if near_first:
        return [(NEAR_BIT, NEAR_BIT)] + cross + [(FAR_BIT, FAR_BIT)]
    return cross + [(NEAR_BIT, NEAR_BIT), (FAR_BIT, FAR_BIT)]


def forward_matrix_loads(loads, hidden_start, weights, others, take_other, targets):
    names = ("wq", "wk", "wv", "wm", "wi", "wo")

    def begin(index):
        other = None if others is None else others[index].at[0]
        loads.start(names[index], weights[index].at[0], targets[index], other, take_other)

    def load(step):
        if step == 0:
            hidden_start()
            for index in range(3):
                begin(index)
            return
        if step == 1:
            loads.wait("h")
        loads.wait(names[step - 1])
        if step <= 3:
            begin(step + 2)

    return load


def forward_body(load, store, meta, micros, vec, bi, outs, refs):
    h_s, wq_s, wk_s, wv_s, wm_s, wi_s, wo_s, qkv_s, c_s, ml_s, a1_s, a2_s, u_s, gp_s, y_s, m_s, f0_s, e0_s, e1_s, bias_s, valid_s = refs
    y_o, qkv_o, c_o, ml_o, a1_o, a2_o, u_o, gp_o = outs
    rows, width = h_s.shape
    hidden = wi_s.shape[1]
    each = rows // len(micros)
    parts = [slice(place * each, (place + 1) * each) for place in range(len(micros))]

    def send(source, target):
        for place, part in enumerate(parts):
            store.start(source.at[part], target.at[place])

    load(0)
    for part, micro in zip(parts, micros):
        by_span(meta, micro, lambda span: fill_masks(span, each, meta, micro, bias_s.at[part], valid_s.at[part]))
    load(1)
    qkv_s[0] = (rows_times(h_s[...], wq_s[...]) + vec(B_QUERY)).astype(BF16)
    load(2)
    qkv_s[1] = rows_times(h_s[...], wk_s[...]).astype(BF16)
    load(3)
    qkv_s[2] = (rows_times(h_s[...], wv_s[...]) + vec(B_VALUE)).astype(BF16)
    for place, part in enumerate(parts):
        store.start(qkv_s.at[:, part], qkv_o.at[place])
    for part, micro in zip(parts, micros):
        by_span(
            meta, micro,
            lambda span: attend_forward(
                span, each, qkv_s.at[0, part], qkv_s.at[1, part], qkv_s.at[2, part], bias_s.at[part], c_s.at[part]
            ),
        )
    send(c_s, c_o)
    load(4)
    f0_s[...] = rows_times(c_s[...], wm_s[...])
    offset_mixer, gain_one, shift_one = (vec(B_MIXER), vec(GAIN_ONE), vec(SHIFT_ONE))

    def first_norm(part):
        total = h_s[part, :].astype(F32) + (f0_s[part, :] + offset_mixer)
        a1_s[part, :] = total
        centred, scale = row_moments(total)
        middle = centred * scale * gain_one + shift_one
        m_s[part, :] = middle
        ml_s[part, :] = middle.astype(BF16)

    over_chunks(rows, first_norm)
    send(a1_s, a1_o)
    send(ml_s, ml_o)
    load(5)
    tile = FFN_TILE
    tiles = hidden // tile

    def project(buffer, which):
        columns = pl.ds(pl.multiple_of(which * tile, tile), tile)
        buffer[...] = rows_times(ml_s[...], wi_s[:, columns])

    def activate(buffer, which):
        columns = pl.ds(pl.multiple_of(which * tile, tile), tile)
        offset = bi(columns)
        for start in range(0, rows, 32):
            part = slice(start, start + 32)
            value, slope = gelu_with_slope(buffer[part, :] + offset)
            u_s[part, columns] = value.astype(BF16)
            gp_s[part, columns] = slope.astype(BF16)

    project(e0_s, 0)

    def two_tiles(index, carry):
        project(e1_s, 2 * index + 1)
        activate(e0_s, 2 * index)
        project(e0_s, jnp.minimum(2 * index + 2, tiles - 1))
        activate(e1_s, 2 * index + 1)
        return carry

    lax.fori_loop(0, tiles // 2, two_tiles, 0)
    send(u_s, u_o)
    send(gp_s, gp_o)
    load(6)
    f0_s[...] = rows_times(u_s[...], wo_s[...])
    offset_outer, gain_two, shift_two = (vec(B_OUTER), vec(GAIN_TWO), vec(SHIFT_TWO))

    def second_norm(part):
        total = m_s[part, :] + (f0_s[part, :] + offset_outer)
        a2_s[part, :] = total
        centred, scale = row_moments(total)
        y_s[part, :] = ((centred * scale * gain_two + shift_two) * valid_s[part, :]).astype(BF16)

    over_chunks(rows, second_norm)
    send(y_s, y_o)
    send(a2_s, a2_o)
    store.wait()


def first_forward_kernel(
    micro_count, bucket, count, lengths, tok, wq, wk, wv, wm, wi, wo, bq, bv, bm, g1, s1, bo, g2, s2, bi,
    y_o, qkv_o, c_o, ml_o, a1_o, a2_o, u_o, gp_o, vec_o, *scratch
):
    *refs, in_sem, out_sem = scratch
    h_s, wq_s, wk_s, wv_s, wm_s, wi_s, wo_s = refs[:7]
    vectors = (bq, bv, bm, g1, s1, bo, g2, s2)
    for place, vector in enumerate(vectors):
        vec_o[place : place + 1, :] = vector[...]

    @pl.when(lax.axis_index("section") == 0)
    def _():
        loads = Loads(in_sem)
        each = h_s.shape[0] // micro_count

        def hidden_start():
            for micro in range(1, micro_count):
                loads.start(("h", micro), tok.at[micro], h_s.at[micro * each : (micro + 1) * each])
            loads.start("h", tok.at[0], h_s.at[0:each])

        inner_load = forward_matrix_loads(
            loads, hidden_start, (wq, wk, wv, wm, wi, wo), None, None, (wq_s, wk_s, wv_s, wm_s, wi_s, wo_s)
        )

        def load(step):
            if step == 1:
                for micro in range(1, micro_count):
                    loads.wait(("h", micro))
            inner_load(step)

        forward_body(
            load, Stores(out_sem), (bucket, count, lengths), tuple(range(micro_count)), lambda place: vectors[place][...],
            lambda columns: bi[:, columns], (y_o, qkv_o, c_o, ml_o, a1_o, a2_o, u_o, gp_o), refs,
        )


def second_forward_kernel(
    bucket, count, lengths, y_own, y_other, wq, wk, wv, wm, wi, wo, xq, xk, xv, xm, xi, xo, vec_own, vec_other, bi_own, bi_other,
    y_o, qkv_o, c_o, ml_o, a1_o, a2_o, u_o, gp_o, *scratch
):
    *refs, in_sem, out_sem = scratch
    h_s, wq_s, wk_s, wv_s, wm_s, wi_s, wo_s = refs[:7]
    section = lax.axis_index("section")
    first = section == 0
    loads = Loads(in_sem)
    load = forward_matrix_loads(
        loads, lambda: loads.start("h", y_other.at[section], h_s, y_own.at[section], first), (wq, wk, wv, wm, wi, wo),
        (xq, xk, xv, xm, xi, xo), first, (wq_s, wk_s, wv_s, wm_s, wi_s, wo_s),
    )

    def vec(place):
        return jnp.where(first, vec_other[place : place + 1, :], vec_own[place : place + 1, :])

    forward_body(
        load, Stores(out_sem), (bucket, count, lengths), (section,), vec,
        lambda columns: jnp.where(first, bi_other[:, columns], bi_own[:, columns]),
        (y_o, qkv_o, c_o, ml_o, a1_o, a2_o, u_o, gp_o), refs,
    )


def forward_shapes(micro_count, each, width, hidden):
    rows = micro_count * each
    flat = (rows, width)
    wide = (rows, hidden)
    square = (width, width)

    def out(*tail):
        return (micro_count,) + tail

    outs = (
        S(out(each, width), BF16), S(out(3, each, width), BF16), S(out(each, width), BF16), S(out(each, width), BF16),
        S(out(each, width), F32), S(out(each, width), F32), S(out(each, hidden), BF16), S(out(each, hidden), BF16),
    )
    scratch = [
        V(flat, BF16), V(square, BF16), V(square, BF16), V(square, BF16), V(square, BF16), V((width, hidden), BF16),
        V((hidden, width), BF16), V((3,) + flat, BF16), V(flat, BF16), V(flat, BF16), V(flat, F32), V(flat, F32),
        V(wide, BF16), V(wide, BF16), V(flat, BF16), V(flat, F32), V(flat, F32), V((rows, FFN_TILE), F32),
        V((rows, FFN_TILE), F32), V((rows, 3 * BUCKET), F32), V((rows, 1), F32),
    ]
    flops = 2 * rows * width * (4 * width + 2 * hidden)
    return outs, scratch, flops


def first_forward(meta, tokens, weights, vectors, bi):
    micro_count, each, width = tokens.shape
    outs, scratch, flops = forward_shapes(micro_count, each, width, bi.shape[1])
    return run_kernel(
        functools.partial(first_forward_kernel, micro_count), outs + (S((8, width), F32),), [ANY] * 8 + [VM],
        [SM] * 3 + [ANY] * 7 + [VM] * 9, scratch, 6 + micro_count, 8 * micro_count, flops, 40_000_000, "first_forward",
    )(*meta, tokens, *weights, *vectors, bi)


def second_forward(meta, y_own, y_other, weights, others, vec_own, vec_other, bi_own, bi_other):
    _, each, width = y_own.shape
    outs, scratch, flops = forward_shapes(1, each, width, bi_own.shape[1])
    return run_kernel(
        second_forward_kernel, outs, [ANY] * 8, [SM] * 3 + [ANY] * 14 + [VM] * 4, scratch, 7, 8, flops, 25_000_000,
        "second_forward",
    )(*meta, y_own, y_other, *weights, *others, vec_own, vec_other, bi_own, bi_other)


def norm_backward(grad, total, gain):
    centred, scale = row_moments(total)
    unit = centred * scale
    spread = grad * gain
    first = jnp.mean(spread, axis=-1, keepdims=True)
    second = jnp.mean(spread * unit, axis=-1, keepdims=True)
    return (spread - first - unit * second) * scale, grad * unit


def layer_of(layer):
    return lax.axis_index("section") != layer


def taken(layer, own, other, place):
    return jnp.where(layer_of(layer), other[place : place + 1, :], own[place : place + 1, :])


def kept_of(layer, own, other):
    if layer == 1:
        return own.at[0], None
    section = lax.axis_index("section")
    return own.at[section], other.at[section]


def feed_kernel(
    layer, bucket, count, lengths, g, a2, a2_x, gp, gp_x, a1, a1_x, wo, wo_x, wi, wi_x, wm, wm_x, vec_own, vec_other,
    dz_home_o, dz_away_o, df_home_o, df_away_o, da1_o, da_o, dc_o, small_o,
    g_s, a2_s, gp_s, a1_s, wo_s, wi_s, wm_s, da2_s, dz_s, df_s, dm_s, da1_s, da_s, dc_s, e0_s, e1_s, valid_s, sums_s, wide_s, in_sem, out_sem,
):
    section = lax.axis_index("section")
    rows, width = a2_s.shape
    hidden = df_s.shape[1]
    second = section == 1
    loads = Loads(in_sem)
    store = Stores(out_sem)
    loads.start("g", g.at[section] if layer == 1 else g, g_s)
    loads.start("a2", kept_of(layer, a2, a2_x)[0], a2_s, kept_of(layer, a2, a2_x)[1], second)
    loads.start("wo", wo.at[0], wo_s, wo_x.at[0], layer_of(layer))
    meta = (bucket, count, lengths)
    by_span(meta, section, lambda span: fill_masks(span, rows, meta, section, None, valid_s))
    sums_s[...] = jnp.zeros_like(sums_s)
    gain_two = taken(layer, vec_own, vec_other, GAIN_TWO)
    gain_one = taken(layer, vec_own, vec_other, GAIN_ONE)
    loads.wait("g", "a2")
    loads.start("gp", kept_of(layer, gp, gp_x)[0], gp_s, kept_of(layer, gp, gp_x)[1], second)
    loads.start("wi", wi.at[0], wi_s, wi_x.at[0], layer_of(layer))

    def second_norm(part):
        grad = g_s[part, :].astype(F32) * valid_s[part, :]
        moved, gained = norm_backward(grad, a2_s[part, :], gain_two)
        da2_s[part, :] = moved
        low = moved.astype(BF16)
        dz_s[part, :] = low
        return gained, grad, low.astype(F32)

    over_chunks_with_sums(rows, second_norm, sums_s.at[0:3])
    half = width // 2
    store.start(dz_s.at[:, pl.ds(pl.multiple_of(section * half, half), half)], dz_home_o)
    store.start(dz_s.at[:, pl.ds(pl.multiple_of((1 - section) * half, half), half)], dz_away_o)
    tile = FFN_TILE
    tiles = hidden // tile

    def project(buffer, which):
        columns = pl.ds(pl.multiple_of(which * tile, tile), tile)
        buffer[...] = rows_times_transposed(dz_s[...], wo_s[columns, :])

    def slope(buffer, which):
        columns = pl.ds(pl.multiple_of(which * tile, tile), tile)
        total = None
        for start in range(0, rows, 32):
            part = slice(start, start + 32)
            low_part = (buffer[part, :] * gp_s[part, columns].astype(F32)).astype(BF16)
            df_s[part, columns] = low_part
            term = fold_rows(low_part.astype(F32))
            total = term if total is None else total + term
        wide_s[:, columns] = total

    loads.wait("wo")
    loads.start("a1", kept_of(layer, a1, a1_x)[0], a1_s, kept_of(layer, a1, a1_x)[1], second)
    loads.start("wm", wm.at[0], wm_s, wm_x.at[0], layer_of(layer))
    project(e0_s, 0)
    loads.wait("gp")

    def two_tiles(index, carry):
        project(e1_s, 2 * index + 1)
        slope(e0_s, 2 * index)
        project(e0_s, jnp.minimum(2 * index + 2, tiles - 1))
        slope(e1_s, 2 * index + 1)
        return carry

    lax.fori_loop(0, tiles // 2, two_tiles, 0)
    half = hidden // 2
    store.start(df_s.at[:, pl.ds(pl.multiple_of(section * half, half), half)], df_home_o)
    store.start(df_s.at[:, pl.ds(pl.multiple_of((1 - section) * half, half), half)], df_away_o)
    loads.wait("wi")
    dm_s[...] = rows_times_transposed(df_s[...], wi_s[...])
    loads.wait("a1")

    def first_norm(part):
        grad = dm_s[part, :] + da2_s[part, :]
        moved, gained = norm_backward(grad, a1_s[part, :], gain_one)
        da1_s[part, :] = moved
        low_part = moved.astype(BF16)
        da_s[part, :] = low_part
        return gained, grad, low_part.astype(F32)

    over_chunks_with_sums(rows, first_norm, sums_s.at[3:6])
    store.start(da1_s, da1_o)
    store.start(da_s, da_o)
    for index in range(6):
        small_o[index : index + 1, :] = jnp.sum(sums_s[index], axis=0, keepdims=True)
    inner_sum = jnp.sum(wide_s[...], axis=0, keepdims=True)
    for index in range(hidden // width):
        small_o[8 + index : 9 + index, :] = inner_sum[:, index * width : (index + 1) * width]
    loads.wait("wm")
    dc_s[...] = rows_times_transposed(da_s[...], wm_s[...]).astype(BF16)
    store.start(dc_s, dc_o)
    store.wait()


def feed_gradient(layer, meta, g, kept, kept_x, weights, others, vec_own, vec_other):
    a1, a2, gp = (kept[name] for name in ("a1", "a2", "gp"))
    a1_x, a2_x, gp_x = (kept_x[name] for name in ("a1", "a2", "gp"))
    rows, width = a1.shape[1:]
    hidden = gp.shape[2]
    flat = (rows, width)
    half = S((rows, width // 2), BF16)
    half_wide = S((rows, hidden // 2), BF16)
    return run_kernel(
        functools.partial(feed_kernel, layer),
        (half, half, half_wide, half_wide, S(flat, F32), S(flat, BF16), S(flat, BF16), S((SMALL_ROWS, width), F32)),
        [ANY] * 7 + [VM], [SM] * 3 + [ANY] * 13 + [VM] * 2,
        [
            V(flat, g.dtype), V(flat, F32), V((rows, hidden), BF16), V(flat, F32), V((hidden, width), BF16), V((width, hidden), BF16),
            V((width, width), BF16), V(flat, F32), V(flat, BF16), V((rows, hidden), BF16), V(flat, F32), V(flat, F32), V(flat, BF16),
            V(flat, BF16), V((rows, FFN_TILE), F32), V((rows, FFN_TILE), F32), V((rows, 1), F32), V((6, 8, width), F32),
            V((8, hidden), F32),
        ],
        7, 7, 2 * rows * width * (2 * hidden + width), 25_000_000, "feed_gradient",
    )(*meta, g, a2, a2_x, gp, gp_x, a1, a1_x, weights[5], others[5], weights[4], others[4], weights[3], others[3], vec_own, vec_other)


def attend_backward(span_rows, row_count, q_ref, k_ref, v_ref, dc_ref, bias_ref, dq_ref, dk_ref, dv_ref):
    blocks = row_count // span_rows
    scale = HEAD_DIM ** (-0.5)

    def one_pair(pair, carry):
        columns = pl.ds(pl.multiple_of(pair * PAIR, PAIR), PAIR)
        lane = lax.broadcasted_iota(jnp.int32, (span_rows, PAIR), 1)
        halves = (lane < HEAD_DIM, lane >= HEAD_DIM)
        for block in range(blocks):
            rows = slice(block * span_rows, (block + 1) * span_rows)
            query = q_ref[rows, columns] * jnp.asarray(scale, BF16)
            keys = k_ref[rows, columns]
            value = v_ref[rows, columns]
            grad = dc_ref[rows, columns]
            zero = jnp.zeros_like(keys)
            bias = bias_ref[rows, 0:span_rows]
            dq = dk = dv = None
            for mine in halves:
                keys_own = jnp.where(mine, keys, zero)
                scores = rows_times_transposed(query, keys_own) + bias
                grad_part = rows_times_transposed(grad, jnp.where(mine, value, zero))
                top = jnp.max(scores, axis=-1, keepdims=True)
                weight = jnp.exp(scores - top)
                part = weight * (1.0 / jnp.sum(weight, axis=-1, keepdims=True))
                mean = jnp.sum(grad_part * part, axis=-1, keepdims=True)
                grad_scores = (part * (grad_part - mean)).astype(BF16)
                terms = (
                    rows_times(grad_scores, keys_own),
                    transposed_times(grad_scores, jnp.where(mine, query, zero)),
                    transposed_times(part.astype(BF16), jnp.where(mine, grad, zero)),
                )
                if dq is None:
                    dq, dk, dv = terms
                else:
                    dq, dk, dv = (dq + terms[0], dk + terms[1], dv + terms[2])
            dq_ref[rows, columns] = (dq * scale).astype(BF16)
            dk_ref[rows, columns] = dk.astype(BF16)
            dv_ref[rows, columns] = dv.astype(BF16)
        return carry

    lax.fori_loop(0, HEADS // 2, one_pair, 0)


def attend_kernel(
    layer, bucket, count, lengths, qkv, qkv_x, dc, da, da1, wq, wk, wv, xq, xk, xv,
    dh_o, dlow_o, home_o, away_o, small_o,
    qkv_s, dc_s, da_s, dh_s, dlow_s, wq_s, wk_s, wv_s, dq_s, dk_s, dv_s, bias_s, sums_s, in_sem, out_sem,
):
    section = lax.axis_index("section")
    rows, width = dc_s.shape
    second = section == 1
    loads = Loads(in_sem)
    store = Stores(out_sem)
    loads.start("qkv", kept_of(layer, qkv, qkv_x)[0], qkv_s, kept_of(layer, qkv, qkv_x)[1], second)
    loads.start("dc", dc, dc_s)
    meta = (bucket, count, lengths)
    by_span(meta, section, lambda span: fill_masks(span, rows, meta, section, bias_s, None))
    loads.wait("qkv", "dc")
    loads.start("da", da, da_s)
    loads.start("da1", da1, dh_s)
    for name, own, received, target in (("wq", wq, xq, wq_s), ("wk", wk, xk, wk_s), ("wv", wv, xv, wv_s)):
        loads.start(name, own.at[0], target, received.at[0], layer_of(layer))
    by_span(
        meta, section,
        lambda span: attend_backward(span, rows, qkv_s.at[0], qkv_s.at[1], qkv_s.at[2], dc_s, bias_s, dq_s, dk_s, dv_s),
    )
    loads.wait("da")
    pairs = ((dq_s, dk_s), (dv_s, da_s))
    for core in range(2):
        @pl.when(section == core)
        def _(core=core):
            for place in range(2):
                pltpu.make_async_copy(pairs[core][place], home_o.at[place], out_sem.at[place]).start()
                pltpu.make_async_copy(pairs[1 - core][place], away_o.at[place], out_sem.at[2 + place]).start()
    loads.wait("da1", "wq", "wk", "wv")
    dh_s[...] += rows_times_transposed(dq_s[...], wq_s[...])
    dh_s[...] += rows_times_transposed(dk_s[...], wk_s[...])
    dh_s[...] += rows_times_transposed(dv_s[...], wv_s[...])
    sums_s[...] = jnp.zeros_like(sums_s)

    def finish(part):
        dlow_s[part, :] = dh_s[part, :].astype(BF16)
        return dq_s[part, :].astype(F32), dv_s[part, :].astype(F32)

    over_chunks_with_sums(rows, finish, sums_s)
    last = [
        pltpu.make_async_copy(dh_s, dh_o, out_sem.at[4]),
        pltpu.make_async_copy(dlow_s, dlow_o, out_sem.at[5]),
    ]
    for copy in last:
        copy.start()
    for index in range(2):
        small_o[index : index + 1, :] = jnp.sum(sums_s[index], axis=0, keepdims=True)
    for place in range(2):
        pltpu.make_async_copy(pairs[0][place], home_o.at[place], out_sem.at[place]).wait()
        pltpu.make_async_copy(pairs[1][place], away_o.at[place], out_sem.at[2 + place]).wait()
    for copy in last:
        copy.wait()


def attend_gradient(layer, meta, kept, kept_x, dc, da, da1, weights, others):
    rows, width = da1.shape
    flat = (rows, width)
    square = (width, width)
    return run_kernel(
        functools.partial(attend_kernel, layer),
        (S(flat, F32), S(flat, BF16), S((2,) + flat, BF16), S((2,) + flat, BF16), S((8, width), F32)),
        [ANY] * 4 + [VM], [SM] * 3 + [ANY] * 11,
        [V((3,) + flat, BF16), V(flat, BF16), V(flat, BF16), V(flat, F32), V(flat, BF16)] + [V(square, BF16)] * 3 + [V(flat, BF16)] * 3
        + [V((rows, 3 * BUCKET), F32), V((2, 8, width), F32)],
        7, 6, 6 * rows * width * width, 15_000_000, "attend_gradient",
    )(*meta, kept["qkv"], kept_x["qkv"], dc, da, da1, *weights[:3], *others[:3])


def by_owner(loads, name, own, other, target):
    rows = target.shape[0] // 2
    section = lax.axis_index("section")
    loads.start((name, 0), own, target.at[pl.ds(pl.multiple_of(section * rows, rows), rows)])
    loads.start((name, 1), other, target.at[pl.ds(pl.multiple_of((1 - section) * rows, rows), rows)])


def both_micros(layer, loads, name, own, other, target):
    if layer == 1:
        by_owner(loads, name, own.at[0], other.at[0], target)
        return
    rows = target.shape[0] // 2
    for micro in range(2):
        part = target.at[micro * rows : (micro + 1) * rows]
        loads.start((name, micro), own.at[micro], part, other.at[micro], lax.axis_index("section") == 1)


def put_rows(target, near_first, value, at_row, at_lane, dest):
    spot = 0 if target.shape[0] == 1 else spot_of(near_first, dest)
    rows, lanes = value.shape
    target[spot, at_row : at_row + rows, at_lane : at_lane + lanes] = value.astype(BF16)


def feed_weights_kernel(
    layer, near_first, u, u_x, ml, ml_x, dz, dz_x, df, df_x,
    send_o, keep_o,
    u_s, ml_s, dz_s, df_s, w_s, in_sem, out_sem,
):
    hidden = u_s.shape[1]
    width = ml_s.shape[1]
    rows = dz.shape[0]
    spots = w_s.shape[0]
    loads = Loads(in_sem)
    store = Stores(out_sem)
    by_owner(loads, "dz", dz, dz_x, dz_s)
    both_micros(layer, loads, "u", u, u_x, u_s)
    loads.wait(("dz", 0), ("dz", 1), ("u", 0), ("u", 1))
    both_micros(layer, loads, "ml", ml, ml_x, ml_s)
    by_owner(loads, "df", df, df_x, df_s)
    half_rows = hidden // spots // 2
    tile = min(width, half_rows * 2) if spots == 1 else width
    for index in range(hidden // tile):
        product = transposed_times(u_s[:, index * tile : (index + 1) * tile], dz_s[...])
        block = min(half_rows, tile)
        for inner in range(tile // block):
            row = index * tile + inner * block
            dest, offset = divmod(row, 2 * half_rows)
            side, at_row = divmod(offset, half_rows)
            put_rows(w_s, near_first, product[inner * block : (inner + 1) * block, :], at_row, side * (width // 2), dest)
    loads.wait(("ml", 0), ("ml", 1), ("df", 0), ("df", 1))
    height = width // spots
    for side in range(2):
        product = transposed_times(ml_s[...], df_s[:, side * width : (side + 1) * width])
        for dest in range(spots):
            put_rows(w_s, near_first, product[dest * height : (dest + 1) * height, :], half_rows + side * height, 0, dest)
    split = spots // 2
    if spots > 1:
        store.start(w_s.at[split:spots], send_o)
        store.start(w_s.at[0:split], keep_o)
    else:
        store.start(w_s, send_o)
        store.start(w_s, keep_o)
    store.wait()


def unit_outs(spots, rows, width):
    half = S((max(spots // 2, 1), rows, width), BF16)
    return half, half


def feed_weights(layer, near_first, spots, kept, kept_x, dz, dz_x, df, df_x):
    u, u_x, ml, ml_x = (kept["u"], kept_x["u"], kept["ml"], kept_x["ml"])
    rows, width = ml.shape[1:]
    hidden = u.shape[2]
    total = hidden // spots // 2 + 2 * (width // spots)
    return run_kernel(
        functools.partial(feed_weights_kernel, layer, near_first), unit_outs(spots, total, width), [ANY] * 2, [ANY] * 8,
        [
            V((2 * rows, hidden), BF16), V((2 * rows, width), BF16), V((2 * rows, width // 2), BF16), V((2 * rows, hidden // 2), BF16),
            V((spots, total, width), BF16),
        ],
        8, 2, 4 * rows * width * hidden, 18_000_000, "feed_weights",
    )(u, u_x, ml, ml_x, dz, dz_x, df, df_x)


def attend_weights_kernel(
    layer, near_first, h, h_x, c, c_x, grads, grads_x, small_one, small_one_x, small_two, small_two_x,
    send_o, keep_o,
    left_s, right_s, w_s, in_sem, out_sem,
):
    section = lax.axis_index("section")
    second = section == 1
    rows, width = grads.shape[1:]
    spots = w_s.shape[0]
    loads = Loads(in_sem)
    store = Stores(out_sem)
    for micro in range(2):
        part = slice(micro * rows, (micro + 1) * rows)
        loads.start(("h", micro), h.at[micro], left_s.at[0, part], h_x.at[micro], second)
    by_owner(loads, "g", grads.at[0], grads_x.at[0], right_s.at[0])
    if layer == 0:
        for micro in range(2):
            part = slice(micro * rows, (micro + 1) * rows)
            loads.start(("c", micro), h.at[micro], left_s.at[1, part], c_x.at[micro], second)
    else:
        for place, (plain, context) in enumerate(((h, c), (h_x, c_x))):
            micro = section if place == 0 else 1 - section
            part = left_s.at[1, pl.ds(pl.multiple_of(micro * rows, rows), rows)]
            loads.start(("c", place), h.at[micro], part, context.at[0], second)
    by_owner(loads, "f", grads.at[1], grads_x.at[1], right_s.at[1])
    height = width // spots
    small = jnp.concatenate([small_one[0:6, :] + small_one_x[0:6, :], small_two[0:2, :] + small_two_x[0:2, :], small_one[8:16, :] + small_one_x[8:16, :]], axis=0)
    low = small.astype(BF16)
    for spot in range(spots):
        w_s[spot, 2 * height : 2 * height + SMALL_ROWS, :] = low
    for side, name in enumerate(("h", "c")):
        grad_name = ("g", "f")[side]
        loads.wait((name, 0), (name, 1), (grad_name, 0), (grad_name, 1))
        product = transposed_times(left_s[side], right_s[side])
        for dest in range(spots):
            put_rows(w_s, near_first, product[dest * height : (dest + 1) * height, :], side * height, 0, dest)
    split = spots // 2
    if spots > 1:
        store.start(w_s.at[split:spots], send_o)
        store.start(w_s.at[0:split], keep_o)
    else:
        store.start(w_s, send_o)
        store.start(w_s, keep_o)
    store.wait()


def attend_weights(layer, near_first, spots, h, h_x, c, c_x, grads, grads_x, smalls):
    rows, width = grads.shape[1:]
    total = 2 * (width // spots) + SMALL_ROWS
    return run_kernel(
        functools.partial(attend_weights_kernel, layer, near_first), unit_outs(spots, total, width), [ANY] * 2, [ANY] * 6 + [VM] * 4,
        [V((2, 2 * rows, width), BF16), V((2, 2 * rows, width), BF16), V((spots, total, width), BF16)],
        8, 2, 8 * rows * width * width, 10_000_000, "attend_weights",
    )(h, h_x, c, c_x, grads, grads_x, *smalls)


def add_kernel(count, *refs):
    keeps = refs[0:count]
    parts = refs[count : 2 * count]
    outs = list(refs[2 * count :])
    for keep, part in zip(keeps, parts):
        spots, rows, _ = keep.shape
        if spots == 1:
            target = outs.pop(0)
            target[...] = keep[0].astype(F32) + part[0].astype(F32)
            continue
        halves = (outs.pop(0), outs.pop(0))
        for half in range(2):
            base = (1 - half) * (spots // 2)

            def one(spot, carry):
                halves[half][spot] = (keep[base + spot].astype(F32) + part[base + spot].astype(F32)).astype(BF16)
                return carry

            lax.fori_loop(0, spots // 2, one, 0)


def add_arrived(pairs):
    outs = []
    for keep, _ in pairs:
        spots, rows, width = keep.shape
        if spots == 1:
            outs.append(S((rows, width), F32))
        else:
            outs.extend([S((spots // 2, rows, width), BF16)] * 2)
    moved = sum(3 * keep.size for keep, _ in pairs)
    results = list(
        pl.pallas_call(
            functools.partial(add_kernel, len(pairs)),
            out_shape=tuple(outs),
            in_specs=[VM] * (2 * len(pairs)),
            out_specs=(VM,) * len(outs),
            compiler_params=pltpu.CompilerParams(vmem_limit_bytes=ADD_LIMIT),
            cost_estimate=pl.CostEstimate(flops=moved, bytes_accessed=2 * moved, transcendentals=0),
            name="add_arrived",
        )(*[keep for keep, _ in pairs], *[part for _, part in pairs])
    )
    taken_back = []
    for keep, _ in pairs:
        if keep.shape[0] == 1:
            taken_back.append((results.pop(0),))
        else:
            taken_back.append((results.pop(0), results.pop(0)))
    return taken_back


ADD_LIMIT = 40_000 * 1024


def finish_kernel(
    feed_first, feed_second, attend_first, attend_second, feed_back_first, feed_back_second, attend_back_first, attend_back_second,
    q_o, k_o, v_o, m_o, i_o, o_o, small_o, wide_o,
):
    section = lax.axis_index("section")
    groups = lax.axis_size("dp")
    me = lax.axis_index("dp")
    height, width = q_o.shape
    half_rows = o_o.shape[0] // 2
    hidden = i_o.shape[1]
    for core in range(2):
        @pl.when(section == core)
        def _(core=core):
            mine = (feed_first, attend_first) if core == 0 else (feed_second, attend_second)
            back = (feed_back_first, attend_back_first) if core == 0 else (feed_back_second, attend_back_second)
            sides = (mine, back) if core == 0 else (back, mine)
            for side, (feed, attend) in enumerate(sides):
                for part in range(2):
                    o_o[part * half_rows : (part + 1) * half_rows, side * (width // 2) : (side + 1) * (width // 2)] = feed[
                        0:half_rows, part * (width // 2) : (part + 1) * (width // 2)
                    ]
                    i_o[:, (2 * side + part) * width : (2 * side + part + 1) * width] = feed[
                        half_rows + part * height : half_rows + (part + 1) * height, :
                    ]
            q_o[...] = sides[0][1][0:height, :]
            k_o[...] = sides[0][1][height : 2 * height, :]
            v_o[...] = sides[1][1][0:height, :]
            m_o[...] = sides[1][1][height : 2 * height, :]
            lines = mine[1][2 * height : 2 * height + SMALL_ROWS, :]
            small_o[...] = pltpu.roll(lines[0:8, :], jnp.bitwise_and(width - me * height, 1023) % width, 1)
            span = hidden // groups
            row = me // (width // span)
            pick = lax.broadcasted_iota(jnp.int32, (8, width), 0) == row
            chosen = jnp.sum(jnp.where(pick, lines[8:16, :], 0.0), axis=0, keepdims=True)
            offset = (me % (width // span)) * span
            wide_o[...] = pltpu.roll(jnp.broadcast_to(chosen, (8, width)), (width - offset) % width, 1)


def finish(groups, width, hidden, results):
    height = width // groups
    square = S((height, width), F32)
    return pl.pallas_call(
        finish_kernel,
        out_shape=(square, square, square, square, S((height, hidden), F32), S((hidden // groups, width), F32), S((8, width), F32), S((8, width), F32)),
        in_specs=[VM] * 8,
        out_specs=(VM,) * 8,
        compiler_params=pltpu.CompilerParams(vmem_limit_bytes=ADD_LIMIT),
        name="finish_gradients",
    )(*results)


def exchange(value, bits):
    groups = lax.axis_size("dp")
    pairs = [(2 * group + core, 2 * (group ^ (1 << bits[core])) + core) for group in range(groups) for core in range(2)]
    return lax.ppermute(value, ("dp", "section"), pairs)


def swap(value):
    return lax.ppermute(value, "section", [(0, 1), (1, 0)])


def hand_over(value, source):
    return lax.ppermute(value, "section", [(source, 1 - source)])


NAMES = ("qkv", "c", "ml", "a1", "a2", "u", "gp")
F1, T1, F0, T0 = (("f", 1), ("t", 1), ("f", 0), ("t", 0))
NEAR_FIRST = {F1: False, T1: True, F0: False, T0: True}
SCHEDULE = (
    (),
    (),
    (),
    (),
    (),
    (F1, T1),
    (),
    (F1, T1),
    (F1, T1),
    (F0,),
    (F1, T1, T0),
    (F0, T0),
    (F0, T0),
    (F0, T0),
)


def per_device(
    tokens, cotangent, bucket, batch_size, lengths, query_weight, query_offset, keys_weight, value_weight, value_offset,
    mixer_weight, mixer_offset, first_gain, first_shift, inner_weight, inner_offset, outer_weight, outer_offset,
    second_gain, second_shift,
):
    section = lax.axis_index("section")
    groups = lax.axis_size("dp")
    width = tokens.shape[2]
    hidden = inner_offset.shape[1]
    hypercube = groups == 16
    spots = groups if hypercube else 1
    first = section == 0
    meta = (bucket, batch_size, lengths)
    weights = (query_weight, keys_weight, value_weight, mixer_weight, inner_weight, outer_weight)
    vectors = (query_offset, value_offset, mixer_offset, first_gain, first_shift, outer_offset, second_gain, second_shift)
    others = tuple(swap(weight) for weight in weights)
    bi_other = swap(inner_offset)
    y_first, *kept_first, vec_own = first_forward(meta, tokens, weights, vectors, inner_offset)
    vec_other = swap(vec_own)
    y_x = hand_over(y_first, 0)
    y_second, *kept_second = second_forward(meta, y_first, y_x, weights, others, vec_own, vec_other, inner_offset, bi_other)
    kept = {0: dict(zip(NAMES, kept_first)), 1: dict(zip(NAMES, kept_second))}
    kept_x = {0: {name: hand_over(value, 0) for name, value in kept[0].items()}, 1: dict(kept[1])}
    for name in ("u", "ml", "c"):
        kept_x[1][name] = swap(kept[1][name])
    entries = {1: (y_first, y_x), 0: (tokens, tokens)}
    y_last_x = hand_over(y_second, 0)
    moving = {}
    results = {}

    def boundary(value, names):
        if not names or not hypercube:
            return value
        added = add_arrived([(moving[name][0], moving[name][1]) for name in names])
        held = lax.optimization_barrier((value, added))
        for name, parts in zip(names, held[1]):
            if len(parts) == 1:
                results[name] = parts[0]
            else:
                step = moving[name][2] + 1
                moving[name] = (parts[1], exchange(parts[0], step_bits(NEAR_FIRST[name])[step]), step)
        return held[0]

    def begin(name, send, keep):
        if hypercube:
            moving[name] = (keep, exchange(send, step_bits(NEAR_FIRST[name])[0]), 0)
        else:
            moving[name] = send

    grad = cotangent
    dh = {}
    for layer in (1, 0):
        turn = 4 * (1 - layer)
        grad = boundary(grad, SCHEDULE[turn])
        dz, dz_away, df, df_away, da1, da, dc, small_one = feed_gradient(
            layer, meta, grad, kept[layer], kept_x[layer], weights, others, vec_own, vec_other
        )
        dz_x, df_x, small_one_x = (swap(dz_away), swap(df_away), swap(small_one))
        dz = boundary(dz, SCHEDULE[turn + 1])
        begin(("f", layer), *feed_weights(layer, NEAR_FIRST["f", layer], spots, kept[layer], kept_x[layer], dz, dz_x, df, df_x))
        dc = boundary(lax.optimization_barrier((dc, moving["f", layer][0]))[0], SCHEDULE[turn + 2])
        dh[layer], grad, grads, grads_away, small_two = attend_gradient(
            layer, meta, kept[layer], kept_x[layer], dc, da, da1, weights, others
        )
        grads_x, small_two_x = (swap(grads_away), swap(small_two))
        grads = boundary(grads, SCHEDULE[turn + 3])
        begin(
            ("t", layer),
            *attend_weights(
                layer, NEAR_FIRST["t", layer], spots, *entries[layer], kept[layer]["c"], kept_x[layer]["c"], grads, grads_x,
                (small_one, small_one_x, small_two, small_two_x),
            ),
        )
        grad = lax.optimization_barrier((grad, moving["t", layer][0]))[0]
    dh_x1 = hand_over(dh[1], 0)
    dh_x0 = hand_over(dh[0], 1)
    layer_out = jnp.stack([jnp.where(first, y_first[0], y_last_x[0]), jnp.where(first, y_first[1], y_second[0])])
    input_grad = jnp.stack([jnp.where(first, dh[0], dh_x1), jnp.where(first, dh_x0, dh[1])])
    if hypercube:
        anchor = jnp.zeros((), F32)
        for names in SCHEDULE[8:]:
            anchor = boundary(anchor, names)
        back = {name: hand_over(results[name], 1 - name[1]) for name in (F1, T1, F0, T0)}
        done = finish(
            groups, width, hidden,
            (results[F0], results[F1], results[T0], results[T1], back[F0], back[F1], back[T0], back[T1]),
        )
        query_grad, keys_grad, value_grad, mixer_grad, inner_grad, outer_grad, lines, wide_line = done
        height = width // groups
        small = [lines[index, :height] for index in range(8)]
        small_wide = wide_line[0, : hidden // groups]
    else:
        def scatter(value):
            return lax.psum_scatter(value, "dp", scatter_dimension=0, tiled=True).astype(F32)

        found = []
        for layer in (1, 0):
            feed = moving["f", layer][0]
            attend = moving["t", layer][0]
            half_rows = hidden // 2
            outer_half = jnp.concatenate([feed[:half_rows, : width // 2], feed[:half_rows, width // 2 :]], axis=0)
            parts = [scatter(outer_half), scatter(feed[half_rows : half_rows + width]), scatter(feed[half_rows + width :])]
            parts += [scatter(attend[:width]), scatter(attend[width : 2 * width])]
            lines = attend[2 * width :].astype(F32)
            parts += [scatter(lines[index]) for index in range(8)] + [scatter(lines[8:12].reshape(-1))]
            found.append(parts)
        mine = [jnp.where(first, b, a) for a, b in zip(*found)]
        back = [swap(jnp.where(first, a, b)) for a, b in zip(found[0][:5], found[1][:5])]
        low = [jnp.where(first, a, b) for a, b in zip(mine, back)]
        high = [jnp.where(first, b, a) for a, b in zip(mine, back)]
        outer_grad = jnp.concatenate([low[0], high[0]], axis=1)
        inner_grad = jnp.concatenate([low[1], low[2], high[1], high[2]], axis=1)
        query_grad, keys_grad, value_grad, mixer_grad = (low[3], low[4], high[3], high[4])
        small, small_wide = (mine[5:13], mine[13])
    second_gain_grad, second_shift_grad, outer_offset_grad, first_gain_grad, first_shift_grad, mixer_offset_grad = small[:6]
    outputs = (
        layer_out, input_grad, query_grad, small[6], keys_grad, value_grad, small[7], mixer_grad, mixer_offset_grad,
        first_gain_grad, first_shift_grad, inner_grad, small_wide, outer_grad, outer_offset_grad, second_gain_grad,
        second_shift_grad,
    )
    return tuple(piece[None] for piece in outputs)


def solution(mesh):
    matrix = P("section", None, None)
    vector = P("section", None)
    in_specs = (
        P("dp", None, None), P("dp", None, None), P("dp"), P("dp"), P("dp", None), matrix, vector, matrix, matrix, vector,
        matrix, vector, vector, vector, matrix, vector, matrix, vector, vector, vector,
    )
    rows = P("section", "dp", None, None)
    grad = P("section", "dp", None)
    small = P("section", "dp")
    out_specs = (rows, rows, grad, small, grad, grad, small, grad, small, small, small, grad, small, grad, small, small, small)
    return jax.shard_map(per_device, mesh=mesh, in_specs=in_specs, out_specs=out_specs, check_vma=False)
```

time: 422 us -> 391 us (0.927)
  other arithmetic: 43.2 us -> 5.65 us
  waiting for transfers between devices: 122 us -> 141 us
  local copies, waits for them, and re-layouts: 26.6 us -> 14.6 us
    another operation x48 -> x0, other arithmetic: 24.4 us -> none
    ppermute x7 -> x15, starting transfers between devices: 17.6 us -> 40 us  [hand_over(): return lax.ppermute(value, 'section', [(source, 1 - source)])]
    ppermute x36 -> x16, starting transfers between devices: 39.2 us -> 21.7 us  [exchange(): return lax.ppermute(value, ('dp', 'section'), pairs)]
    ppermute x19 -> x21, waiting for transfers between devices: 7.72 us -> 19.6 us  [swap(): return lax.ppermute(value, 'section', [(0, 1), (1, 0)])]
    slice x49 -> x2, local copies, waits for them, and re-layouts: 11.1 us -> 1.1 us  [the longest x1 0.56 us: per_device(): small_wide = wide_line[0, :hidden // groups]]
    ppermute x36 -> x16, waiting for transfers between devices: 113 us -> 122 us  [exchange(): return lax.ppermute(value, ('dp', 'section'), pairs)]
    convert_element_type x10 -> x0, local copies, waits for them, and re-layouts: 7.89 us -> none  [arrive(): self.sends = [total[half:].astype(BF16) for total in totals]]
    unnamed x154 -> x72, local copies, waits for them, and re-layouts: 6.5 us -> 13.5 us
  transfers between devices with their start and end apart: 62 -> 52, of which waited for: 24 -> 17; matrix products, arithmetic and copies ran while one was open for 14% -> 1% of each run, Pallas kernels for 31% -> 35%
where the time goes in v3:
time: 391 us; the launch traced here: 384 us
  Pallas kernels  154 us (39%)
  waiting for transfers between devices  141 us (36%)
  starting transfers between devices  66.8 us (17%)
  local copies, waits for them, and re-layouts  14.6 us (4%)
  other arithmetic  5.65 us (1%)
    ppermute x16, waiting for transfers between devices, exchange(): return lax.ppermute(value, ('dp', 'section'), pairs)  122 us
    ppermute x15, starting transfers between devices, hand_over(): return lax.ppermute(value, 'section', [(source, 1 - source)])  40 us
    pallas_call x2, Pallas kernels, attend_gradient(): run_kernel(functools.partial(attend_kernel, layer), (S(flat, F32), S(flat...  31.5 us
    pallas_call x1, Pallas kernels, first_forward(): run_kernel(functools.partial(first_forward_kernel, micro_count), outs + (...  31.1 us
    pallas_call x2, Pallas kernels, feed_gradient(): run_kernel(functools.partial(feed_kernel, layer), (half, half, half_wide,...  28 us
    pallas_call x2, Pallas kernels, feed_weights(): run_kernel(functools.partial(feed_weights_kernel, layer, near_first), uni...  21.8 us
    ppermute x16, starting transfers between devices, exchange(): return lax.ppermute(value, ('dp', 'section'), pairs)  21.7 us
    ppermute x21, waiting for transfers between devices, swap(): return lax.ppermute(value, 'section', [(0, 1), (1, 0)])  19.6 us
  transfers between devices with their start and end apart: 52, of which 17 were waited for; matrix products, arithmetic and copies ran while one was open for 1% of the time, Pallas kernels for 35%

profile of v3, /device:TPU:0, one launch (start us, length us, event | category | flops | bytes accessed | tf_op | source)
XLA Modules:
  0.0 383.6 jit_solution(7074773834818075968)
XLA Ops:
  1.3 31.1 %first_forward.1 = (bf16[2,384,768]{2,1,0:T(8,128)(2,1)}, bf16[2,3,384,768]{3,2,1,0:T(8,128)(2,1)}, bf16[2,384,768]{2,1,0:T(8,128)(2,1)}, bf16[2,384,768]{2,1,0:...) custom-call(s32[2]{0:T(128)} %bucket.11, ...), custom_call_target="tpu_custom_call" | custom-call | flops 10871635968 | bytes 40000000 | tf_op jit(solution)/shard_map/first_forward/pallas_call | solution.py:444
  42.4 3.4 collective-permute-done.3.xv
  47.2 17.1 %second_forward.1 = (bf16[1,384,768]{2,1,0:T(8,128)(2,1)}, bf16[1,3,384,768]{3,2,1,0:T(8,128)(2,1)}, bf16[1,384,768]{2,1,0:T(8,128)(2,1)}, bf16[1,384,768]{2,1,0...) custom-call(s32[2]{0:T(128)} %bucket.11, ...), custom_call_target="tpu_custom_call" | custom-call | flops 5435817984 | bytes 25000000 | tf_op jit(solution)/shard_map/second_forward/pallas_call | solution.py:453
  64.7 3.4 collective-permute-start.19
  68.1 3.5 collective-permute-start.20
  71.6 14.0 %feed_gradient.2 = (bf16[384,384]{1,0:T(8,128)(2,1)}, bf16[384,384]{1,0:T(8,128)(2,1)}, bf16[384,1536]{1,0:T(8,128)(2,1)}, bf16[384,1536]{1,0:T(8,128)(2,1)}, f3...) custom-call(s32[2]{0:T(128)} %bucket.11, s32[2]{0:T(128)} %count.11, ...), custom_call_target="tpu_custom_call" | custom-call | flops 4076863488 | bytes 25000000 | tf_op jit(solution)/shard_map/feed_gradient/pallas_call | solution.py:587
  86.2 3.0 collective-permute-done.13.dz_x
  92.1 4.2 %collective-permute-start.22 = (bf16[2,384,3072]{2,1,0:T(8,128)(2,1)}, bf16[2,384,3072]{2,1,0:T(8,128)(2,1)}, u32[]{:S(2)}, u32[]{:S(2)}) collective-permute-start(bf16[2,384,3072]{2,1,0:T(8,128)(2,1)} %get-tuple-element.147.u), channel_id=1, source_target_pairs={{0,1},{2,3},{4,5},{6,7},{8,9},{10,11},{12,13},{14,15},{16,17},{18,... | collective-permute-start | bytes 14155784 | tf_op jit(solution)/shard_map/ppermute | solution.py:971
  98.7 10.9 %feed_weights.2 = (bf16[8,192,768]{2,1,0:T(8,128)(2,1)}, bf16[8,192,768]{2,1,0:T(8,128)(2,1)}) custom-call(bf16[1,384,3072]{2,1,0:T(8,128)(2,1)} %get-tuple-element.125.u, bf16[1,384,3072]{2,1,0:T(8,128)(2,1)} %copy-done.29, bf16[1,384,768]{2,1,0:T(8,128)(2,1)} %get-tuple-element.126.ml, bf16[1,384,768]{2,1,0:T(8,128)(2,1)} %copy-done.31, ...), custom_call_target="tpu_custom_call" | custom-call | flops 3623878656 | bytes 18000000 | tf_op jit(solution)/shard_map/feed_weights/pallas_call | solution.py:790
  109.6 15.6 %attend_gradient.2 = (f32[384,768]{1,0:T(8,128)}, bf16[384,768]{1,0:T(8,128)(2,1)}, bf16[2,384,768]{2,1,0:T(8,128)(2,1)}, bf16[2,384,768]{2,1,0:T(8,128)(2,1)}, f32[8,768]{1,0:T(8,128)}) custom-call(s32[2]{0:T(128)} %bucket.11, s32[2]{0:T(128)} %count.11, s32[2,6]{1,0:T(2,128)} %lengths.11, bf16[1,3,384,768]{3,2,1,0:T(8,128)(2,1)} %get-tuple-element.120.qkv.qkv_x, ...), custom_call_target="tpu_custom_call" | custom-call | flops 1358954496 | bytes 15000000 | tf_op jit(solution)/shard_map/attend_gradient/pallas_call | solution.py:705
  128.3 3.4 collective-permute-start.21
  131.7 3.0 collective-permute-done.18.small_two_x
  134.7 3.2 collective-permute-start.24
  138.0 3.6 collective-permute-start.10
  141.7 6.9 %attend_weights.2 = (bf16[8,112,768]{2,1,0:T(8,128)(2,1)}, bf16[8,112,768]{2,1,0:T(8,128)(2,1)}) custom-call(bf16[2,384,768]{2,1,0:T(8,128)(2,1)} %get-tuple-element.116.y_own.h, bf16[2,384,768]{2,1,0:T(8,128)(2,1)} %collective-permute-done.y_other.h_x, bf16[1,384,768]{2,1,0:T(8,128)(2,1)} %get-tuple-element.136.c, ...), custom_call_target="tpu_custom_call" | custom-call | flops 1811939328 | bytes 10000000 | tf_op jit(solution)/shard_map/attend_weights/pallas_call | solution.py:849
  152.6 13.9 %feed_gradient.3 = (bf16[384,384]{1,0:T(8,128)(2,1)}, bf16[384,384]{1,0:T(8,128)(2,1)}, bf16[384,1536]{1,0:T(8,128)(2,1)}, bf16[384,1536]{1,0:T(8,128)(2,1)}, f3...) custom-call(s32[2]{0:T(128)} %bucket.11, s32[2]{0:T(128)} %count.11, ...), custom_call_target="tpu_custom_call" | custom-call | flops 4076863488 | bytes 25000000 | tf_op jit(solution)/shard_map/feed_gradient/pallas_call | solution.py:587
  166.6 12.1 %collective-permute-done.25.refs_3_ = bf16[8,112,768]{2,1,0:T(8,128)(2,1)} collective-permute-done((bf16[8,112,768]{2,1,0:T(8,128)(2,1)}, bf16[8,112,768]{2,1,0:T(8,128)(2,1)}, u32[]{:S(2)}, u32[]{:S(2)}) %collective-permute-start.25) | collective-permute-done | bytes 1376288 | tf_op jit(solution)/shard_map/ppermute | solution.py:963
  180.1 4.0 %add_arrived.8 = (bf16[4,192,768]{2,1,0:T(8,128)(2,1)}, bf16[4,192,768]{2,1,0:T(8,128)(2,1)S(1)}, bf16[4,112,768]{2,1,0:T(8,128)(2,1)S(1)}, bf16[4,112,768]{2,1,0:T(8,128)(2,1)S(1)}) custom-call(bf16[8,192,768]{2,1,0:T(8,128)(2,1)S(1)} %copy-done, bf16[8,112,768]{2,1,0:T(8,128)(2,1)S(1)} %copy-done.2, bf16[8,192,768]{2,1,0:T(8,128)(2,1)} %collective-permute-done.24.refs_2_, ...), custom_call_target="tpu_custom_call" | custom-call | flops 5603328 | bytes 11206656 | tf_op jit(solution)/shard_map/add_arrived/pallas_call | solution.py:887
  186.8 3.4 collective-permute-start.35
  191.0 11.0 %feed_weights.3 = (bf16[8,192,768]{2,1,0:T(8,128)(2,1)}, bf16[8,192,768]{2,1,0:T(8,128)(2,1)}) custom-call(bf16[2,384,3072]{2,1,0:T(8,128)(2,1)} %get-tuple-element.147.u, bf16[2,384,3072]{2,1,0:T(8,128)(2,1)} %collective-permute-done.22.u_x, bf16[2,384,768]{2,1,0:T(8,128)(2,1)} %get-tuple-element.148.ml, bf16[2,384,768]{2,1,0:T(8,128)(2,1)} %collective-permute-done.23.ml_x, ...), custom_call_target="tpu_custom_call" | custom-call | flops 3623878656 | bytes 18000000 | tf_op jit(solution)/shard_map/feed_weights/pallas_call | solution.py:790
  203.6 15.9 %attend_gradient.3 = (f32[384,768]{1,0:T(8,128)}, bf16[384,768]{1,0:T(8,128)(2,1)}, bf16[2,384,768]{2,1,0:T(8,128)(2,1)}, bf16[2,384,768]{2,1,0:T(8,128)(2,1)}, f32[8,768]{1,0:T(8,128)}) custom-call(s32[2]{0:T(128)} %bucket.11, s32[2]{0:T(128)} %count.11, s32[2,6]{1,0:T(2,128)} %lengths.11, bf16[2,3,384,768]{3,2,1,0:T(8,128)(2,1)} %get-tuple-element.119.qkv, ...), custom_call_target="tpu_custom_call" | custom-call | flops 1358954496 | bytes 15000000 | tf_op jit(solution)/shard_map/attend_gradient/pallas_call | solution.py:705
  220.6 17.8 %collective-permute-done.32.refs_3_ = bf16[4,112,768]{2,1,0:T(8,128)(2,1)S(1)} collective-permute-done((bf16[4,112,768]{2,1,0:T(8,128)(2,1)}, bf16[4,112,768]{2,1,0:T(8,128)(2,1)S(1)}, u32[]{:S(2)}, u32[]{:S(2)}) %collective-permute-start.32) | collective-permute-done | bytes 688160 | tf_op jit(solution)/shard_map/ppermute | solution.py:963
  244.6 7.0 %attend_weights.3 = (bf16[8,112,768]{2,1,0:T(8,128)(2,1)}, bf16[8,112,768]{2,1,0:T(8,128)(2,1)}) custom-call(bf16[2,384,768]{2,1,0:T(8,128)(2,1)} %h_x.1, bf16[2,384,768]{2,1,0:T(8,128)(2,1)} %h_x.1, bf16[2,384,768]{2,1,0:T(8,128)(2,1)} %get-tuple-element.183.c, bf16[2,384,768]{2,1,0:T(8,128)(2,1)} %collective-permute-done.35.c_x, ...), custom_call_target="tpu_custom_call" | custom-call | flops 1811939328 | bytes 10000000 | tf_op jit(solution)/shard_map/attend_weights/pallas_call | solution.py:849
  258.0 3.1 collective-permute-done.34.refs_3_
  261.2 35.9 %collective-permute-done.33.refs_2_ = bf16[2,192,768]{2,1,0:T(8,128)(2,1)S(1)} collective-permute-done((bf16[2,192,768]{2,1,0:T(8,128)(2,1)}, bf16[2,192,768]{2,1,0:T(8,128)(2,1)S(1)}, u32[]{:S(2)}, u32[]{:S(2)}) %collective-permute-start.33) | collective-permute-done | bytes 589856 | tf_op jit(solution)/shard_map/ppermute | solution.py:963
  297.3 2.7 collective-permute-start.39
  300.3 20.2 %collective-permute-done.40.refs_4_ = bf16[1,112,768]{2,1,0:T(8,128)(2,1)S(1)} collective-permute-done((bf16[1,112,768]{2,1,0:T(8,128)(2,1)S(1)}, bf16[1,112,768]{2,1,0:T(8,128)(2,1)S(1)}, u32[]{:S(2)}, u32[]{:S(2)}) %collective-permute-start.40) | collective-permute-done | bytes 172064 | tf_op jit(solution)/shard_map/ppermute | solution.py:963
  324.9 7.1 %collective-permute-done.43.refs_3_ = bf16[4,112,768]{2,1,0:T(8,128)(2,1)S(1)} collective-permute-done((bf16[4,112,768]{2,1,0:T(8,128)(2,1)S(1)}, bf16[4,112,768]{2,1,0:T(8,128)(2,1)S(1)}, u32[]{:S(2)}, u32[]{:S(2)}) %collective-permute-start.43) | collective-permute-done | bytes 688160 | tf_op jit(solution)/shard_map/ppermute | solution.py:963
  337.6 7.1 %collective-permute-done.45.refs_3_ = bf16[2,112,768]{2,1,0:T(8,128)(2,1)S(1)} collective-permute-done((bf16[2,112,768]{2,1,0:T(8,128)(2,1)}, bf16[2,112,768]{2,1,0:T(8,128)(2,1)S(1)}, u32[]{:S(2)}, u32[]{:S(2)}) %collective-permute-start.45) | collective-permute-done | bytes 344096 | tf_op jit(solution)/shard_map/ppermute | solution.py:963
  346.7 3.4 collective-permute-start.46
  353.8 16.6 %collective-permute-done.47.refs_3_ = bf16[1,112,768]{2,1,0:T(8,128)(2,1)S(1)} collective-permute-done((bf16[1,112,768]{2,1,0:T(8,128)(2,1)S(1)}, bf16[1,112,768]{2,1,0:T(8,128)(2,1)S(1)}, u32[]{:S(2)}, u32[]{:S(2)}) %collective-permute-start.47) | collective-permute-done | bytes 172064 | tf_op jit(solution)/shard_map/ppermute | solution.py:963
  373.3 3.1 collective-permute-start.51
  (170 shorter events, 71.4 us)
Async XLA Ops:
  0.7 45.1 %collective-permute-start.5 = (bf16[1,768,3072]{2,1,0:T(8,128)(2,1)}, bf16[1,768,3072]{2,1,0:T(8,128)(2,1)}, u32[]{:S(2)}, u32[]{:S(2)}) collective-permute-start(bf16[1,768,3072]{2,1,0:T(8,128)(2,1)} %wi.7), channel_id=1, source_target_pairs={{0,1},{1,0},{2,3},{3,2},{4,5},{5,4},{6,7},{7,6},{8,9},{9,8},{10,11... | collective-permute-start | bytes 14155784 | tf_op jit(solution)/shard_map/ppermute | solution.py:967
  1.2 45.6 %collective-permute-start.6 = (bf16[1,3072,768]{2,1,0:T(8,128)(2,1)}, bf16[1,3072,768]{2,1,0:T(8,128)(2,1)}, u32[]{:S(2)}, u32[]{:S(2)}) collective-permute-start(bf16[1,3072,768]{2,1,0:T(8,128)(2,1)} %wo.7), channel_id=1, source_target_pairs={{0,1},{1,0},{2,3},{3,2},{4,5},{5,4},{6,7},{7,6},{8,9},{9,8},{10,11... | collective-permute-start | bytes 14155784 | tf_op jit(solution)/shard_map/ppermute | solution.py:967
  64.3 32.0 %collective-permute-start.11 = (bf16[1,384,3072]{2,1,0:T(8,128)(2,1)}, bf16[1,384,3072]{2,1,0:T(8,128)(2,1)S(1)}, u32[]{:S(2)}, u32[]{:S(2)}) collective-permute-start(bf16[1,384,3072]{2,1,0:T(8,128)(2,1)} %get-tuple-element.125.u), channel_id=1, source_target_pairs={{0,1},{1,0},{2,3},{3,2},{4,5},{5,4},{6,7},{7,6},{8,9},{9,8},{10,11... | collective-permute-start | bytes 7077896 | tf_op jit(solution)/shard_map/ppermute | solution.py:967
  64.7 61.1 %collective-permute-start.19 = (f32[2,384,768]{2,1,0:T(8,128)}, f32[2,384,768]{2,1,0:T(8,128)}, u32[]{:S(2)}, u32[]{:S(2)}) collective-permute-start(f32[2,384,768]{2,1,0:T(8,128)} %get-tuple-element.143.a2), channel_id=1, source_target_pairs={{0,1},{2,3},{4,5},{6,7},{8,9},{10,11},{12,13},{14,15},{16,17},{18,... | collective-permute-start | bytes 7077896 | tf_op jit(solution)/shard_map/ppermute | solution.py:971
  68.1 82.1 %collective-permute-start.20 = (bf16[2,384,3072]{2,1,0:T(8,128)(2,1)}, bf16[2,384,3072]{2,1,0:T(8,128)(2,1)}, u32[]{:S(2)}, u32[]{:S(2)}) collective-permute-start(bf16[2,384,3072]{2,1,0:T(8,128)(2,1)} %get-tuple-element.144.gp), channel_id=1, source_target_pairs={{0,1},{2,3},{4,5},{6,7},{8,9},{10,11},{12,13},{14,15},{16,17},{18,... | collective-permute-start | bytes 14155784 | tf_op jit(solution)/shard_map/ppermute | solution.py:971
  92.1 98.2 %collective-permute-start.22 = (bf16[2,384,3072]{2,1,0:T(8,128)(2,1)}, bf16[2,384,3072]{2,1,0:T(8,128)(2,1)}, u32[]{:S(2)}, u32[]{:S(2)}) collective-permute-start(bf16[2,384,3072]{2,1,0:T(8,128)(2,1)} %get-tuple-element.147.u), channel_id=1, source_target_pairs={{0,1},{2,3},{4,5},{6,7},{8,9},{10,11},{12,13},{14,15},{16,17},{18,... | collective-permute-start | bytes 14155784 | tf_op jit(solution)/shard_map/ppermute | solution.py:971
  125.2 12.7 %collective-permute-start.16 = (bf16[2,384,768]{2,1,0:T(8,128)(2,1)}, bf16[2,384,768]{2,1,0:T(8,128)(2,1)}, u32[]{:S(2)}, u32[]{:S(2)}) collective-permute-start(bf16[2,384,768]{2,1,0:T(8,128)(2,1)} %get-tuple-element.138), channel_id=1, source_target_pairs={{0,1},{1,0},{2,3},{3,2},{4,5},{5,4},{6,7},{7,6},{8,9},{9,8},{10,11... | collective-permute-start | bytes 3538952 | tf_op jit(solution)/shard_map/ppermute | solution.py:967
  128.3 20.3 %collective-permute-start.21 = (f32[2,384,768]{2,1,0:T(8,128)S(1)}, f32[2,384,768]{2,1,0:T(8,128)}, u32[]{:S(2)}, u32[]{:S(2)}) collective-permute-start(f32[2,384,768]{2,1,0:T(8,128)S(1)} %copy-done.22), channel_id=1, source_target_pairs={{0,1},{2,3},{4,5},{6,7},{8,9},{10,11},{12,13},{14,15},{16,17},{18,... | collective-permute-start | bytes 7077896 | tf_op jit(solution)/shard_map/ppermute | solution.py:971
  134.7 31.8 %collective-permute-start.24 = (bf16[8,192,768]{2,1,0:T(8,128)(2,1)}, bf16[8,192,768]{2,1,0:T(8,128)(2,1)}, u32[]{:S(2)}, u32[]{:S(2)}) collective-permute-start(bf16[8,192,768]{2,1,0:T(8,128)(2,1)} %get-tuple-element.150), channel_id=1, source_target_pairs={{0,2},{1,5},{2,0},{3,7},{4,6},{5,1},{6,4},{7,3},{8,10},{9,13},{10,... | collective-permute-start | bytes 7077896 | tf_op jit(solution)/shard_map/ppermute | solution.py:963
  138.0 65.7 %collective-permute-start.10 = (bf16[2,3,384,768]{3,2,1,0:T(8,128)(2,1)}, bf16[2,3,384,768]{3,2,1,0:T(8,128)(2,1)}, u32[]{:S(2)}, u32[]{:S(2)}) collective-permute-start(bf16[2,3,384,768]{3,2,1,0:T(8,128)(2,1)} %get-tuple-element.119.qkv), channel_id=1, source_target_pairs={{0,1},{2,3},{4,5},{6,7},{8,9},{10,11},{12,13},{14,15},{16,17},{18,... | collective-permute-start | bytes 10616840 | tf_op jit(solution)/shard_map/ppermute | solution.py:971
  148.6 30.1 %collective-permute-start.25 = (bf16[8,112,768]{2,1,0:T(8,128)(2,1)}, bf16[8,112,768]{2,1,0:T(8,128)(2,1)}, u32[]{:S(2)}, u32[]{:S(2)}) collective-permute-start(bf16[8,112,768]{2,1,0:T(8,128)(2,1)} %get-tuple-element.151), channel_id=1, source_target_pairs={{0,8},{1,9},{2,10},{3,11},{4,12},{5,13},{6,14},{7,15},{8,0},{9,1},... | collective-permute-start | bytes 4128776 | tf_op jit(solution)/shard_map/ppermute | solution.py:963
  150.2 36.6 %collective-permute-start.23 = (bf16[2,384,768]{2,1,0:T(8,128)(2,1)}, bf16[2,384,768]{2,1,0:T(8,128)(2,1)}, u32[]{:S(2)}, u32[]{:S(2)}) collective-permute-start(bf16[2,384,768]{2,1,0:T(8,128)(2,1)} %get-tuple-element.148.ml), channel_id=1, source_target_pairs={{0,1},{2,3},{4,5},{6,7},{8,9},{10,11},{12,13},{14,15},{16,17},{18,... | collective-permute-start | bytes 3538952 | tf_op jit(solution)/shard_map/ppermute | solution.py:971
  166.5 24.4 %collective-permute-start.27 = (bf16[384,1536]{1,0:T(8,128)(2,1)}, bf16[384,1536]{1,0:T(8,128)(2,1)}, u32[]{:S(2)}, u32[]{:S(2)}) collective-permute-start(bf16[384,1536]{1,0:T(8,128)(2,1)} %get-tuple-element.159), channel_id=1, source_target_pairs={{0,1},{1,0},{2,3},{3,2},{4,5},{5,4},{6,7},{7,6},{8,9},{9,8},{10,11... | collective-permute-start | bytes 3538952 | tf_op jit(solution)/shard_map/ppermute | solution.py:967
  178.7 12.2 %collective-permute-start.26 = (bf16[384,384]{1,0:T(8,128)(2,1)}, bf16[384,384]{1,0:T(8,128)(2,1)}, u32[]{:S(2)}, u32[]{:S(2)}) collective-permute-start(bf16[384,384]{1,0:T(8,128)(2,1)} %get-tuple-element.157), channel_id=1, source_target_pairs={{0,1},{1,0},{2,3},{3,2},{4,5},{5,4},{6,7},{7,6},{8,9},{9,8},{10,11... | collective-permute-start | bytes 884744 | tf_op jit(solution)/shard_map/ppermute | solution.py:967
  186.8 57.1 %collective-permute-start.35 = (bf16[2,384,768]{2,1,0:T(8,128)(2,1)}, bf16[2,384,768]{2,1,0:T(8,128)(2,1)}, u32[]{:S(2)}, u32[]{:S(2)}) collective-permute-start(bf16[2,384,768]{2,1,0:T(8,128)(2,1)} %get-tuple-element.183.c), channel_id=1, source_target_pairs={{0,1},{2,3},{4,5},{6,7},{8,9},{10,11},{12,13},{14,15},{16,17},{18,... | collective-permute-start | bytes 3538952 | tf_op jit(solution)/shard_map/ppermute | solution.py:971
  190.3 48.9 %collective-permute-start.31 = (bf16[4,192,768]{2,1,0:T(8,128)(2,1)}, bf16[4,192,768]{2,1,0:T(8,128)(2,1)S(1)}, u32[]{:S(2)}, u32[]{:S(2)}) collective-permute-start(bf16[4,192,768]{2,1,0:T(8,128)(2,1)} %get-tuple-element.171), channel_id=1, source_target_pairs={{0,4},{1,3},{2,6},{3,1},{4,0},{5,7},{6,2},{7,5},{8,12},{9,11},{10,... | collective-permute-start | bytes 3538952 | tf_op jit(solution)/shard_map/ppermute | solution.py:963
  201.9 52.8 %collective-permute-start.30 = (bf16[8,192,768]{2,1,0:T(8,128)(2,1)}, bf16[8,192,768]{2,1,0:T(8,128)(2,1)}, u32[]{:S(2)}, u32[]{:S(2)}) collective-permute-start(bf16[8,192,768]{2,1,0:T(8,128)(2,1)} %get-tuple-element.166), channel_id=1, source_target_pairs={{0,2},{1,5},{2,0},{3,7},{4,6},{5,1},{6,4},{7,3},{8,10},{9,13},{10,... | collective-permute-start | bytes 7077896 | tf_op jit(solution)/shard_map/ppermute | solution.py:963
  219.5 24.4 %collective-permute-start.36 = (bf16[2,384,768]{2,1,0:T(8,128)(2,1)}, bf16[2,384,768]{2,1,0:T(8,128)(2,1)}, u32[]{:S(2)}, u32[]{:S(2)}) collective-permute-start(bf16[2,384,768]{2,1,0:T(8,128)(2,1)} %get-tuple-element.185), channel_id=1, source_target_pairs={{0,1},{1,0},{2,3},{3,2},{4,5},{5,4},{6,7},{7,6},{8,9},{9,8},{10,11... | collective-permute-start | bytes 3538952 | tf_op jit(solution)/shard_map/ppermute | solution.py:967
  219.6 18.8 %collective-permute-start.32 = (bf16[4,112,768]{2,1,0:T(8,128)(2,1)}, bf16[4,112,768]{2,1,0:T(8,128)(2,1)S(1)}, u32[]{:S(2)}, u32[]{:S(2)}) collective-permute-start(bf16[4,112,768]{2,1,0:T(8,128)(2,1)} %copy-done.12), channel_id=1, source_target_pairs={{0,2},{1,5},{2,0},{3,7},{4,6},{5,1},{6,4},{7,3},{8,10},{9,13},{10,... | collective-permute-start | bytes 2064392 | tf_op jit(solution)/shard_map/ppermute | solution.py:963
  251.6 68.9 %collective-permute-start.41 = (bf16[8,112,768]{2,1,0:T(8,128)(2,1)}, bf16[8,112,768]{2,1,0:T(8,128)(2,1)S(1)}, u32[]{:S(2)}, u32[]{:S(2)}) collective-permute-start(bf16[8,112,768]{2,1,0:T(8,128)(2,1)} %get-tuple-element.191), channel_id=1, source_target_pairs={{0,8},{1,9},{2,10},{3,11},{4,12},{5,13},{6,14},{7,15},{8,0},{9,1},... | collective-permute-start | bytes 4128776 | tf_op jit(solution)/shard_map/ppermute | solution.py:963
  253.3 43.8 %collective-permute-start.33 = (bf16[2,192,768]{2,1,0:T(8,128)(2,1)}, bf16[2,192,768]{2,1,0:T(8,128)(2,1)S(1)}, u32[]{:S(2)}, u32[]{:S(2)}) collective-permute-start(bf16[2,192,768]{2,1,0:T(8,128)(2,1)} %copy-done.13), channel_id=1, source_target_pairs={{0,8},{1,9},{2,10},{3,11},{4,12},{5,13},{6,14},{7,15},{8,0},{9,1},... | collective-permute-start | bytes 1769480 | tf_op jit(solution)/shard_map/ppermute | solution.py:963
  257.0 75.0 %collective-permute-start.42 = (bf16[4,192,768]{2,1,0:T(8,128)(2,1)S(1)}, bf16[4,192,768]{2,1,0:T(8,128)(2,1)S(1)}, u32[]{:S(2)}, u32[]{:S(2)}) collective-permute-start(bf16[4,192,768]{2,1,0:T(8,128)(2,1)S(1)} %get-tuple-element.193), channel_id=1, source_target_pairs={{0,4},{1,3},{2,6},{3,1},{4,0},{5,7},{6,2},{7,5},{8,12},{9,11},{10,... | collective-permute-start | bytes 3538952 | tf_op jit(solution)/shard_map/ppermute | solution.py:963
  297.3 23.2 %collective-permute-start.39 = (bf16[1,192,768]{2,1,0:T(8,128)(2,1)S(1)}, bf16[1,192,768]{2,1,0:T(8,128)(2,1)S(1)}, u32[]{:S(2)}, u32[]{:S(2)}) collective-permute-start(bf16[1,192,768]{2,1,0:T(8,128)(2,1)S(1)} %get-tuple-element.189), channel_id=1, source_target_pairs={{0,16},{1,17},{2,18},{3,19},{4,20},{5,21},{6,22},{7,23},{8,24},{9,... | collective-permute-start | bytes 884744 | tf_op jit(solution)/shard_map/ppermute | solution.py:963
  299.9 20.6 %collective-permute-start.40 = (bf16[1,112,768]{2,1,0:T(8,128)(2,1)S(1)}, bf16[1,112,768]{2,1,0:T(8,128)(2,1)S(1)}, u32[]{:S(2)}, u32[]{:S(2)}) collective-permute-start(bf16[1,112,768]{2,1,0:T(8,128)(2,1)S(1)} %get-tuple-element.190), channel_id=1, source_target_pairs={{0,16},{1,17},{2,18},{3,19},{4,20},{5,21},{6,22},{7,23},{8,24},{9,... | collective-permute-start | bytes 516104 | tf_op jit(solution)/shard_map/ppermute | solution.py:963
  321.0 11.0 %collective-permute-start.43 = (bf16[4,112,768]{2,1,0:T(8,128)(2,1)S(1)}, bf16[4,112,768]{2,1,0:T(8,128)(2,1)S(1)}, u32[]{:S(2)}, u32[]{:S(2)}) collective-permute-start(bf16[4,112,768]{2,1,0:T(8,128)(2,1)S(1)} %get-tuple-element.194), channel_id=1, source_target_pairs={{0,2},{1,5},{2,0},{3,7},{4,6},{5,1},{6,4},{7,3},{8,10},{9,13},{10,... | collective-permute-start | bytes 2064392 | tf_op jit(solution)/shard_map/ppermute | solution.py:963
  322.6 49.3 %collective-permute-start.28 = (f32[384,768]{1,0:T(8,128)}, f32[384,768]{1,0:T(8,128)}, u32[]{:S(2)}, u32[]{:S(2)}) collective-permute-start(f32[384,768]{1,0:T(8,128)} %get-tuple-element.165), channel_id=1, source_target_pairs={{0,1},{2,3},{4,5},{6,7},{8,9},{10,11},{12,13},{14,15},{16,17},{18,... | collective-permute-start | bytes 3538952 | tf_op jit(solution)/shard_map/ppermute | solution.py:971
  333.1 13.3 %collective-permute-start.44 = (bf16[2,192,768]{2,1,0:T(8,128)(2,1)S(1)}, bf16[2,192,768]{2,1,0:T(8,128)(2,1)S(1)}, u32[]{:S(2)}, u32[]{:S(2)}) collective-permute-start(bf16[2,192,768]{2,1,0:T(8,128)(2,1)S(1)} %get-tuple-element.197), channel_id=1, source_target_pairs={{0,8},{1,9},{2,10},{3,11},{4,12},{5,13},{6,14},{7,15},{8,0},{9,1},... | collective-permute-start | bytes 1769480 | tf_op jit(solution)/shard_map/ppermute | solution.py:963
  333.8 16.4 %collective-permute-start.9 = (bf16[1,384,768]{2,1,0:T(8,128)(2,1)}, bf16[1,384,768]{2,1,0:T(8,128)(2,1)}, u32[]{:S(2)}, u32[]{:S(2)}) collective-permute-start(bf16[1,384,768]{2,1,0:T(8,128)(2,1)} %get-tuple-element.118), channel_id=1, source_target_pairs={{0,1},{2,3},{4,5},{6,7},{8,9},{10,11},{12,13},{14,15},{16,17},{18,... | collective-permute-start | bytes 1769480 | tf_op jit(solution)/shard_map/ppermute | solution.py:971
  335.9 41.8 %collective-permute-start.29 = (f32[384,768]{1,0:T(8,128)}, f32[384,768]{1,0:T(8,128)}, u32[]{:S(2)}, u32[]{:S(2)}) collective-permute-start(f32[384,768]{1,0:T(8,128)} %get-tuple-element.164), channel_id=1, source_target_pairs={{1,0},{3,2},{5,4},{7,6},{9,8},{11,10},{13,12},{15,14},{17,16},{19,... | collective-permute-start | bytes 3538952 | tf_op jit(solution)/shard_map/ppermute | solution.py:971
  346.7 23.8 %collective-permute-start.46 = (bf16[1,192,768]{2,1,0:T(8,128)(2,1)S(1)}, bf16[1,192,768]{2,1,0:T(8,128)(2,1)S(1)}, u32[]{:S(2)}, u32[]{:S(2)}) collective-permute-start(bf16[1,192,768]{2,1,0:T(8,128)(2,1)S(1)} %get-tuple-element.201), channel_id=1, source_target_pairs={{0,16},{1,17},{2,18},{3,19},{4,20},{5,21},{6,22},{7,23},{8,24},{9,... | collective-permute-start | bytes 884744 | tf_op jit(solution)/shard_map/ppermute | solution.py:963
  350.1 20.4 %collective-permute-start.47 = (bf16[1,112,768]{2,1,0:T(8,128)(2,1)S(1)}, bf16[1,112,768]{2,1,0:T(8,128)(2,1)S(1)}, u32[]{:S(2)}, u32[]{:S(2)}) collective-permute-start(bf16[1,112,768]{2,1,0:T(8,128)(2,1)S(1)} %get-tuple-element.202), channel_id=1, source_target_pairs={{0,16},{1,17},{2,18},{3,19},{4,20},{5,21},{6,22},{7,23},{8,24},{9,... | collective-permute-start | bytes 516104 | tf_op jit(solution)/shard_map/ppermute | solution.py:963
  351.5 29.3 %collective-permute-start.49 = (f32[192,768]{1,0:T(8,128)S(1)}, f32[192,768]{1,0:T(8,128)S(1)}, u32[]{:S(2)}, u32[]{:S(2)}) collective-permute-start(f32[192,768]{1,0:T(8,128)S(1)} %get-tuple-element.204.feed_second), channel_id=1, source_target_pairs={{0,1},{2,3},{4,5},{6,7},{8,9},{10,11},{12,13},{14,15},{16,17},{18,... | collective-permute-start | bytes 1769480 | tf_op jit(solution)/shard_map/ppermute | solution.py:971
  (56 other events, 589.6 us)
